TPU v7x, 128 devices: a whole 4x4x4 slice. The times are simulated.
128 devices in a mesh: rows: 64 (over y, z, x), rep: 2 (over core).
Axes of the slice: x: 4, y: 4, z: 4, core: 2. Of those that a mesh axis runs over, the one named last changes fastest.
Arguments:
- margin_blocks: float32 [256, 16, 128, 128], P('rows', 'rep'), may hold values from -1 to 1
- margin_cols: int32 [256, 16], P('rows', 'rep'), may hold values from 0 to 255, as said below
- factor_blocks: float32 [256, 16, 128, 128], P('rows'), may hold values from -0.5 to 0.5
- factor_cols: int32 [256, 16], P('rows'), may hold values from 0 to 255, as said below
- product_cols: int32 [256, 24], P('rows'), may hold values from 0 to 255, as said below
- metric_cols: int32 [256, 24], P('rows'), may hold values from 0 to 255, as said below
Outputs:
- product: float32 [256, 24, 128, 128], P('rows', 'rep')
- metric: float32 [256, 24, 128, 128], P('rows', 'rep')
Inputs may be any that keep to these rules, and one draw needn't show every extreme that they name: `margin_cols`: each block row holds 16 distinct block columns, its own index among them, each within 8 of the row index cyclically modulo 256. `factor_cols`: each block row holds 16 distinct block columns, each in the block rows of an index of rows at most 2 away from the row's own (column // 4 against row // 4, cyclically); every block column is named by exactly 16 block rows. `product_cols`: each block row holds 24 distinct block columns, its own index among them, each within 16 of the row index cyclically. `metric_cols`: each block row holds 24 distinct block columns, its own index among them, each within 16 of the row index cyclically.
All inputs are finite; a program needn't handle non-finite values.
Results may differ from a plain program's by a relative error of at most 0.0003.
Values sent between devices are 32-bit elements; how exact they have to be, the bound alone decides.
No kernel may reach another device: no remote copies, remote signals or barrier semaphores. Data moves between devices by JAX's collectives and lax.ppermute only.
A program may use at most 192 MiB of HBM per device.

v0:
```python
import jax
import jax.numpy as jnp
from jax import lax
from jax.sharding import PartitionSpec as P

HIGHEST = lax.Precision.HIGHEST
OFFSETS = (-2, -1, 1, 2)


def passed_along(array, axis, by):
    devices = lax.axis_size(axis)
    return lax.ppermute(array, axis, [(i, (i + by) % devices) for i in range(devices)])


def shards(margin_blocks, margin_cols, factor_blocks, factor_cols, product_cols, metric_cols):
    row_count = factor_blocks.shape[0]
    slots_factor = factor_blocks.shape[1]
    block_size = factor_blocks.shape[2]
    cycle_size = lax.axis_size("rows")
    position = lax.axis_index("rows")
    core_index = lax.axis_index("rep")
    total_rows = row_count * cycle_size
    first_row = (position - 2) * row_count
    patterns = jnp.concatenate([factor_cols, product_cols], axis=1)
    pattern_layers = {}
    for offset in OFFSETS:
        pattern_layers[offset] = passed_along(patterns, "rows", -offset)
    halo_patterns = jnp.concatenate(
        [pattern_layers[-2], pattern_layers[-1], patterns, pattern_layers[1], pattern_layers[2]],
        axis=0,
    )
    halo_factor_cols = halo_patterns[:, :slots_factor]
    halo_product_cols = halo_patterns[:, slots_factor:]
    factor_layers = {}
    for offset in OFFSETS:
        factor_layers[offset] = passed_along(factor_blocks, "rows", -offset)
    halo_factor = jnp.concatenate(
        [factor_layers[-2], factor_layers[-1], factor_blocks, factor_layers[1], factor_layers[2]],
        axis=0,
    )
    relative = (margin_cols - first_row) % total_rows

    def product_row(packed):
        margin_row, relative_row, kept_row = packed
        picked = halo_factor[relative_row]
        partial_terms = jnp.einsum("kab,kmbc->kmac", margin_row, picked, precision=HIGHEST)
        selector = (halo_factor_cols[relative_row][:, :, None] == kept_row[None, None, :]).astype(
            jnp.float32
        )
        return jnp.einsum("kmy,kmac->yac", selector, partial_terms, precision=HIGHEST)

    partial_product = lax.map(product_row, (margin_blocks, relative, product_cols))
    product = lax.psum_scatter(partial_product, "rep", scatter_dimension=1, tiled=True)
    product_width = product.shape[1]
    product_layers = {}
    for offset in OFFSETS:
        product_layers[offset] = passed_along(product, "rows", -offset)
    halo_product = jnp.concatenate(
        [product_layers[-2], product_layers[-1], product, product_layers[1], product_layers[2]],
        axis=0,
    )
    halo_product_share = lax.dynamic_slice_in_dim(
        halo_product_cols, core_index * product_width, product_width, 1
    )
    flat_cols = halo_factor_cols.reshape(-1)
    entry_count = flat_cols.shape[0]
    targets = position * row_count + jnp.arange(row_count, dtype=jnp.int32)
    matches = (flat_cols[None, :] == targets[:, None]).astype(jnp.int32)
    ranking = jnp.cumsum(matches, axis=1) - 1
    slot_range = jnp.arange(slots_factor, dtype=jnp.int32)
    chosen = matches[:, None, :] * (ranking[:, None, :] == slot_range[None, :, None]).astype(
        jnp.int32
    )
    entries = jnp.sum(chosen * jnp.arange(entry_count, dtype=jnp.int32)[None, None, :], axis=2)
    flat_factor = halo_factor.reshape(-1, block_size, block_size)

    def metric_row(packed):
        entry_row, kept_row = packed
        source_rows = entry_row // slots_factor
        factor_here = flat_factor[entry_row]
        product_here = halo_product[source_rows]
        partial_terms = jnp.einsum("tba,tybc->tyac", factor_here, product_here, precision=HIGHEST)
        selector = (halo_product_share[source_rows][:, :, None] == kept_row[None, None, :]).astype(
            jnp.float32
        )
        return jnp.einsum("tyx,tyac->xac", selector, partial_terms, precision=HIGHEST)

    partial_metric = lax.map(metric_row, (entries, metric_cols))
    metric = lax.psum_scatter(partial_metric, "rep", scatter_dimension=1, tiled=True)
    return (product, metric)


def solution(mesh):
    return jax.shard_map(
        shards,
        mesh=mesh,
        in_specs=(
            P("rows", "rep", None, None),
            P("rows", "rep"),
            P("rows", None, None, None),
            P("rows", None),
            P("rows", None),
            P("rows", None),
        ),
        out_specs=(P("rows", "rep", None, None), P("rows", "rep", None, None)),
        check_vma=False,
    )
```

profile of v0, /device:TPU:1, one launch (start us, length us, event | category | flops | bytes accessed | tf_op | source)
XLA Modules:
  0.0 1083.5 jit_solution(5972009479241228692)
XLA Ops:
  11.2 6.6 collective-permute-start.6
  21.5 265.4 %collective-permute-done = s32[4,40]{1,0:T(4,128)S(1)} collective-permute-done((s32[4,40]{1,0:T(4,128)S(1)}, s32[4,40]{1,0:T(4,128)S(1)}, u32[]{:S(2)}, u32[]{:S(2)}) %collective-permute-start) | collective-permute-done | bytes 672 | tf_op jit(solution)/shard_map/ppermute | solution.py:12
  287.2 7.6 collective-permute-done.1
  315.6 5.0 copy-done.1
  320.5 185.1 %while.22 = (s32[]{:T(128)}, f32[4,24,128,128]{3,2,1,0:T(8,128)}, s32[4,8]{1,0:T(4,128)S(1)}, s32[20,16]{1,0:T(8,128)S(1)}, s32[4,24]{1,0:T(4,128)}, /*index=5*/...) while((s32[]{:T(128)}, f32[4,24,128,128]{3,2,1,0:T(8,128)}, s32[4,8]{1,0:T(4,128)S(1)}, ...), condition=%wide.region_1.2_spmd, body=%wide.region_0.1_spmd.sunk | while | flops 3825209344 | bytes 63970332 | solution.py:52
  320.6 11.4 %gather_fusion = f32[8,16,128,128]{3,2,1,0:T(8,128)} fusion(f32[20,16,128,128]{3,2,1,0:T(8,128)} %get-tuple-element.278, s32[1024]{0:T(1024)S(1)} %pad_clamp_fusion.5), kind=kCustom, calls=%fused_computation.1.clone.1 | custom fusion | bytes 16777248 | tf_op jit(solution)/shard_map/while/body/eval_jaxpr/gather | solution.py:45
  332.0 17.5 %convolution_bitcast_fusion.8 = f32[8,16,128,128]{2,3,1,0:T(8,128)} fusion(f32[8,16,128,128]{3,2,1,0:T(8,128)} %gather_fusion, f32[4,8,128,128]{3,2,1,0:T(8,128)} %get-tuple-element.279, s32[]{:T(128)} %get-tuple-element.265), kind=kOutput, calls=%fused_computation.5.clone.1 | convolution fusion | flops 3221225472 | bytes 17302016 | tf_op jit(solution)/shard_map/while/body/eval_jaxpr/kab,kmbc->kmac/dot_general | solution.py:46
  349.5 9.3 copy.56
  360.1 5.3 convolution_bitcast_fusion.9
  366.8 11.4 %gather_fusion = f32[8,16,128,128]{3,2,1,0:T(8,128)} fusion(f32[20,16,128,128]{3,2,1,0:T(8,128)} %get-tuple-element.278, s32[1024]{0:T(1024)S(1)} %pad_clamp_fusion.5), kind=kCustom, calls=%fused_computation.1.clone.1 | custom fusion | bytes 16777248 | tf_op jit(solution)/shard_map/while/body/eval_jaxpr/gather | solution.py:45
  378.2 17.5 %convolution_bitcast_fusion.8 = f32[8,16,128,128]{2,3,1,0:T(8,128)} fusion(f32[8,16,128,128]{3,2,1,0:T(8,128)} %gather_fusion, f32[4,8,128,128]{3,2,1,0:T(8,128)} %get-tuple-element.279, s32[]{:T(128)} %get-tuple-element.265), kind=kOutput, calls=%fused_computation.5.clone.1 | convolution fusion | flops 3221225472 | bytes 17302016 | tf_op jit(solution)/shard_map/while/body/eval_jaxpr/kab,kmbc->kmac/dot_general | solution.py:46
  395.8 9.3 copy.56
  406.3 5.3 convolution_bitcast_fusion.9
  413.1 11.4 %gather_fusion = f32[8,16,128,128]{3,2,1,0:T(8,128)} fusion(f32[20,16,128,128]{3,2,1,0:T(8,128)} %get-tuple-element.278, s32[1024]{0:T(1024)S(1)} %pad_clamp_fusion.5), kind=kCustom, calls=%fused_computation.1.clone.1 | custom fusion | bytes 16777248 | tf_op jit(solution)/shard_map/while/body/eval_jaxpr/gather | solution.py:45
  424.5 17.5 %convolution_bitcast_fusion.8 = f32[8,16,128,128]{2,3,1,0:T(8,128)} fusion(f32[8,16,128,128]{3,2,1,0:T(8,128)} %gather_fusion, f32[4,8,128,128]{3,2,1,0:T(8,128)} %get-tuple-element.279, s32[]{:T(128)} %get-tuple-element.265), kind=kOutput, calls=%fused_computation.5.clone.1 | convolution fusion | flops 3221225472 | bytes 17302016 | tf_op jit(solution)/shard_map/while/body/eval_jaxpr/kab,kmbc->kmac/dot_general | solution.py:46
  442.0 9.3 copy.56
  452.6 5.3 convolution_bitcast_fusion.9
  459.4 11.4 %gather_fusion = f32[8,16,128,128]{3,2,1,0:T(8,128)} fusion(f32[20,16,128,128]{3,2,1,0:T(8,128)} %get-tuple-element.278, s32[1024]{0:T(1024)S(1)} %pad_clamp_fusion.5), kind=kCustom, calls=%fused_computation.1.clone.1 | custom fusion | bytes 16777248 | tf_op jit(solution)/shard_map/while/body/eval_jaxpr/gather | solution.py:45
  470.8 17.5 %convolution_bitcast_fusion.8 = f32[8,16,128,128]{2,3,1,0:T(8,128)} fusion(f32[8,16,128,128]{3,2,1,0:T(8,128)} %gather_fusion, f32[4,8,128,128]{3,2,1,0:T(8,128)} %get-tuple-element.279, s32[]{:T(128)} %get-tuple-element.265), kind=kOutput, calls=%fused_computation.5.clone.1 | convolution fusion | flops 3221225472 | bytes 17302016 | tf_op jit(solution)/shard_map/while/body/eval_jaxpr/kab,kmbc->kmac/dot_general | solution.py:46
  488.3 9.3 copy.56
  498.9 5.3 convolution_bitcast_fusion.9
  507.2 43.9 %all-reduce.6.cloned.1.call-done = f32[4,24,128,128]{3,2,1,0:T(8,128)} async-done(((f32[4,24,128,128]{3,2,1,0:T(8,128)}), f32[4,24,128,128]{3,2,1,0:T(8,128)}) %all-reduce.6.cloned.1.call-update) | async-done | bytes 6291472
  558.1 6.6 collective-permute-start.10
  566.9 64.0 %collective-permute-done.8 = f32[4,12,128,128]{3,2,1,0:T(8,128)} collective-permute-done((f32[4,12,128,128]{3,2,1,0:T(8,128)}, f32[4,12,128,128]{3,2,1,0:T(8,128)}, u32[]{:S(2)}, u32[]{:S(2)}) %collective-permute-start.8) | collective-permute-done | bytes 3145760 | tf_op jit(solution)/shard_map/ppermute | solution.py:12
  633.0 65.9 %collective-permute-done.9 = f32[4,12,128,128]{3,2,1,0:T(8,128)} collective-permute-done((f32[4,12,128,128]{3,2,1,0:T(8,128)}, f32[4,12,128,128]{3,2,1,0:T(8,128)}, u32[]{:S(2)}, u32[]{:S(2)}) %collective-permute-start.9) | collective-permute-done | bytes 3145760 | tf_op jit(solution)/shard_map/ppermute | solution.py:12
  703.5 58.7 %collective-permute-done.11 = f32[4,12,128,128]{3,2,1,0:T(8,128)} collective-permute-done((f32[4,12,128,128]{3,2,1,0:T(8,128)}, f32[4,12,128,128]{3,2,1,0:T(8,128)}, u32[]{:S(2)}, u32[]{:S(2)}) %collective-permute-start.11) | collective-permute-done | bytes 3145760 | tf_op jit(solution)/shard_map/ppermute | solution.py:12
  771.7 261.5 %while.23 = (s32[]{:T(128)}, f32[4,24,128,128]{3,2,1,0:T(8,128)}, s32[4,16]{1,0:T(4,128)S(1)}, s32[20,12]{1,0:T(8,128)S(1)}, s32[4,24]{1,0:T(4,128)}, /*index=5*...) while((s32[]{:T(128)}, f32[4,24,128,128]{3,2,1,0:T(8,128)}, s32[4,16]{1,0:T(4,128)S(1)}, ...), condition=%wide.region_7.8_spmd, body=%wide.region_6.7_spmd.sunk | while | flops 5737815040 | bytes 95958136 | solution.py:88
  771.7 11.3 %gather_fusion.2 = f32[16,12,128,128]{3,2,1,0:T(8,128)} fusion(f32[20,12,128,128]{3,2,1,0:T(8,128)} %get-tuple-element.302, s32[1024]{0:T(1024)S(1)} %get-tuple-element.255), kind=kCustom, calls=%fused_computation.3.clone.1 | custom fusion | bytes 25165888 | tf_op jit(solution)/shard_map/while/body/eval_jaxpr/gather | solution.py:81
  783.0 7.6 gather_fusion.3
  790.6 23.8 %convolution_bitcast_fusion.10 = f32[16,12,128,128]{2,3,1,0:T(8,128)} fusion(f32[16,12,128,128]{3,2,1,0:T(8,128)} %gather_fusion.2, f32[16,128,128]{2,1,0:T(8,128)S(1)} %gather_fusion.3), kind=kOutput, calls=%fused_computation.22.clone.1 | convolution fusion | flops 4831838208 | bytes 26214400 | tf_op jit(solution)/shard_map/while/body/eval_jaxpr/tba,tybc->tyac/dot_general | solution.py:82
  814.4 12.7 %copy.58 = f32[16,12,128,128]{3,0,1,2:T(8,128)} copy(f32[16,12,128,128]{2,3,1,0:T(8,128)} %convolution_bitcast_fusion.10) | data formatting | bytes 25165824 | tf_op jit(solution)/shard_map/while/body/eval_jaxpr/tba,tybc->tyac/transpose | solution.py:82
  828.5 7.1 convolution_bitcast_fusion.11
  837.1 11.3 %gather_fusion.2 = f32[16,12,128,128]{3,2,1,0:T(8,128)} fusion(f32[20,12,128,128]{3,2,1,0:T(8,128)} %get-tuple-element.302, s32[1024]{0:T(1024)S(1)} %get-tuple-element.255), kind=kCustom, calls=%fused_computation.3.clone.1 | custom fusion | bytes 25165888 | tf_op jit(solution)/shard_map/while/body/eval_jaxpr/gather | solution.py:81
  848.4 7.6 gather_fusion.3
  856.0 23.8 %convolution_bitcast_fusion.10 = f32[16,12,128,128]{2,3,1,0:T(8,128)} fusion(f32[16,12,128,128]{3,2,1,0:T(8,128)} %gather_fusion.2, f32[16,128,128]{2,1,0:T(8,128)S(1)} %gather_fusion.3), kind=kOutput, calls=%fused_computation.22.clone.1 | convolution fusion | flops 4831838208 | bytes 26214400 | tf_op jit(solution)/shard_map/while/body/eval_jaxpr/tba,tybc->tyac/dot_general | solution.py:82
  879.8 12.7 %copy.58 = f32[16,12,128,128]{3,0,1,2:T(8,128)} copy(f32[16,12,128,128]{2,3,1,0:T(8,128)} %convolution_bitcast_fusion.10) | data formatting | bytes 25165824 | tf_op jit(solution)/shard_map/while/body/eval_jaxpr/tba,tybc->tyac/transpose | solution.py:82
  893.9 7.1 convolution_bitcast_fusion.11
  902.5 11.3 %gather_fusion.2 = f32[16,12,128,128]{3,2,1,0:T(8,128)} fusion(f32[20,12,128,128]{3,2,1,0:T(8,128)} %get-tuple-element.302, s32[1024]{0:T(1024)S(1)} %get-tuple-element.255), kind=kCustom, calls=%fused_computation.3.clone.1 | custom fusion | bytes 25165888 | tf_op jit(solution)/shard_map/while/body/eval_jaxpr/gather | solution.py:81
  913.8 7.6 gather_fusion.3
  921.4 23.8 %convolution_bitcast_fusion.10 = f32[16,12,128,128]{2,3,1,0:T(8,128)} fusion(f32[16,12,128,128]{3,2,1,0:T(8,128)} %gather_fusion.2, f32[16,128,128]{2,1,0:T(8,128)S(1)} %gather_fusion.3), kind=kOutput, calls=%fused_computation.22.clone.1 | convolution fusion | flops 4831838208 | bytes 26214400 | tf_op jit(solution)/shard_map/while/body/eval_jaxpr/tba,tybc->tyac/dot_general | solution.py:82
  945.2 12.7 %copy.58 = f32[16,12,128,128]{3,0,1,2:T(8,128)} copy(f32[16,12,128,128]{2,3,1,0:T(8,128)} %convolution_bitcast_fusion.10) | data formatting | bytes 25165824 | tf_op jit(solution)/shard_map/while/body/eval_jaxpr/tba,tybc->tyac/transpose | solution.py:82
  959.3 7.1 convolution_bitcast_fusion.11
  967.8 11.3 %gather_fusion.2 = f32[16,12,128,128]{3,2,1,0:T(8,128)} fusion(f32[20,12,128,128]{3,2,1,0:T(8,128)} %get-tuple-element.302, s32[1024]{0:T(1024)S(1)} %get-tuple-element.255), kind=kCustom, calls=%fused_computation.3.clone.1 | custom fusion | bytes 25165888 | tf_op jit(solution)/shard_map/while/body/eval_jaxpr/gather | solution.py:81
  979.2 7.6 gather_fusion.3
  986.8 23.8 %convolution_bitcast_fusion.10 = f32[16,12,128,128]{2,3,1,0:T(8,128)} fusion(f32[16,12,128,128]{3,2,1,0:T(8,128)} %gather_fusion.2, f32[16,128,128]{2,1,0:T(8,128)S(1)} %gather_fusion.3), kind=kOutput, calls=%fused_computation.22.clone.1 | convolution fusion | flops 4831838208 | bytes 26214400 | tf_op jit(solution)/shard_map/while/body/eval_jaxpr/tba,tybc->tyac/dot_general | solution.py:82
  1010.5 12.7 %copy.58 = f32[16,12,128,128]{3,0,1,2:T(8,128)} copy(f32[16,12,128,128]{2,3,1,0:T(8,128)} %convolution_bitcast_fusion.10) | data formatting | bytes 25165824 | tf_op jit(solution)/shard_map/while/body/eval_jaxpr/tba,tybc->tyac/transpose | solution.py:82
  1024.6 7.1 convolution_bitcast_fusion.11
  1033.2 39.5 %all-reduce.8.cloned.1.call-done = f32[4,24,128,128]{3,2,1,0:T(8,128)} async-done(((f32[4,24,128,128]{3,2,1,0:T(8,128)}), f32[4,24,128,128]{3,2,1,0:T(8,128)}) %all-reduce.8.cloned.1.call-update) | async-done | bytes 6291472
  (109 shorter events, 81.1 us)
Async XLA Ops:
  7.2 543.9 %all-reduce.6.cloned.1.call-start = ((), (), s32[]{:S(2)}) async-start(), calls=%async_computation | async-start | bytes 12582912
  7.2 293.9 %collective-permute-start.4 = (f32[4,16,128,128]{3,2,1,0:T(8,128)}, f32[4,16,128,128]{3,2,1,0:T(8,128)}, u32[]{:S(2)}, u32[]{:S(2)}) collective-permute-start(f32[4,16,128,128]{3,2,1,0:T(8,128)} %param.12), channel_id=1, source_target_pairs={{0,4},{2,6},{4,8},{6,10},{8,12},{10,14},{12,16},{14,18},{16,20},{1... | collective-permute-start | bytes 12582920 | tf_op jit(solution)/shard_map/ppermute | solution.py:12
  10.9 292.9 %collective-permute-start.5 = (f32[4,16,128,128]{3,2,1,0:T(8,128)}, f32[4,16,128,128]{3,2,1,0:T(8,128)}, u32[]{:S(2)}, u32[]{:S(2)}) collective-permute-start(f32[4,16,128,128]{3,2,1,0:T(8,128)} %param.12), channel_id=1, source_target_pairs={{0,2},{2,4},{4,6},{6,8},{8,10},{10,12},{12,14},{14,16},{16,18},{18... | collective-permute-start | bytes 12582920 | tf_op jit(solution)/shard_map/ppermute | solution.py:12
  11.2 295.6 %collective-permute-start.6 = (f32[4,16,128,128]{3,2,1,0:T(8,128)}, f32[4,16,128,128]{3,2,1,0:T(8,128)}, u32[]{:S(2)}, u32[]{:S(2)}) collective-permute-start(f32[4,16,128,128]{3,2,1,0:T(8,128)} %param.12), channel_id=1, source_target_pairs={{0,126},{2,0},{4,2},{6,4},{8,6},{10,8},{12,10},{14,12},{16,14},{18... | collective-permute-start | bytes 12582920 | tf_op jit(solution)/shard_map/ppermute | solution.py:12
  17.7 291.5 %collective-permute-start.7 = (f32[4,16,128,128]{3,2,1,0:T(8,128)}, f32[4,16,128,128]{3,2,1,0:T(8,128)}, u32[]{:S(2)}, u32[]{:S(2)}) collective-permute-start(f32[4,16,128,128]{3,2,1,0:T(8,128)} %param.12), channel_id=1, source_target_pairs={{0,124},{2,126},{4,0},{6,2},{8,4},{10,6},{12,8},{14,10},{16,12},{1... | collective-permute-start | bytes 12582920 | tf_op jit(solution)/shard_map/ppermute | solution.py:12
  19.7 267.2 %collective-permute-start = (s32[4,40]{1,0:T(4,128)S(1)}, s32[4,40]{1,0:T(4,128)S(1)}, u32[]{:S(2)}, u32[]{:S(2)}) collective-permute-start(s32[4,40]{1,0:T(4,128)S(1)} %pad_add_fusion), channel_id=1, source_target_pairs={{0,4},{2,6},{4,8},{6,10},{8,12},{10,14},{12,16},{14,18},{16,20},{1... | collective-permute-start | bytes 1928 | tf_op jit(solution)/shard_map/ppermute | solution.py:12
  286.8 7.9 collective-permute-start.1
  294.7 2.4 collective-permute-start.2
  297.1 3.9 collective-permute-start.3
  301.1 5.1 copy-start.2
  311.7 8.8 copy-start.1
  320.5 185.4 %copy-start.3 = (u32[128]{0:T(128)S(1)}, u32[128]{0:T(128)}, u32[]{:S(2)}) copy-start(u32[128]{0:T(128)} %constant.122) | copy-start | bytes 1540
  505.7 567.0 %all-reduce.8.cloned.1.call-start = ((), (), s32[]{:S(2)}) async-start(), calls=%async_computation.1 | async-start | bytes 12582912
  555.0 75.9 %collective-permute-start.8 = (f32[4,12,128,128]{3,2,1,0:T(8,128)}, f32[4,12,128,128]{3,2,1,0:T(8,128)}, u32[]{:S(2)}, u32[]{:S(2)}) collective-permute-start(f32[4,12,128,128]{3,2,1,0:T(8,128)} %constant_dynamic-slice_fusion.5), channel_id=1, source_target_pairs={{0,4},{2,6},{4,8},{6,10},{8,12},{10,14},{12,16},{14,18},{16,20},{1... | collective-permute-start | bytes 9437192 | tf_op jit(solution)/shard_map/ppermute | solution.py:12
  557.8 141.1 %collective-permute-start.9 = (f32[4,12,128,128]{3,2,1,0:T(8,128)}, f32[4,12,128,128]{3,2,1,0:T(8,128)}, u32[]{:S(2)}, u32[]{:S(2)}) collective-permute-start(f32[4,12,128,128]{3,2,1,0:T(8,128)} %constant_dynamic-slice_fusion.5), channel_id=1, source_target_pairs={{0,2},{2,4},{4,6},{6,8},{8,10},{10,12},{12,14},{14,16},{16,18},{18... | collective-permute-start | bytes 9437192 | tf_op jit(solution)/shard_map/ppermute | solution.py:12
  558.1 143.4 %collective-permute-start.10 = (f32[4,12,128,128]{3,2,1,0:T(8,128)}, f32[4,12,128,128]{3,2,1,0:T(8,128)}, u32[]{:S(2)}, u32[]{:S(2)}) collective-permute-start(f32[4,12,128,128]{3,2,1,0:T(8,128)} %constant_dynamic-slice_fusion.5), channel_id=1, source_target_pairs={{0,126},{2,0},{4,2},{6,4},{8,6},{10,8},{12,10},{14,12},{16,14},{18... | collective-permute-start | bytes 9437192 | tf_op jit(solution)/shard_map/ppermute | solution.py:12
  564.7 197.6 %collective-permute-start.11 = (f32[4,12,128,128]{3,2,1,0:T(8,128)}, f32[4,12,128,128]{3,2,1,0:T(8,128)}, u32[]{:S(2)}, u32[]{:S(2)}) collective-permute-start(f32[4,12,128,128]{3,2,1,0:T(8,128)} %constant_dynamic-slice_fusion.5), channel_id=1, source_target_pairs={{0,124},{2,126},{4,0},{6,2},{8,4},{10,6},{12,8},{14,10},{16,12},{1... | collective-permute-start | bytes 9437192 | tf_op jit(solution)/shard_map/ppermute | solution.py:12
  566.5 134.5 %slice-start = ((s8[6291456]{0:T(1024)(128)(4,1)}), s8[4194304]{0:T(1024)(128)(4,1)S(1)}, s32[]{:S(2)}) async-start(s8[6291456]{0:T(1024)(128)(4,1)} %bitcast.115), calls=%async_computation.2 | async-start | bytes 8388608
  566.9 134.2 %slice-start.1 = ((s8[6291456]{0:T(1024)(128)(4,1)}), s8[2097152]{0:T(1024)(128)(4,1)S(1)}, s32[]{:S(2)}) async-start(s8[6291456]{0:T(1024)(128)(4,1)} %bitcast.115), calls=%async_computation.3 | async-start | bytes 4194304
  764.4 7.3 copy-start
Sparse Core Ops, SparseCore 0:
  505.8 45.2 all-reduce.5
  1033.3 39.3 all-reduce.7
where the time goes:
time: 1090 us; the launch traced here: 1080 us
  waiting for transfers between devices  551 us (51%)
  local copies, waits for them, and re-layouts  276 us (25%)
  matrix products  215 us (20%)
  starting transfers between devices  23.8 us (2%)
  between operations  14.9 us (1%)
    ppermute x12, waiting for transfers between devices, passed_along(): lax.ppermute(array, axis, [(i, (i + by) % devices) for i in range(devices)])  467 us
    dot_general x4, matrix products, metric_row(): jnp.einsum('tba,tybc->tyac', factor_here, product_here, precision=HIGHEST)  95.2 us
    unnamed x4, waiting for transfers between devices  83.4 us
    dot_general x4, matrix products, product_row(): jnp.einsum('kab,kmbc->kmac', margin_row, picked, precision=HIGHEST)  70.2 us
    transpose x4, local copies, waits for them, and re-layouts, metric_row(): jnp.einsum('tba,tybc->tyac', factor_here, product_here, precision=HIGHEST)  51 us
    gather x4, local copies, waits for them, and re-layouts, product_row(): picked = halo_factor[relative_row]  45.6 us
    gather x4, local copies, waits for them, and re-layouts, metric_row(): product_here = halo_product[source_rows]  45.3 us
    transpose x4, local copies, waits for them, and re-layouts, product_row(): jnp.einsum('kab,kmbc->kmac', margin_row, picked, precision=HIGHEST)  37.2 us
  transfers between devices with their start and end apart: 14, of which 9 were waited for; matrix products, arithmetic and copies ran while one was open for 2% of the time, Pallas kernels for 0%

commit v1 on v0

v1 whole, which is shorter than its diff:
```python
import functools

import jax
import jax.numpy as jnp
from jax import lax
from jax.experimental import pallas as pl
from jax.experimental.pallas import tpu as pltpu
from jax.sharding import PartitionSpec as P

F32 = jnp.float32
BF16 = jnp.bfloat16
WINDOW = 36


def ring(array, by):
    devices = lax.axis_size("rows")
    return lax.ppermute(array, "rows", [(i, (i + by) % devices) for i in range(devices)])


def swap(array):
    return lax.ppermute(array, "rep", [(0, 1), (1, 0)])


def split(block):
    high = block.astype(BF16)
    return high, (block - high.astype(F32)).astype(BF16)


def wrap(index, total):
    if total & (total - 1) == 0:
        return jnp.bitwise_and(index, total - 1)
    return lax.rem(index + total, total)


def clear(ref, first=0, last=None):
    zero = jnp.zeros(ref.shape[1:], ref.dtype)

    def body(i, carry):
        ref[i] = zero
        return carry

    lax.fori_loop(first, ref.shape[0] if last is None else last, body, 0, unroll=4)


def margin_left_kernel(total, meta, cols_a, cols_b, table_a, table_b, out):
    position, core = meta[0], meta[1]
    for group in range(5):
        for c in range(2):
            clear(out.at[group, c])
    first = 4 * position - 8
    for cols, table in ((cols_a, table_a), (cols_b, table_b)):
        for row in range(4):

            def body(k, carry, cols=cols, table=table, row=row):
                rel = wrap(cols[row, k] - first, total)
                within = jnp.bitwise_and(rel, 3) - 2 * core

                @pl.when((within >= 0) & (within < 2))
                def _():
                    group = lax.shift_right_logical(rel, 2)
                    high, low = split(table[row, k])
                    out[group, within, row, :, :128] = high
                    out[group, within, row, :, 128:] = low

                return carry

            lax.fori_loop(0, table.shape[1], body, 0)


def factor_left_kernel(total, meta, *refs):
    patterns, tables, out = refs[:5], refs[5:15], refs[15]
    position = meta[0]
    for group in range(5):
        for c in range(2):
            clear(out.at[group, c])
            cols, table = patterns[group], tables[2 * group + c]

            def body(m, carry, cols=cols, table=table, group=group, c=c):
                rel = wrap(cols[c, m] - 4 * position, total)

                @pl.when(rel < 4)
                def _():
                    high, low = split(table[m].T)
                    out[group, c, rel, :, :128] = high
                    out[group, c, rel, :, 128:] = low

                return carry

            lax.fori_loop(0, table.shape[0], body, 0)


def stage_kernel(gs, crs, starts, counts, total, by_rows, row0, col0, has_acc, *refs):
    count, depth = len(gs), len(crs)
    meta, outcols = refs[:2]
    patterns = refs[2 : 2 + count]
    refs = refs[2 + count :]
    lefts, tables = refs[0], refs[1 : 1 + count * depth]
    refs = refs[1 + count * depth :]
    acc = None
    if has_acc:
        acc, refs = refs[:2], refs[2:]
    outs, refs = refs[:2], refs[2:]
    right_high, right_low, dense = refs
    core = meta[1]
    base = 4 * meta[0] - 16
    rows = dense.shape[1]
    spare = right_high.shape[1] - 1
    for gi in range(count):
        clear(right_high.at[gi], 0, counts[gi])
        clear(right_low.at[gi], 0, counts[gi])
        for ci, c in enumerate(crs):
            cols, table = patterns[gi], tables[gi * depth + ci]

            def right_body(m, carry, gi=gi, ci=ci, c=c, cols=cols, table=table):
                rel = wrap(cols[c, col0 + m] - base, total) - starts[gi]
                rel = jnp.where((rel >= 0) & (rel < counts[gi]), rel, spare)
                high, low = split(table[m])
                right_high[gi, rel, ci] = high
                right_low[gi, rel, ci] = low
                return carry

            lax.fori_loop(0, table.shape[0], right_body, 0, unroll=4)

    def left_of(g, c):
        if rows == 4:
            return lefts[g + 2, c]
        if by_rows:
            return jnp.stack([lefts[g + 2, c, row0], lefts[g + 2, c, 2 + row0]])
        return lefts[g + 2, c, row0 : row0 + 2]

    def rights(ref, gi, at):
        return jnp.concatenate(
            [ref[gi, at].reshape(128 * depth, 128), ref[gi, at + 1].reshape(128 * depth, 128)], axis=1
        )

    done = (0, 0)
    for gi, g in enumerate(gs):
        left = [left_of(g, c).reshape(rows * 128, 256) for c in crs]
        highs = [part[:, :128] for part in left]
        lows = [part[:, 128:] for part in left]
        left = jnp.concatenate(highs + lows + highs, axis=1)

        def body(q, carry, gi=gi, left=left, add=False):
            rh, rl = rights(right_high, gi, 2 * q), rights(right_low, gi, 2 * q)
            out = jnp.dot(left, jnp.concatenate([rh, rh, rl], axis=0), preferred_element_type=F32)
            to = starts[gi] + 2 * q
            for j in range(2):
                value = out[:, 128 * j : 128 * j + 128].reshape(rows, 128, 128)
                dense[to + j] = dense[to + j] + value if add else value
            return carry

        start, stop = starts[gi], starts[gi] + counts[gi]
        low, high = max(start, done[0]), min(stop, done[1])
        if low >= high:
            spans = [(start, stop, False)]
        else:
            spans = [(start, low, False), (low, high, True), (high, stop, False)]
        for first, last, add in spans:
            if last > first:
                lax.fori_loop(
                    (first - start) // 2, (last - start) // 2, functools.partial(body, add=add), 0, unroll=2
                )
        done = (start, stop) if gi == 0 else (min(start, done[0]), max(stop, done[1]))
    clear(dense, 0, done[0])
    clear(dense, done[1], WINDOW)
    kept_rows, kept_cols = outs[0].shape[:2]
    for which in range(2):
        side = core if which == 0 else 1 - core
        for row in range(kept_rows):
            source = side * kept_rows + row if by_rows else row
            at_row = 2 * side + row0 + row if by_rows else row0 + row
            at_col = 0 if by_rows else kept_cols * side

            def out_body(y, carry, which=which, row=row, source=source, at_row=at_row, at_col=at_col):
                rel = wrap(outcols[at_row, at_col + y] - base, total)
                value = dense[rel, source]
                if acc is not None:
                    value = value + acc[which][row, y]
                outs[which][row, y] = value
                return carry

            lax.fori_loop(0, kept_cols, out_body, 0, unroll=4)


SMEM = pl.BlockSpec(memory_space=pltpu.SMEM)
VMEM = pl.BlockSpec(memory_space=pltpu.VMEM)
PARAMS = pltpu.CompilerParams(vmem_limit_bytes=60 << 20)


def stage(name, gs, crs, by_rows, part, total, meta, outcols, patterns, left, tables, acc, col0):
    if by_rows:
        starts, counts = [4 * (g + 2) for g in gs], [20] * len(gs)
        out = (2 if part is None else 1, outcols.shape[1], 128, 128)
        row0, rows = part or 0, 2 * out[0]
    else:
        starts, counts = [max(0, 4 * g) for g in gs], [WINDOW - 4 * abs(g) for g in gs]
        out = (4 if part is None else 2, outcols.shape[1] // 2, 128, 128)
        row0, rows = 2 * (part or 0), out[0]
    kernel = functools.partial(
        stage_kernel, gs, crs, starts, counts, total, by_rows, row0, col0, bool(acc)
    )
    shape = jax.ShapeDtypeStruct(out, F32)
    blocks = [tables[g][c] for g in gs for c in crs]
    window = max(counts)
    return pl.pallas_call(
        kernel,
        name=name,
        out_shape=[shape, shape],
        in_specs=[SMEM] * (2 + len(gs)) + [VMEM] * (1 + len(blocks) + len(acc)),
        out_specs=[VMEM, VMEM],
        scratch_shapes=[
            pltpu.VMEM((len(gs), window + 1, len(crs), 128, 128), BF16),
            pltpu.VMEM((len(gs), window + 1, len(crs), 128, 128), BF16),
            pltpu.VMEM((WINDOW, rows, 128, 128), F32),
        ],
        compiler_params=PARAMS,
        cost_estimate=pl.CostEstimate(
            flops=0,
            transcendentals=0,
            bytes_accessed=0,
        ),
    )(meta, outcols, *[patterns[g] for g in gs], left, *blocks, *acc)


def left_call(kernel, name, scalars, arrays):
    out = jax.ShapeDtypeStruct((5, 2, 4, 128, 256), BF16)
    return pl.pallas_call(
        kernel,
        name=name,
        out_shape=out,
        in_specs=[SMEM] * len(scalars) + [VMEM] * len(arrays),
        out_specs=VMEM,
        compiler_params=PARAMS,
        cost_estimate=pl.CostEstimate(
            flops=0, transcendentals=0, bytes_accessed=0
        ),
    )(*scalars, *arrays)


def halo(own, after_near):
    tables = {0: own}
    near = {g: [ring(a, -g) for a in own] for g in (-1, 1)}
    tables.update(near)
    (first, second), tied = after_near((near[-1][0], near[1][0]))
    tables[-2] = [ring(first, 1)]
    tables[2] = [ring(second, -1)]
    tables[-2].append(ring(near[-1][1], 1))
    tables[2].append(ring(near[1][1], -1))
    return tables, tied


def shards(margin_blocks, margin_cols, factor_blocks, factor_cols, product_cols, metric_cols):
    total = factor_blocks.shape[0] * lax.axis_size("rows")
    position = lax.axis_index("rows")
    core = lax.axis_index("rep")
    meta = jnp.stack([position, core]).astype(jnp.int32)
    slots = factor_cols.shape[1]
    own = [lax.dynamic_index_in_dim(factor_blocks, 2 * core + c, 0, keepdims=False) for c in range(2)]
    patterns = {0: lax.dynamic_slice_in_dim(jnp.concatenate([factor_cols, product_cols], axis=1), 2 * core, 2, 0)}
    for g in (-2, -1, 1, 2):
        patterns[g] = ring(patterns[0], -g)

    def margin_after(near):
        other = swap(margin_blocks)
        other_cols = swap(margin_cols)
        left = left_call(
            functools.partial(margin_left_kernel, total), "margin_left",
            [meta, margin_cols, other_cols], [margin_blocks, other],
        )
        return lax.optimization_barrier((near, (left, patterns)))

    factors, (left, patterns) = halo(own, margin_after)
    part = lambda name, gs, crs, which, acc: stage(
        name, gs, crs, True, which, total, meta, product_cols, patterns, left, factors, acc, 0
    )
    acc = part("product_near", (0, -1, 1), (0, 1), None, ())
    acc = part("product_far0", (-2, 2), (0,), None, acc)
    base = acc[0] + swap(acc[1])
    finals = [part("product_far1", (-2, 2), (1,), which, ()) for which in range(2)]
    rows = [kept[0] + swap(sent)[0] + base[c] for c, (kept, sent) in enumerate(finals)]

    def product_after(near):
        both = jnp.stack(rows)
        width = both.shape[1] // 2
        mine = lax.dynamic_slice_in_dim(both, core * width, width, 1)
        theirs = swap(lax.dynamic_slice_in_dim(both, (1 - core) * width, width, 1))
        low, high = jnp.where(core == 0, mine, theirs), jnp.where(core == 0, theirs, mine)
        return lax.optimization_barrier((near, jnp.concatenate([low, high], axis=0)))

    products, product = halo(rows, product_after)
    left = left_call(
        functools.partial(factor_left_kernel, total), "factor_left",
        [meta] + [patterns[g] for g in range(-2, 3)], [factors[g][c] for g in range(-2, 3) for c in range(2)],
    )
    part = lambda name, gs, crs, which, acc: stage(
        name, gs, crs, False, which, total, meta, metric_cols, patterns, left, products, acc, slots
    )
    acc = part("metric_own", (0,), (0, 1), None, ())
    acc = part("metric_near", (-1, 1), (0, 1), None, acc)
    acc = part("metric_far0", (-2, 2), (0,), None, acc)
    base = acc[0] + swap(acc[1])
    finals = [part("metric_far1", (-2, 2), (1,), which, ()) for which in range(2)]
    metric = jnp.concatenate([kept + swap(sent) for kept, sent in finals], axis=0) + base
    return (product, metric)


def solution(mesh):
    return jax.shard_map(
        shards,
        mesh=mesh,
        in_specs=(
            P("rows", "rep", None, None),
            P("rows", "rep"),
            P("rows", None, None, None),
            P("rows", None),
            P("rows", None),
            P("rows", None),
        ),
        out_specs=(P("rows", "rep", None, None), P("rows", "rep", None, None)),
        check_vma=False,
    )
```

time: 1090 us -> 345 us (0.32)
  waiting for transfers between devices: 551 us -> 131 us
  local copies, waits for them, and re-layouts: 276 us -> 8.83 us
  matrix products: 215 us -> 0 us
  Pallas kernels: 0 us -> 130 us
  starting transfers between devices: 23.8 us -> 57.9 us
  between operations: 14.9 us -> 0.87 us
  other arithmetic: 3.33 us -> 16 us
    ppermute x12 -> x29, waiting for transfers between devices: 467 us -> 131 us  [the longest x20 126 us: ring(): lax.ppermute(array, 'rows', [(i, (i + by) % devices) for i in range(devic...]
    dot_general x16 -> x0, matrix products: 215 us -> none  [the longest x4 95.2 us: metric_row(): jnp.einsum('tba,tybc->tyac', factor_here, product_here, precision=HIGHEST)]
    pallas_call x0 -> x11, Pallas kernels: none -> 130 us  [the longest x9 113 us: stage(): pl.pallas_call(kernel, name=name, out_shape=[shape, shape], in_specs=[SME...]
    gather x24 -> x0, local copies, waits for them, and re-layouts: 126 us -> none  [the longest x4 45.6 us: product_row(): picked = halo_factor[relative_row]]
    transpose x8 -> x0, local copies, waits for them, and re-layouts: 88.2 us -> none  [the longest x4 51 us: metric_row(): jnp.einsum('tba,tybc->tyac', factor_here, product_here, precision=HIGHEST)]
    unnamed x4 -> x0, waiting for transfers between devices: 83.4 us -> none
    ppermute x12 -> x29, starting transfers between devices: 23.5 us -> 57.9 us  [the longest x20 48.6 us: ring(): lax.ppermute(array, 'rows', [(i, (i + by) % devices) for i in range(devic...]
    unnamed x24 -> x54, local copies, waits for them, and re-layouts: 31.6 us -> 7.1 us
  transfers between devices with their start and end apart: 14 -> 29, of which waited for: 9 -> 13; matrix products, arithmetic and copies ran while one was open for 2% -> 3% of each run, Pallas kernels for 0% -> 34%
where the time goes in v1:
time: 345 us
  waiting for transfers between devices  131 us (38%)
  Pallas kernels  130 us (38%)
  starting transfers between devices  57.9 us (17%)
  other arithmetic  16 us (5%)
  local copies, waits for them, and re-layouts  8.83 us (3%)
    ppermute x20, waiting for transfers between devices, ring(): lax.ppermute(array, 'rows', [(i, (i + by) % devices) for i in range(devic...  126 us
    pallas_call x9, Pallas kernels, stage(): pl.pallas_call(kernel, name=name, out_shape=[shape, shape], in_specs=[SME...  113 us
    ppermute x20, starting transfers between devices, ring(): lax.ppermute(array, 'rows', [(i, (i + by) % devices) for i in range(devic...  48.6 us
    pallas_call x2, Pallas kernels, left_call(): pl.pallas_call(kernel, name=name, out_shape=out, in_specs=[SMEM] * len(sc...  16.6 us
    ppermute x9, starting transfers between devices, swap(): return lax.ppermute(array, 'rep', [(0, 1), (1, 0)])  9.33 us
    unnamed x54, local copies, waits for them, and re-layouts  7.1 us
  transfers between devices with their start and end apart: 29, of which 13 were waited for; matrix products, arithmetic and copies ran while one was open for 3% of the time, Pallas kernels for 34%

profile of v1, /device:TPU:1, one launch (start us, length us, event | category | flops | bytes accessed | tf_op | source)
XLA Modules:
  0.0 344.7 jit_solution(4883796944822061161)
XLA Ops:
  0.6 1.5 collective-permute-start.3
  2.1 1.7 dynamic-slice_bitcast_fusion
  3.9 1.4 collective-permute-start
  5.2 7.3 %collective-permute-start.1 = (f32[16,128,128]{2,1,0:T(8,128)S(1)}, f32[16,128,128]{2,1,0:T(8,128)}, u32[]{:S(2)}, u32[]{:S(2)}) collective-permute-start(f32[16,128,128]{2,1,0:T(8,128)S(1)} %get-tuple-element.63.refs_6_.refs_9_), channel_id=1, source_target_pairs={{0,126},{2,0},{4,2},{6,4},{8,6},{10,8},{12,10},{14,12},{16,14},{18... | collective-permute-start | bytes 3145736 | tf_op jit(solution)/shard_map/ppermute | solution.py:17
  14.6 22.1 %collective-permute-done.4.refs_2_.refs_0_ = s32[2,40]{1,0:T(2,128)S(1)} collective-permute-done((s32[2,40]{1,0:T(2,128)S(1)}, s32[2,40]{1,0:T(2,128)S(1)}, u32[]{:S(2)}, u32[]{:S(2)}) %collective-permute-start.4) | collective-permute-done | bytes 352 | tf_op jit(solution)/shard_map/ppermute | solution.py:17
  36.6 1.5 collective-permute-start.6
  38.8 5.3 %margin_left.1.refs_4_.refs_5_ = bf16[5,2,4,128,256]{4,3,2,1,0:T(8,128)(2,1)} custom-call(s32[2]{0:T(128)} %pad_add_fusion.1.meta.refs_0_, s32[4,8]{1,0:T(4,128)} %cols_a.1, s32[4,8]{1,0:T(4,128)} %copy-done.25, f32[4,8,128,128]{3,2,1,0:T(8,128)} %table_a.1, f32[4,8,128,128]{3,2,1,0:T(8,128)} %collective-permute-done.3.table_b), custom_call_target="tpu_custom_call" | custom-call | tf_op jit(solution)/shard_map/margin_left/pallas_call | solution.py:227
  44.2 1.6 collective-permute-start.10
  46.4 6.5 %collective-permute-start.14 = (f32[16,128,128]{2,1,0:T(8,128)}, f32[16,128,128]{2,1,0:T(8,128)}, u32[]{:S(2)}, u32[]{:S(2)}) collective-permute-start(f32[16,128,128]{2,1,0:T(8,128)} %collective-permute-done.1.refs_10_.refs_11_), channel_id=1, source_target_pairs={{0,126},{2,0},{4,2},{6,4},{8,6},{10,8},{12,10},{14,12},{16,14},{18... | collective-permute-start | bytes 3145736 | tf_op jit(solution)/shard_map/ppermute | solution.py:17
  52.9 14.1 %collective-permute-done.10.refs_11_.refs_12_ = f32[16,128,128]{2,1,0:T(8,128)S(1)} collective-permute-done((f32[16,128,128]{2,1,0:T(8,128)S(1)}, f32[16,128,128]{2,1,0:T(8,128)S(1)}, u32[]{:S(2)}, u32[]{:S(2)}) %collective-permute-start.10) | collective-permute-done | bytes 1048608 | tf_op jit(solution)/shard_map/ppermute | solution.py:17
  68.0 6.0 %collective-permute-done.8.refs_9_.refs_8_ = f32[16,128,128]{2,1,0:T(8,128)} collective-permute-done((f32[16,128,128]{2,1,0:T(8,128)S(1)}, f32[16,128,128]{2,1,0:T(8,128)}, u32[]{:S(2)}, u32[]{:S(2)}) %collective-permute-start.8) | collective-permute-done | bytes 1048608 | tf_op jit(solution)/shard_map/ppermute | solution.py:17
  74.1 17.5 %product_near.1 = (f32[2,24,128,128]{3,2,1,0:T(8,128)}, f32[2,24,128,128]{3,2,1,0:T(8,128)}) custom-call(s32[2]{0:T(128)} %pad_add_fusion.1.meta.refs_0_, s32[4,24]{1,0:T(4,128)} %refs_1_.12, s32[2,40]{1,0:T(2,128)} %copy-done.21, s32[2,40]{1,0:T(2,128)} %copy-done.22, s32[2,40]{1,0:T(2,128)} %copy-done.23, ...), custom_call_target="tpu_custom_call" | custom-call | tf_op jit(solution)/shard_map/product_near/pallas_call | solution.py:205
  91.6 4.9 %collective-permute-done.13.refs_5_ = f32[16,128,128]{2,1,0:T(8,128)S(1)} collective-permute-done((f32[16,128,128]{2,1,0:T(8,128)S(1)}, f32[16,128,128]{2,1,0:T(8,128)S(1)}, u32[]{:S(2)}, u32[]{:S(2)}) %collective-permute-start.13) | collective-permute-done | bytes 1048608 | tf_op jit(solution)/shard_map/ppermute | solution.py:17
  96.4 1.1 copy-done.11
  97.5 12.7 %product_far0.1 = (f32[2,24,128,128]{3,2,1,0:T(8,128)}, f32[2,24,128,128]{3,2,1,0:T(8,128)}) custom-call(s32[2]{0:T(128)} %pad_add_fusion.1.meta.refs_0_, s32[4,24]{1,0:T(4,128)} %refs_1_.12, s32[2,40]{1,0:T(2,128)} %copy-done.19, s32[2,40]{1,0:T(2,128)} %copy-done.20, bf16[5,2,4,128,256]{4,3,2,1,0:T(8,128)(2,1)} %margin_left.1.refs_4_.refs_5_, ...), custom_call_target="tpu_custom_call" | custom-call | tf_op jit(solution)/shard_map/product_far0/pallas_call | solution.py:205
  110.2 2.9 collective-permute-start.15
  113.1 1.5 collective-permute-start.9
  114.6 23.2 %collective-permute-done.11.refs_6_.refs_14_ = f32[16,128,128]{2,1,0:T(8,128)S(1)} collective-permute-done((f32[16,128,128]{2,1,0:T(8,128)S(1)}, f32[16,128,128]{2,1,0:T(8,128)S(1)}, u32[]{:S(2)}, u32[]{:S(2)}) %collective-permute-start.11) | collective-permute-done | bytes 1048608 | tf_op jit(solution)/shard_map/ppermute | solution.py:17
  137.8 5.5 %collective-permute-done.9.refs_5_.refs_6_ = f32[16,128,128]{2,1,0:T(8,128)S(1)} collective-permute-done((f32[16,128,128]{2,1,0:T(8,128)}, f32[16,128,128]{2,1,0:T(8,128)S(1)}, u32[]{:S(2)}, u32[]{:S(2)}) %collective-permute-start.9) | collective-permute-done | bytes 1048608 | tf_op jit(solution)/shard_map/ppermute | solution.py:17
  144.3 7.9 %product_far1.2 = (f32[1,24,128,128]{3,2,1,0:T(8,128)}, f32[1,24,128,128]{3,2,1,0:T(8,128)}) custom-call(s32[2]{0:T(128)} %pad_add_fusion.1.meta.refs_0_, s32[4,24]{1,0:T(4,128)} %refs_1_.12, s32[2,40]{1,0:T(2,128)} %copy-done.19, s32[2,40]{1,0:T(2,128)} %copy-done.20, bf16[5,2,4,128,256]{4,3,2,1,0:T(8,128)(2,1)} %margin_left.1.refs_4_.refs_5_, ...), custom_call_target="tpu_custom_call" | custom-call | tf_op jit(solution)/shard_map/product_far1/pallas_call | solution.py:205
  153.3 8.0 %product_far1.3 = (f32[1,24,128,128]{3,2,1,0:T(8,128)}, f32[1,24,128,128]{3,2,1,0:T(8,128)}) custom-call(s32[2]{0:T(128)} %pad_add_fusion.1.meta.refs_0_, s32[4,24]{1,0:T(4,128)} %refs_1_.12, s32[2,40]{1,0:T(2,128)} %copy-done.19, s32[2,40]{1,0:T(2,128)} %copy-done.20, bf16[5,2,4,128,256]{4,3,2,1,0:T(8,128)(2,1)} %margin_left.1.refs_4_.refs_5_, ...), custom_call_target="tpu_custom_call" | custom-call | tf_op jit(solution)/shard_map/product_far1/pallas_call | solution.py:205
  161.4 2.5 add.58
  163.9 1.0 collective-permute-done.18
  165.0 2.8 slice_add_fusion
  167.8 1.4 fusion
  169.4 6.9 %collective-permute-start.17 = (f32[24,128,128]{2,1,0:T(8,128)S(1)}, f32[24,128,128]{2,1,0:T(8,128)}, u32[]{:S(2)}, u32[]{:S(2)}) collective-permute-start(f32[24,128,128]{2,1,0:T(8,128)S(1)} %bitcast.12), channel_id=1, source_target_pairs={{0,126},{2,0},{4,2},{6,4},{8,6},{10,8},{12,10},{14,12},{16,14},{18... | collective-permute-start | bytes 4718600 | tf_op jit(solution)/shard_map/ppermute | solution.py:17
  176.3 6.9 %collective-permute-start.22 = (f32[24,128,128]{2,1,0:T(8,128)S(1)}, f32[24,128,128]{2,1,0:T(8,128)}, u32[]{:S(2)}, u32[]{:S(2)}) collective-permute-start(f32[24,128,128]{2,1,0:T(8,128)S(1)} %bitcast.9), channel_id=1, source_target_pairs={{0,126},{2,0},{4,2},{6,4},{8,6},{10,8},{12,10},{14,12},{16,14},{18... | collective-permute-start | bytes 4718600 | tf_op jit(solution)/shard_map/ppermute | solution.py:17
  183.2 1.7 broadcast_select_fusion.1
  184.9 2.0 pad_maximum_fusion
  186.9 23.6 %collective-permute-done.16.refs_5_ = f32[24,128,128]{2,1,0:T(8,128)} collective-permute-done((f32[24,128,128]{2,1,0:T(8,128)S(1)}, f32[24,128,128]{2,1,0:T(8,128)}, u32[]{:S(2)}, u32[]{:S(2)}) %collective-permute-start.16) | collective-permute-done | bytes 1572896 | tf_op jit(solution)/shard_map/ppermute | solution.py:17
  210.5 6.9 %collective-permute-start.27 = (f32[24,128,128]{2,1,0:T(8,128)}, f32[24,128,128]{2,1,0:T(8,128)}, u32[]{:S(2)}, u32[]{:S(2)}) collective-permute-start(f32[24,128,128]{2,1,0:T(8,128)} %collective-permute-done.17.refs_7_), channel_id=1, source_target_pairs={{0,126},{2,0},{4,2},{6,4},{8,6},{10,8},{12,10},{14,12},{16,14},{18... | collective-permute-start | bytes 4718600 | tf_op jit(solution)/shard_map/ppermute | solution.py:17
  217.4 11.3 %factor_left.1.refs_4_.refs_3_ = bf16[5,2,4,128,256]{4,3,2,1,0:T(8,128)(2,1)} custom-call(s32[2]{0:T(128)} %pad_add_fusion.1.meta.refs_0_, s32[2,40]{1,0:T(2,128)} %copy-done.19, s32[2,40]{1,0:T(2,128)} %copy-done.22, s32[2,40]{1,0:T(2,128)} %copy-done.21, s32[2,40]{1,0:T(2,128)} %copy-done.23, s32[2,40]{1,0:T(2,128)} %copy-done.20, ...), custom_call_target="tpu_custom_call" | custom-call | tf_op jit(solution)/shard_map/factor_left/pallas_call | solution.py:227
  228.7 12.3 %metric_own.1 = (f32[4,12,128,128]{3,2,1,0:T(8,128)}, f32[4,12,128,128]{3,2,1,0:T(8,128)}) custom-call(s32[2]{0:T(128)} %pad_add_fusion.1.meta.refs_0_, s32[4,24]{1,0:T(4,128)} %refs_1_.17, s32[2,40]{1,0:T(2,128)} %copy-done.21, bf16[5,2,4,128,256]{4,3,2,1,0:T(8,128)(2,1)} %factor_left.1.refs_4_.refs_3_, f32[24,128,128]{2,1,0:T(8,128)} %bitcast.13, ...), custom_call_target="tpu_custom_call" | custom-call | tf_op jit(solution)/shard_map/metric_own/pallas_call | solution.py:205
  240.9 3.3 collective-permute-done.20.refs_6_
  244.2 6.9 %collective-permute-start.23 = (f32[24,128,128]{2,1,0:T(8,128)}, f32[24,128,128]{2,1,0:T(8,128)S(1)}, u32[]{:S(2)}, u32[]{:S(2)}) collective-permute-start(f32[24,128,128]{2,1,0:T(8,128)} %collective-permute-done.22.refs_8_), channel_id=1, source_target_pairs={{0,126},{2,0},{4,2},{6,4},{8,6},{10,8},{12,10},{14,12},{16,14},{18... | collective-permute-start | bytes 4718600 | tf_op jit(solution)/shard_map/ppermute | solution.py:17
  251.1 20.1 %metric_near.1 = (f32[4,12,128,128]{3,2,1,0:T(8,128)}, f32[4,12,128,128]{3,2,1,0:T(8,128)}) custom-call(s32[2]{0:T(128)} %pad_add_fusion.1.meta.refs_0_, s32[4,24]{1,0:T(4,128)} %refs_1_.17, s32[2,40]{1,0:T(2,128)} %copy-done.22, s32[2,40]{1,0:T(2,128)} %copy-done.23, bf16[5,2,4,128,256]{4,3,2,1,0:T(8,128)(2,1)} %factor_left.1.refs_4_.refs_3_, ...), custom_call_target="tpu_custom_call" | custom-call | tf_op jit(solution)/shard_map/metric_near/pallas_call | solution.py:205
  271.2 6.8 %collective-permute-done.26.refs_5_ = f32[24,128,128]{2,1,0:T(8,128)} collective-permute-done((f32[24,128,128]{2,1,0:T(8,128)}, f32[24,128,128]{2,1,0:T(8,128)}, u32[]{:S(2)}, u32[]{:S(2)}) %collective-permute-start.26) | collective-permute-done | bytes 1572896 | tf_op jit(solution)/shard_map/ppermute | solution.py:17
  277.9 15.0 %metric_far0.1 = (f32[4,12,128,128]{3,2,1,0:T(8,128)}, f32[4,12,128,128]{3,2,1,0:T(8,128)}) custom-call(s32[2]{0:T(128)} %pad_add_fusion.1.meta.refs_0_, s32[4,24]{1,0:T(4,128)} %refs_1_.17, s32[2,40]{1,0:T(2,128)} %copy-done.19, s32[2,40]{1,0:T(2,128)} %copy-done.20, bf16[5,2,4,128,256]{4,3,2,1,0:T(8,128)(2,1)} %factor_left.1.refs_4_.refs_3_, ...), custom_call_target="tpu_custom_call" | custom-call | tf_op jit(solution)/shard_map/metric_far0/pallas_call | solution.py:205
  293.0 2.0 collective-permute-start.28
  294.9 16.6 %collective-permute-done.21.refs_5_ = f32[24,128,128]{2,1,0:T(8,128)S(1)} collective-permute-done((f32[24,128,128]{2,1,0:T(8,128)}, f32[24,128,128]{2,1,0:T(8,128)S(1)}, u32[]{:S(2)}, u32[]{:S(2)}) %collective-permute-start.21) | collective-permute-done | bytes 1572896 | tf_op jit(solution)/shard_map/ppermute | solution.py:17
  311.5 1.1 copy-done.6
  312.7 1.1 copy-done.7
  313.8 9.9 %metric_far1.2 = (f32[2,12,128,128]{3,2,1,0:T(8,128)}, f32[2,12,128,128]{3,2,1,0:T(8,128)}) custom-call(s32[2]{0:T(128)} %pad_add_fusion.1.meta.refs_0_, s32[4,24]{1,0:T(4,128)} %refs_1_.17, s32[2,40]{1,0:T(2,128)} %copy-done.19, s32[2,40]{1,0:T(2,128)} %copy-done.20, bf16[5,2,4,128,256]{4,3,2,1,0:T(8,128)(2,1)} %factor_left.1.refs_4_.refs_3_, ...), custom_call_target="tpu_custom_call" | custom-call | tf_op jit(solution)/shard_map/metric_far1/pallas_call | solution.py:205
  323.7 1.2 collective-permute-start.24
  324.9 9.9 %metric_far1.3 = (f32[2,12,128,128]{3,2,1,0:T(8,128)}, f32[2,12,128,128]{3,2,1,0:T(8,128)}) custom-call(s32[2]{0:T(128)} %pad_add_fusion.1.meta.refs_0_, s32[4,24]{1,0:T(4,128)} %refs_1_.17, s32[2,40]{1,0:T(2,128)} %copy-done.19, s32[2,40]{1,0:T(2,128)} %copy-done.20, bf16[5,2,4,128,256]{4,3,2,1,0:T(8,128)(2,1)} %factor_left.1.refs_4_.refs_3_, ...), custom_call_target="tpu_custom_call" | custom-call | tf_op jit(solution)/shard_map/metric_far1/pallas_call | solution.py:205
  335.0 3.3 collective-permute-done.25
  338.6 1.7 copy-done.12
  340.3 4.5 %maximum_add_fusion = f32[4,12,128,128]{3,2,1,0:T(8,128)} fusion(f32[2,12,128,128]{3,2,1,0:T(8,128)S(1)} %add.67, f32[2,12,128,128]{3,2,1,0:T(8,128)S(1)} %add.66, f32[4,12,128,128]{3,2,1,0:T(8,128)S(1)} %copy-done.12, f32[4,12,128,128]{3,2,1,0:T(8,128)} %collective-permute-done.28), kind=kLoop, calls=%fused_computation.5 | loop fusion | flops 2359296 | bytes 12582912 | tf_op jit(solution)/shard_map/add | solution.py:303
  (87 shorter events, 7.1 us)
Async XLA Ops:
  0.6 37.5 %collective-permute-start.3 = (f32[4,8,128,128]{3,2,1,0:T(8,128)}, f32[4,8,128,128]{3,2,1,0:T(8,128)}, u32[]{:S(2)}, u32[]{:S(2)}) collective-permute-start(f32[4,8,128,128]{3,2,1,0:T(8,128)} %table_a.1), channel_id=1, source_target_pairs={{0,1},{1,0},{2,3},{3,2},{4,5},{5,4},{6,7},{7,6},{8,9},{9,8},{10,11... | collective-permute-start | bytes 6291464 | tf_op jit(solution)/shard_map/ppermute | solution.py:21
  2.1 10.4 %copy-start.18 = (s32[4,24]{1,0:T(4,128)S(1)}, s32[4,24]{1,0:T(4,128)}, u32[]{:S(2)}) copy-start(s32[4,24]{1,0:T(4,128)} %refs_1_.12) | copy-start | bytes 1156
  2.1 10.4 %copy-start.26 = (s32[4,16]{1,0:T(4,128)S(1)}, s32[4,16]{1,0:T(4,128)}, u32[]{:S(2)}) copy-start(s32[4,16]{1,0:T(4,128)} %param.9) | copy-start | bytes 772
  2.1 10.5 %copy-start.24 = (s32[4,8]{1,0:T(4,128)S(1)}, s32[4,8]{1,0:T(4,128)}, u32[]{:S(2)}) copy-start(s32[4,8]{1,0:T(4,128)} %cols_a.1) | copy-start | bytes 388
  3.9 40.3 %copy-start.3 = (f32[16,128,128]{2,1,0:T(8,128)}, f32[16,128,128]{2,1,0:T(8,128)S(1)}, u32[]{:S(2)}) copy-start(f32[16,128,128]{2,1,0:T(8,128)S(1)} %get-tuple-element.63.refs_6_.refs_9_) | copy-start | bytes 3145732
  3.9 41.9 %copy-start.2 = (f32[16,128,128]{2,1,0:T(8,128)}, f32[16,128,128]{2,1,0:T(8,128)S(1)}, u32[]{:S(2)}) copy-start(f32[16,128,128]{2,1,0:T(8,128)S(1)} %get-tuple-element.62.refs_7_.refs_10_) | copy-start | bytes 3145732
  3.9 42.0 %collective-permute-start = (f32[16,128,128]{2,1,0:T(8,128)S(1)}, f32[16,128,128]{2,1,0:T(8,128)S(1)}, u32[]{:S(2)}, u32[]{:S(2)}) collective-permute-start(f32[16,128,128]{2,1,0:T(8,128)S(1)} %get-tuple-element.63.refs_6_.refs_9_), channel_id=1, source_target_pairs={{0,2},{2,4},{4,6},{6,8},{8,10},{10,12},{12,14},{14,16},{16,18},{18... | collective-permute-start | bytes 3145736 | tf_op jit(solution)/shard_map/ppermute | solution.py:17
  5.2 40.7 %collective-permute-start.1 = (f32[16,128,128]{2,1,0:T(8,128)S(1)}, f32[16,128,128]{2,1,0:T(8,128)}, u32[]{:S(2)}, u32[]{:S(2)}) collective-permute-start(f32[16,128,128]{2,1,0:T(8,128)S(1)} %get-tuple-element.63.refs_6_.refs_9_), channel_id=1, source_target_pairs={{0,126},{2,0},{4,2},{6,4},{8,6},{10,8},{12,10},{14,12},{16,14},{18... | collective-permute-start | bytes 3145736 | tf_op jit(solution)/shard_map/ppermute | solution.py:17
  12.6 31.6 %copy-start.21 = (s32[2,40]{1,0:T(2,128)}, s32[2,40]{1,0:T(2,128)S(1)}, u32[]{:S(2)}) copy-start(s32[2,40]{1,0:T(2,128)S(1)} %constant_dynamic-slice_fusion.refs_2_) | copy-start | bytes 964
  12.6 24.0 %collective-permute-start.4 = (s32[2,40]{1,0:T(2,128)S(1)}, s32[2,40]{1,0:T(2,128)S(1)}, u32[]{:S(2)}, u32[]{:S(2)}) collective-permute-start(s32[2,40]{1,0:T(2,128)S(1)} %constant_dynamic-slice_fusion.refs_2_), channel_id=1, source_target_pairs={{0,4},{2,6},{4,8},{6,10},{8,12},{10,14},{12,16},{14,18},{16,20},{1... | collective-permute-start | bytes 968 | tf_op jit(solution)/shard_map/ppermute | solution.py:17
  12.7 1.2 collective-permute-start.2
  13.9 24.9 %copy-start.25 = (s32[4,8]{1,0:T(4,128)}, s32[4,8]{1,0:T(4,128)S(1)}, u32[]{:S(2)}) copy-start(s32[4,8]{1,0:T(4,128)S(1)} %collective-permute-done.2.cols_b) | copy-start | bytes 388
  13.9 30.3 %collective-permute-start.5 = (s32[2,40]{1,0:T(2,128)S(1)}, s32[2,40]{1,0:T(2,128)S(1)}, u32[]{:S(2)}, u32[]{:S(2)}) collective-permute-start(s32[2,40]{1,0:T(2,128)S(1)} %constant_dynamic-slice_fusion.refs_2_), channel_id=1, source_target_pairs={{0,2},{2,4},{4,6},{6,8},{8,10},{10,12},{12,14},{14,16},{16,18},{18... | collective-permute-start | bytes 968 | tf_op jit(solution)/shard_map/ppermute | solution.py:17
  36.6 7.5 %copy-start.19 = (s32[2,40]{1,0:T(2,128)}, s32[2,40]{1,0:T(2,128)S(1)}, u32[]{:S(2)}) copy-start(s32[2,40]{1,0:T(2,128)S(1)} %collective-permute-done.4.refs_2_.refs_0_) | copy-start | bytes 964
  36.6 9.1 %collective-permute-start.6 = (s32[2,40]{1,0:T(2,128)S(1)}, s32[2,40]{1,0:T(2,128)S(1)}, u32[]{:S(2)}, u32[]{:S(2)}) collective-permute-start(s32[2,40]{1,0:T(2,128)S(1)} %constant_dynamic-slice_fusion.refs_2_), channel_id=1, source_target_pairs={{0,126},{2,0},{4,2},{6,4},{8,6},{10,8},{12,10},{14,12},{16,14},{18... | collective-permute-start | bytes 968 | tf_op jit(solution)/shard_map/ppermute | solution.py:17
  38.1 7.7 %collective-permute-start.7 = (s32[2,40]{1,0:T(2,128)S(1)}, s32[2,40]{1,0:T(2,128)S(1)}, u32[]{:S(2)}, u32[]{:S(2)}) collective-permute-start(s32[2,40]{1,0:T(2,128)S(1)} %constant_dynamic-slice_fusion.refs_2_), channel_id=1, source_target_pairs={{0,124},{2,126},{4,0},{6,2},{8,4},{10,6},{12,8},{14,10},{16,12},{1... | collective-permute-start | bytes 968 | tf_op jit(solution)/shard_map/ppermute | solution.py:17
  44.2 29.9 %copy-start.22 = (s32[2,40]{1,0:T(2,128)}, s32[2,40]{1,0:T(2,128)S(1)}, u32[]{:S(2)}) copy-start(s32[2,40]{1,0:T(2,128)S(1)} %collective-permute-done.5.refs_3_.refs_1_.refs_2_) | copy-start | bytes 964
  44.2 22.9 %collective-permute-start.10 = (f32[16,128,128]{2,1,0:T(8,128)S(1)}, f32[16,128,128]{2,1,0:T(8,128)S(1)}, u32[]{:S(2)}, u32[]{:S(2)}) collective-permute-start(f32[16,128,128]{2,1,0:T(8,128)S(1)} %get-tuple-element.62.refs_7_.refs_10_), channel_id=1, source_target_pairs={{0,126},{2,0},{4,2},{6,4},{8,6},{10,8},{12,10},{14,12},{16,14},{18... | collective-permute-start | bytes 3145736 | tf_op jit(solution)/shard_map/ppermute | solution.py:17
  45.8 28.3 %copy-start.23 = (s32[2,40]{1,0:T(2,128)}, s32[2,40]{1,0:T(2,128)S(1)}, u32[]{:S(2)}) copy-start(s32[2,40]{1,0:T(2,128)S(1)} %collective-permute-done.6.refs_4_.refs_3_) | copy-start | bytes 964
  45.8 28.3 %collective-permute-start.8 = (f32[16,128,128]{2,1,0:T(8,128)S(1)}, f32[16,128,128]{2,1,0:T(8,128)}, u32[]{:S(2)}, u32[]{:S(2)}) collective-permute-start(f32[16,128,128]{2,1,0:T(8,128)S(1)} %get-tuple-element.62.refs_7_.refs_10_), channel_id=1, source_target_pairs={{0,2},{2,4},{4,6},{6,8},{8,10},{10,12},{12,14},{14,16},{16,18},{18... | collective-permute-start | bytes 3145736 | tf_op jit(solution)/shard_map/ppermute | solution.py:17
  45.9 51.6 %copy-start.20 = (s32[2,40]{1,0:T(2,128)}, s32[2,40]{1,0:T(2,128)S(1)}, u32[]{:S(2)}) copy-start(s32[2,40]{1,0:T(2,128)S(1)} %collective-permute-done.7.refs_3_.refs_4_) | copy-start | bytes 964
  45.9 28.2 %copy-start.8 = (f32[16,128,128]{2,1,0:T(8,128)}, f32[16,128,128]{2,1,0:T(8,128)S(1)}, u32[]{:S(2)}) copy-start(f32[16,128,128]{2,1,0:T(8,128)S(1)} %collective-permute-done.refs_8_.refs_7_) | copy-start | bytes 3145732
  45.9 50.5 %collective-permute-start.13 = (f32[16,128,128]{2,1,0:T(8,128)S(1)}, f32[16,128,128]{2,1,0:T(8,128)S(1)}, u32[]{:S(2)}, u32[]{:S(2)}) collective-permute-start(f32[16,128,128]{2,1,0:T(8,128)S(1)} %collective-permute-done.refs_8_.refs_7_), channel_id=1, source_target_pairs={{0,2},{2,4},{4,6},{6,8},{8,10},{10,12},{12,14},{14,16},{16,18},{18... | collective-permute-start | bytes 3145736 | tf_op jit(solution)/shard_map/ppermute | solution.py:17
  46.4 50.0 %collective-permute-start.14 = (f32[16,128,128]{2,1,0:T(8,128)}, f32[16,128,128]{2,1,0:T(8,128)}, u32[]{:S(2)}, u32[]{:S(2)}) collective-permute-start(f32[16,128,128]{2,1,0:T(8,128)} %collective-permute-done.1.refs_10_.refs_11_), channel_id=1, source_target_pairs={{0,126},{2,0},{4,2},{6,4},{8,6},{10,8},{12,10},{14,12},{16,14},{18... | collective-permute-start | bytes 3145736 | tf_op jit(solution)/shard_map/ppermute | solution.py:17
  97.5 15.6 %copy-start.10 = (f32[16,128,128]{2,1,0:T(8,128)S(1)}, f32[16,128,128]{2,1,0:T(8,128)}, u32[]{:S(2)}) copy-start(f32[16,128,128]{2,1,0:T(8,128)} %copy-done.9) | copy-start | bytes 3145732
  110.2 51.2 %collective-permute-start.15 = (f32[2,24,128,128]{3,2,1,0:T(8,128)}, f32[2,24,128,128]{3,2,1,0:T(8,128)}, u32[]{:S(2)}, u32[]{:S(2)}) collective-permute-start(f32[2,24,128,128]{3,2,1,0:T(8,128)} %get-tuple-element.44), channel_id=1, source_target_pairs={{0,1},{1,0},{2,3},{3,2},{4,5},{5,4},{6,7},{7,6},{8,9},{9,8},{10,11... | collective-permute-start | bytes 9437192 | tf_op jit(solution)/shard_map/ppermute | solution.py:21
  113.1 24.7 %collective-permute-start.11 = (f32[16,128,128]{2,1,0:T(8,128)S(1)}, f32[16,128,128]{2,1,0:T(8,128)S(1)}, u32[]{:S(2)}, u32[]{:S(2)}) collective-permute-start(f32[16,128,128]{2,1,0:T(8,128)S(1)} %copy-done.10), channel_id=1, source_target_pairs={{0,126},{2,0},{4,2},{6,4},{8,6},{10,8},{12,10},{14,12},{16,14},{18... | collective-permute-start | bytes 3145736 | tf_op jit(solution)/shard_map/ppermute | solution.py:17
  113.1 30.2 %collective-permute-start.9 = (f32[16,128,128]{2,1,0:T(8,128)}, f32[16,128,128]{2,1,0:T(8,128)S(1)}, u32[]{:S(2)}, u32[]{:S(2)}) collective-permute-start(f32[16,128,128]{2,1,0:T(8,128)} %collective-permute-done.8.refs_9_.refs_8_), channel_id=1, source_target_pairs={{0,2},{2,4},{4,6},{6,8},{8,10},{10,12},{12,14},{14,16},{16,18},{18... | collective-permute-start | bytes 3145736 | tf_op jit(solution)/shard_map/ppermute | solution.py:17
  137.8 5.5 %copy-start.4 = (f32[16,128,128]{2,1,0:T(8,128)}, f32[16,128,128]{2,1,0:T(8,128)S(1)}, u32[]{:S(2)}) copy-start(f32[16,128,128]{2,1,0:T(8,128)S(1)} %collective-permute-done.11.refs_6_.refs_14_) | copy-start | bytes 3145732
  152.3 9.1 %copy-start.13 = (f32[2,24,128,128]{3,2,1,0:T(8,128)S(1)}, f32[2,24,128,128]{3,2,1,0:T(8,128)}, u32[]{:S(2)}) copy-start(f32[2,24,128,128]{3,2,1,0:T(8,128)} %get-tuple-element.43) | copy-start | bytes 9437188
  152.3 11.7 %collective-permute-start.12 = (f32[1,24,128,128]{3,2,1,0:T(8,128)}, f32[1,24,128,128]{3,2,1,0:T(8,128)}, u32[]{:S(2)}, u32[]{:S(2)}) collective-permute-start(f32[1,24,128,128]{3,2,1,0:T(8,128)} %get-tuple-element.35), channel_id=1, source_target_pairs={{0,1},{1,0},{2,3},{3,2},{4,5},{5,4},{6,7},{7,6},{8,9},{9,8},{10,11... | collective-permute-start | bytes 4718600 | tf_op jit(solution)/shard_map/ppermute | solution.py:21
  161.2 3.8 %collective-permute-start.18 = (f32[1,24,128,128]{3,2,1,0:T(8,128)}, f32[1,24,128,128]{3,2,1,0:T(8,128)}, u32[]{:S(2)}, u32[]{:S(2)}) collective-permute-start(f32[1,24,128,128]{3,2,1,0:T(8,128)} %get-tuple-element.46), channel_id=1, source_target_pairs={{0,1},{1,0},{2,3},{3,2},{4,5},{5,4},{6,7},{7,6},{8,9},{9,8},{10,11... | collective-permute-start | bytes 4718600 | tf_op jit(solution)/shard_map/ppermute | solution.py:21
  161.4 3.6 %copy-start.15 = (f32[1,24,128,128]{3,2,1,0:T(8,128)S(1)}, f32[1,24,128,128]{3,2,1,0:T(8,128)}, u32[]{:S(2)}) copy-start(f32[1,24,128,128]{3,2,1,0:T(8,128)} %get-tuple-element.45) | copy-start | bytes 4718596
  167.8 15.4 %copy-start = (f32[1,24,128,128]{3,2,1,0:T(8,128)}, f32[1,24,128,128]{3,2,1,0:T(8,128)S(1)}, u32[]{:S(2)}) copy-start(f32[1,24,128,128]{3,2,1,0:T(8,128)S(1)} %get-tuple-element.64) | copy-start | bytes 4718596
  167.8 15.4 %copy-start.1 = (f32[1,24,128,128]{3,2,1,0:T(8,128)}, f32[1,24,128,128]{3,2,1,0:T(8,128)S(1)}, u32[]{:S(2)}) copy-start(f32[1,24,128,128]{3,2,1,0:T(8,128)S(1)} %get-tuple-element.65) | copy-start | bytes 4718596
  169.2 14.0 %collective-permute-start.19 = (f32[2,12,128,128]{3,2,1,0:T(8,128)}, f32[2,12,128,128]{3,2,1,0:T(8,128)}, u32[]{:S(2)}, u32[]{:S(2)}) collective-permute-start(f32[2,12,128,128]{3,2,1,0:T(8,128)} %fusion), channel_id=1, source_target_pairs={{0,1},{1,0},{2,3},{3,2},{4,5},{5,4},{6,7},{7,6},{8,9},{9,8},{10,11... | collective-permute-start | bytes 4718600 | tf_op jit(solution)/shard_map/ppermute | solution.py:21
  169.4 41.2 %collective-permute-start.16 = (f32[24,128,128]{2,1,0:T(8,128)S(1)}, f32[24,128,128]{2,1,0:T(8,128)}, u32[]{:S(2)}, u32[]{:S(2)}) collective-permute-start(f32[24,128,128]{2,1,0:T(8,128)S(1)} %bitcast.11), channel_id=1, source_target_pairs={{0,2},{2,4},{4,6},{6,8},{8,10},{10,12},{12,14},{14,16},{16,18},{18... | collective-permute-start | bytes 4718600 | tf_op jit(solution)/shard_map/ppermute | solution.py:17
  169.4 41.2 %collective-permute-start.17 = (f32[24,128,128]{2,1,0:T(8,128)S(1)}, f32[24,128,128]{2,1,0:T(8,128)}, u32[]{:S(2)}, u32[]{:S(2)}) collective-permute-start(f32[24,128,128]{2,1,0:T(8,128)S(1)} %bitcast.12), channel_id=1, source_target_pairs={{0,126},{2,0},{4,2},{6,4},{8,6},{10,8},{12,10},{14,12},{16,14},{18... | collective-permute-start | bytes 4718600 | tf_op jit(solution)/shard_map/ppermute | solution.py:17
  176.2 68.0 %collective-permute-start.20 = (f32[24,128,128]{2,1,0:T(8,128)S(1)}, f32[24,128,128]{2,1,0:T(8,128)}, u32[]{:S(2)}, u32[]{:S(2)}) collective-permute-start(f32[24,128,128]{2,1,0:T(8,128)S(1)} %bitcast.8), channel_id=1, source_target_pairs={{0,2},{2,4},{4,6},{6,8},{8,10},{10,12},{12,14},{14,16},{16,18},{18... | collective-permute-start | bytes 4718600 | tf_op jit(solution)/shard_map/ppermute | solution.py:17
  176.3 68.0 %collective-permute-start.22 = (f32[24,128,128]{2,1,0:T(8,128)S(1)}, f32[24,128,128]{2,1,0:T(8,128)}, u32[]{:S(2)}, u32[]{:S(2)}) collective-permute-start(f32[24,128,128]{2,1,0:T(8,128)S(1)} %bitcast.9), channel_id=1, source_target_pairs={{0,126},{2,0},{4,2},{6,4},{8,6},{10,8},{12,10},{14,12},{16,14},{18... | collective-permute-start | bytes 4718600 | tf_op jit(solution)/shard_map/ppermute | solution.py:17
  210.5 67.4 %collective-permute-start.26 = (f32[24,128,128]{2,1,0:T(8,128)}, f32[24,128,128]{2,1,0:T(8,128)}, u32[]{:S(2)}, u32[]{:S(2)}) collective-permute-start(f32[24,128,128]{2,1,0:T(8,128)} %collective-permute-done.16.refs_5_), channel_id=1, source_target_pairs={{0,2},{2,4},{4,6},{6,8},{8,10},{10,12},{12,14},{14,16},{16,18},{18... | collective-permute-start | bytes 4718600 | tf_op jit(solution)/shard_map/ppermute | solution.py:17
  210.5 67.4 %collective-permute-start.27 = (f32[24,128,128]{2,1,0:T(8,128)}, f32[24,128,128]{2,1,0:T(8,128)}, u32[]{:S(2)}, u32[]{:S(2)}) collective-permute-start(f32[24,128,128]{2,1,0:T(8,128)} %collective-permute-done.17.refs_7_), channel_id=1, source_target_pairs={{0,126},{2,0},{4,2},{6,4},{8,6},{10,8},{12,10},{14,12},{16,14},{18... | collective-permute-start | bytes 4718600 | tf_op jit(solution)/shard_map/ppermute | solution.py:17
  244.2 67.3 %collective-permute-start.21 = (f32[24,128,128]{2,1,0:T(8,128)}, f32[24,128,128]{2,1,0:T(8,128)S(1)}, u32[]{:S(2)}, u32[]{:S(2)}) collective-permute-start(f32[24,128,128]{2,1,0:T(8,128)} %collective-permute-done.20.refs_6_), channel_id=1, source_target_pairs={{0,2},{2,4},{4,6},{6,8},{8,10},{10,12},{12,14},{14,16},{16,18},{18... | collective-permute-start | bytes 4718600 | tf_op jit(solution)/shard_map/ppermute | solution.py:17
  244.2 67.3 %collective-permute-start.23 = (f32[24,128,128]{2,1,0:T(8,128)}, f32[24,128,128]{2,1,0:T(8,128)S(1)}, u32[]{:S(2)}, u32[]{:S(2)}) collective-permute-start(f32[24,128,128]{2,1,0:T(8,128)} %collective-permute-done.22.refs_8_), channel_id=1, source_target_pairs={{0,126},{2,0},{4,2},{6,4},{8,6},{10,8},{12,10},{14,12},{16,14},{18... | collective-permute-start | bytes 4718600 | tf_op jit(solution)/shard_map/ppermute | solution.py:17
  293.0 45.6 %collective-permute-start.28 = (f32[4,12,128,128]{3,2,1,0:T(8,128)}, f32[4,12,128,128]{3,2,1,0:T(8,128)}, u32[]{:S(2)}, u32[]{:S(2)}) collective-permute-start(f32[4,12,128,128]{3,2,1,0:T(8,128)} %get-tuple-element.59), channel_id=1, source_target_pairs={{0,1},{1,0},{2,3},{3,2},{4,5},{5,4},{6,7},{7,6},{8,9},{9,8},{10,11... | collective-permute-start | bytes 9437192 | tf_op jit(solution)/shard_map/ppermute | solution.py:21
  323.7 11.2 %copy-start.17 = (f32[2,12,128,128]{3,2,1,0:T(8,128)S(1)}, f32[2,12,128,128]{3,2,1,0:T(8,128)}, u32[]{:S(2)}) copy-start(f32[2,12,128,128]{3,2,1,0:T(8,128)} %get-tuple-element.48) | copy-start | bytes 4718596
  323.7 11.2 %collective-permute-start.24 = (f32[2,12,128,128]{3,2,1,0:T(8,128)}, f32[2,12,128,128]{3,2,1,0:T(8,128)S(1)}, u32[]{:S(2)}, u32[]{:S(2)}) collective-permute-start(f32[2,12,128,128]{3,2,1,0:T(8,128)} %get-tuple-element.49), channel_id=1, source_target_pairs={{0,1},{1,0},{2,3},{3,2},{4,5},{5,4},{6,7},{7,6},{8,9},{9,8},{10,11... | collective-permute-start | bytes 4718600 | tf_op jit(solution)/shard_map/ppermute | solution.py:21
  334.7 3.6 %collective-permute-start.25 = (f32[2,12,128,128]{3,2,1,0:T(8,128)}, f32[2,12,128,128]{3,2,1,0:T(8,128)S(1)}, u32[]{:S(2)}, u32[]{:S(2)}) collective-permute-start(f32[2,12,128,128]{3,2,1,0:T(8,128)} %get-tuple-element.51), channel_id=1, source_target_pairs={{0,1},{1,0},{2,3},{3,2},{4,5},{5,4},{6,7},{7,6},{8,9},{9,8},{10,11... | collective-permute-start | bytes 4718600 | tf_op jit(solution)/shard_map/ppermute | solution.py:21
  (8 other events, 14.3 us)

commit v2 on v1

v2 whole, which is shorter than its diff:
```python
import functools

import jax
import jax.numpy as jnp
from jax import lax
from jax.experimental import pallas as pl
from jax.experimental.pallas import tpu as pltpu
from jax.sharding import PartitionSpec as P

F32 = jnp.float32
BF16 = jnp.bfloat16
WINDOW = 36


def ring(array, by):
    devices = lax.axis_size("rows")
    return lax.ppermute(array, "rows", [(i, (i + by) % devices) for i in range(devices)])


def swap(array):
    return lax.ppermute(array, "rep", [(0, 1), (1, 0)])


def split(block):
    high = block.astype(BF16)
    return high, (block - high.astype(F32)).astype(BF16)


def block_of(table, index):
    return table[pl.ds(pl.multiple_of(index * 128, 128), 128), :]


def wrap(index, total):
    if total & (total - 1) == 0:
        return jnp.bitwise_and(index, total - 1)
    return lax.rem(index + total, total)


def clear(ref, first=0, last=None):
    zero = jnp.zeros(ref.shape[1:], ref.dtype)

    def body(i, carry):
        ref[i] = zero
        return carry

    lax.fori_loop(first, ref.shape[0] if last is None else last, body, 0, unroll=4)


def copy_last(out, parts, row_of):
    for part, ref in enumerate(parts):
        for gi, group in enumerate((0, 4)):
            for row in range(2):
                ref[gi, 0, row] = out[group, 1, row_of(part, row)]


def margin_left_kernel(total, meta, cols_a, cols_b, table_a, table_b, out, part_a, part_b):
    position, core = meta[0], meta[1]
    for group in range(5):
        for c in range(2):
            clear(out.at[group, c])
    first = 4 * position - 8
    for cols, table in ((cols_a, table_a), (cols_b, table_b)):
        for row in range(4):

            def body(k, carry, cols=cols, table=table, row=row):
                rel = wrap(cols[row, k] - first, total)
                within = jnp.bitwise_and(rel, 3) - 2 * core

                @pl.when((within >= 0) & (within < 2))
                def _():
                    group = lax.shift_right_logical(rel, 2)
                    high, low = split(table[row, k])
                    out[group, within, row, :, :128] = high
                    out[group, within, row, :, 128:] = low

                return carry

            lax.fori_loop(0, table.shape[1], body, 0)
    copy_last(out, (part_a, part_b), lambda part, row: 2 * row + part)


def factor_left_kernel(pieces, total, meta, *refs):
    patterns, refs = refs[:5], refs[5:]
    out, part_a, part_b = refs[-3:]
    tables, refs = [], list(refs[:-3])
    for number in pieces:
        tables.append([refs.pop(0) for _ in range(number)])
    position = meta[0]
    for group in range(5):
        for c in range(2):
            clear(out.at[group, c])
            cols, first = patterns[group], 0
            for table in tables[2 * group + c]:

                def body(m, carry, cols=cols, table=table, group=group, c=c, first=first):
                    rel = wrap(cols[c, first + m] - 4 * position, total)

                    @pl.when(rel < 4)
                    def _():
                        high, low = split(block_of(table, m).T)
                        out[group, c, rel, :, :128] = high
                        out[group, c, rel, :, 128:] = low

                    return carry

                lax.fori_loop(0, table.shape[0] // 128, body, 0)
                first += table.shape[0] // 128
    copy_last(out, (part_a, part_b), lambda part, row: 2 * part + row)


def stage_kernel(gs, crs, pieces, starts, counts, total, by_rows, row0, col0, has_acc, *refs):
    count, depth = len(gs), len(crs)
    meta, outcols = refs[:2]
    patterns = refs[2 : 2 + count]
    refs = refs[2 + count :]
    lefts, refs = refs[0], list(refs[1:])
    tables = []
    for number in pieces:
        tables.append([refs.pop(0) for _ in range(number)])
    acc = None
    if has_acc:
        acc, refs = refs[:2], refs[2:]
    right_high, right_low, dense = refs[-3:]
    outs = refs[:-3]
    portions = len(outs) // 2
    core = meta[1]
    base = 4 * meta[0] - 16
    rows = dense.shape[1]
    spare = right_high.shape[1] - 1
    for gi in range(count):
        clear(right_high.at[gi], 0, counts[gi])
        clear(right_low.at[gi], 0, counts[gi])
        for ci, c in enumerate(crs):
            cols, first = patterns[gi], col0
            for table in tables[gi * depth + ci]:

                def right_body(m, carry, gi=gi, ci=ci, c=c, cols=cols, table=table, first=first):
                    rel = wrap(cols[c, first + m] - base, total) - starts[gi]
                    rel = jnp.where((rel >= 0) & (rel < counts[gi]), rel, spare)
                    high, low = split(block_of(table, m))
                    right_high[gi, rel, ci] = high
                    right_low[gi, rel, ci] = low
                    return carry

                lax.fori_loop(0, table.shape[0] // 128, right_body, 0, unroll=4)
                first += table.shape[0] // 128

    def rights(ref, gi, at):
        return jnp.concatenate(
            [ref[gi, at + j].reshape(128 * depth, 128) for j in range(4)], axis=1
        )

    done = (0, 0)
    for gi, g in enumerate(gs):
        if lefts.shape[0] == 5:
            left = [lefts[g + 2, c].reshape(rows * 128, 256) for c in crs]
        else:
            left = [lefts[gi, 0].reshape(rows * 128, 256)]
        highs = [part[:, :128] for part in left]
        lows = [part[:, 128:] for part in left]
        left = jnp.concatenate(highs + lows + highs, axis=1)

        def body(q, carry, gi=gi, left=left, add=False):
            rh, rl = rights(right_high, gi, 4 * q), rights(right_low, gi, 4 * q)
            out = jnp.dot(left, jnp.concatenate([rh, rh, rl], axis=0), preferred_element_type=F32)
            to = starts[gi] + 4 * q
            for j in range(4):
                value = out[:, 128 * j : 128 * j + 128].reshape(rows, 128, 128)
                dense[to + j] = dense[to + j] + value if add else value
            return carry

        start, stop = starts[gi], starts[gi] + counts[gi]
        low, high = max(start, done[0]), min(stop, done[1])
        if low >= high:
            spans = [(start, stop, False)]
        else:
            spans = [(start, low, False), (low, high, True), (high, stop, False)]
        for first, last, add in spans:
            if last > first:
                lax.fori_loop(
                    (first - start) // 4, (last - start) // 4, functools.partial(body, add=add), 0, unroll=2
                )
        done = (start, stop) if gi == 0 else (min(start, done[0]), max(stop, done[1]))
    clear(dense, 0, done[0])
    clear(dense, done[1], WINDOW)
    kept_rows, kept_cols = outs[0].shape[0] * portions, outs[0].shape[1]
    each = outs[0].shape[0]
    for which in range(2):
        side = core if which == 0 else 1 - core
        for row in range(kept_rows):
            source = side * kept_rows + row if by_rows else row
            at_row = 2 * side + row0 + row if by_rows else row0 + row
            at_col = 0 if by_rows else kept_cols * side

            def out_body(y, carry, which=which, row=row, source=source, at_row=at_row, at_col=at_col):
                rel = wrap(outcols[at_row, at_col + y] - base, total)
                value = dense[rel, source]
                if acc is not None:
                    value = value + acc[which][row, y]
                outs[which * portions + row // each][row % each, y] = value
                return carry

            lax.fori_loop(0, kept_cols, out_body, 0, unroll=4)


SMEM = pl.BlockSpec(memory_space=pltpu.SMEM)
VMEM = pl.BlockSpec(memory_space=pltpu.VMEM)
PARAMS = pltpu.CompilerParams(vmem_limit_bytes=60 << 20)


def stage(name, gs, crs, by_rows, part, total, meta, outcols, patterns, left, tables, acc, col0, portions=1):
    if by_rows:
        starts, counts = [4 * (g + 2) for g in gs], [20] * len(gs)
        out = (2 if part is None else 1, outcols.shape[1], 128, 128)
        row0, rows = part or 0, 2 * out[0]
    else:
        starts, counts = [max(0, 4 * g) for g in gs], [WINDOW - 4 * abs(g) for g in gs]
        out = (4 if part is None else 2, outcols.shape[1] // 2, 128, 128)
        row0, rows = 2 * (part or 0), out[0]
    tables = [tables[g][c] for g in gs for c in crs]
    kernel = functools.partial(
        stage_kernel, gs, crs, [len(t) for t in tables], starts, counts, total, by_rows, row0, col0, bool(acc)
    )
    shape = jax.ShapeDtypeStruct((out[0] // portions,) + out[1:], F32)
    blocks = [piece for table in tables for piece in table]
    window = max(counts)
    return pl.pallas_call(
        kernel,
        name=name,
        out_shape=[shape] * (2 * portions),
        in_specs=[SMEM] * (2 + len(gs)) + [VMEM] * (1 + len(blocks) + len(acc)),
        out_specs=[VMEM] * (2 * portions),
        scratch_shapes=[
            pltpu.VMEM((len(gs), window + 1, len(crs), 128, 128), BF16),
            pltpu.VMEM((len(gs), window + 1, len(crs), 128, 128), BF16),
            pltpu.VMEM((WINDOW, rows, 128, 128), F32),
        ],
        compiler_params=PARAMS,
        cost_estimate=pl.CostEstimate(
            flops=0,
            transcendentals=0,
            bytes_accessed=0,
        ),
    )(
        meta, outcols, *[patterns[g] for g in gs], left[0 if part is None else 1 + part], *blocks, *acc
    )


def left_call(kernel, name, scalars, arrays):
    out = jax.ShapeDtypeStruct((5, 2, 4, 128, 256), BF16)
    last = jax.ShapeDtypeStruct((2, 1, 2, 128, 256), BF16)
    return pl.pallas_call(
        kernel,
        name=name,
        out_shape=[out, last, last],
        in_specs=[SMEM] * len(scalars) + [VMEM] * len(arrays),
        out_specs=[VMEM] * 3,
        compiler_params=PARAMS,
        cost_estimate=pl.CostEstimate(
            flops=0, transcendentals=0, bytes_accessed=0
        ),
    )(*scalars, *arrays)


def halo(own, after_first, before_last):
    first, last = ({g: ring(row, -g) for g in (-1, 1)} for row in own)
    near = after_first(first[-1], first[1])
    first[-2], first[2] = ring(near[0], 1), ring(near[1], -1)
    near = before_last(last[-1], last[1])
    last[-2], last[2] = ring(near[0], 1), ring(near[1], -1)
    tables = {g: [(first[g],), (last[g],)] for g in (-2, -1, 1, 2)}
    tables[0] = [(row,) for row in own]
    return tables


def shards(margin_blocks, margin_cols, factor_blocks, factor_cols, product_cols, metric_cols):
    total = factor_blocks.shape[0] * lax.axis_size("rows")
    position = lax.axis_index("rows")
    core = lax.axis_index("rep")
    meta = jnp.stack([position, core]).astype(jnp.int32)
    slots = factor_cols.shape[1]
    pattern = lax.dynamic_slice_in_dim(jnp.concatenate([factor_cols, product_cols], axis=1), 2 * core, 2, 0)
    own = [
        lax.dynamic_index_in_dim(factor_blocks, 2 * core + c, 0, keepdims=False).reshape(slots * 128, 128)
        for c in range(2)
    ]
    columns = jnp.pad(pattern.astype(F32), ((0, 6), (0, 128 - pattern.shape[1])))
    own[0] = jnp.concatenate([own[0], columns], axis=0)
    margin_left = left_call(
        functools.partial(margin_left_kernel, total), "margin_left",
        [meta, margin_cols, swap(margin_cols)], [margin_blocks, swap(margin_blocks)],
    )

    def after_margin(below, above):
        return lax.optimization_barrier((below, above, margin_left))[:2]

    factors = halo(own, after_margin, lambda below, above: (below, above))
    patterns = {0: pattern}
    for g in (-2, -1, 1, 2):
        patterns[g] = factors[g][0][0][slots * 128 : slots * 128 + 2, : pattern.shape[1]].astype(jnp.int32)
    part = lambda name, gs, crs, which, acc: stage(
        name, gs, crs, True, which, total, meta, product_cols, patterns, margin_left, factors, acc, 0,
        2 if gs == (-2, 2) and which is None else 1,
    )
    acc = part("product_near", (0, -1, 1), (0, 1), None, ())
    acc = part("product_far0", (-2, 2), (0,), None, acc)
    finals = [part("product_far1", (-2, 2), (1,), which, acc[which::2]) for which in range(2)]
    rows = [(kept + swap(sent))[0] for kept, sent in finals]
    both = jnp.stack(rows)
    rows = [row.reshape(-1, 128) for row in rows]
    half = both.shape[1] // 2
    mine = lax.dynamic_slice_in_dim(both, core * half, half, 1)
    theirs = swap(lax.dynamic_slice_in_dim(both, (1 - core) * half, half, 1))
    low, high = jnp.where(core == 0, mine, theirs), jnp.where(core == 0, theirs, mine)
    made = [jnp.concatenate([low, high], axis=0)]
    blocks = [factors[g][c] for g in range(-2, 3) for c in range(2)]
    factor_left = left_call(
        functools.partial(factor_left_kernel, [len(b) for b in blocks], total), "factor_left",
        [meta] + [patterns[g] for g in range(-2, 3)], [piece for b in blocks for piece in b],
    )
    products = {0: [(row,) for row in rows]}
    part = lambda name, gs, crs, which, acc: stage(
        name, gs, crs, False, which, total, meta, metric_cols, patterns, factor_left, products, acc, slots,
        2 if gs == (-2, 2) and which is None else 1,
    )
    own_acc = part("metric_own", (0,), (0, 1), None, ())

    def after_own(below, above):
        return lax.optimization_barrier((below, above, tuple(own_acc)))[:2]

    def finish_product(below, above):
        below, above, made[0] = lax.optimization_barrier((below, above, made[0]))
        return below, above

    products = halo(rows, after_own, finish_product)
    acc = part("metric_near", (-1, 1), (0, 1), None, own_acc)
    acc = part("metric_far0", (-2, 2), (0,), None, acc)
    finals = [part("metric_far1", (-2, 2), (1,), which, acc[which::2]) for which in range(2)]
    metric = jnp.concatenate([kept + swap(sent) for kept, sent in finals], axis=0)
    return (made[0], metric)


def solution(mesh):
    return jax.shard_map(
        shards,
        mesh=mesh,
        in_specs=(
            P("rows", "rep", None, None),
            P("rows", "rep"),
            P("rows", None, None, None),
            P("rows", None),
            P("rows", None),
            P("rows", None),
        ),
        out_specs=(P("rows", "rep", None, None), P("rows", "rep", None, None)),
        check_vma=False,
    )
```

time: 345 us -> 294 us (0.85)
  waiting for transfers between devices: 131 us -> 86.2 us
  Pallas kernels: 130 us -> 122 us
  local copies, waits for them, and re-layouts: 8.83 us -> 4.7 us
    ppermute x20 -> x16, waiting for transfers between devices: 126 us -> 82 us  [ring(): lax.ppermute(array, 'rows', [(i, (i + by) % devices) for i in range(devic...]
    ppermute x20 -> x16, starting transfers between devices: 48.6 us -> 56.1 us  [ring(): lax.ppermute(array, 'rows', [(i, (i + by) % devices) for i in range(devic...]
    pallas_call x11, Pallas kernels: 130 us -> 122 us  [the longest x9 106 us: stage(): pl.pallas_call(kernel, name=name, out_shape=[shape] * (2 * portions), in_...]
    add x3 -> x2, other arithmetic: 9.83 us -> 4.26 us  [shards(): rows = [(kept + swap(sent))[0] for kept, sent in finals]]
    convert_element_type x0 -> x5, other arithmetic: none -> 4.9 us  [the longest x4 4.32 us: shards(): factors[g][0][0][slots * 128:slots * 128 + 2, :pattern.shape[1]]]
    ppermute x9 -> x7, starting transfers between devices: 9.33 us -> 4.89 us  [swap(): return lax.ppermute(array, 'rep', [(0, 1), (1, 0)])]
    unnamed x54 -> x26, local copies, waits for them, and re-layouts: 7.1 us -> 3.02 us
  transfers between devices with their start and end apart: 29 -> 23, of which waited for: 13 -> 9; matrix products, arithmetic and copies ran while one was open for 3% -> 6% of each run, Pallas kernels for 34% -> 36%
where the time goes in v2:
time: 294 us
  Pallas kernels  122 us (41%)
  waiting for transfers between devices  86.2 us (29%)
  starting transfers between devices  60.9 us (21%)
  other arithmetic  18.9 us (6%)
  local copies, waits for them, and re-layouts  4.7 us (2%)
    pallas_call x9, Pallas kernels, stage(): pl.pallas_call(kernel, name=name, out_shape=[shape] * (2 * portions), in_...  106 us
    ppermute x16, waiting for transfers between devices, ring(): lax.ppermute(array, 'rows', [(i, (i + by) % devices) for i in range(devic...  82 us
    ppermute x16, starting transfers between devices, ring(): lax.ppermute(array, 'rows', [(i, (i + by) % devices) for i in range(devic...  56.1 us
    pallas_call x2, Pallas kernels, left_call(): pl.pallas_call(kernel, name=name, out_shape=[out, last, last], in_specs=[...  16.9 us
  transfers between devices with their start and end apart: 23, of which 9 were waited for; matrix products, arithmetic and copies ran while one was open for 6% of the time, Pallas kernels for 36%

profile of v2, /device:TPU:1, one launch (start us, length us, event | category | flops | bytes accessed | tf_op | source)
XLA Modules:
  0.0 294.0 jit_solution(9363275814491670193)
XLA Ops:
  0.6 1.5 collective-permute-start.3
  2.1 0.8 pad_add_fusion
  2.9 0.6 fusion.2
  3.5 1.7 constant_dynamic-slice_fusion
  5.3 1.4 collective-permute-start
  6.6 7.3 %collective-permute-start.1 = (f32[2056,128]{1,0:T(8,128)S(1)}, f32[2056,128]{1,0:T(8,128)}, u32[]{:S(2)}, u32[]{:S(2)}) collective-permute-start(f32[2056,128]{1,0:T(8,128)S(1)} %select_maximum_fusion.refs_6_.refs_9_), channel_id=1, source_target_pairs={{0,126},{2,0},{4,2},{6,4},{8,6},{10,8},{12,10},{14,12},{16,14},{18... | collective-permute-start | bytes 3158024 | tf_op jit(solution)/shard_map/ppermute | solution.py:17
  14.2 0.8 collective-permute-done.2.cols_b
  15.1 6.0 %collective-permute-start.8 = (f32[2048,128]{1,0:T(8,128)S(1)}, f32[2048,128]{1,0:T(8,128)}, u32[]{:S(2)}, u32[]{:S(2)}) collective-permute-start(f32[2048,128]{1,0:T(8,128)S(1)} %bitcast.7), channel_id=1, source_target_pairs={{0,126},{2,0},{4,2},{6,4},{8,6},{10,8},{12,10},{14,12},{16,14},{18... | collective-permute-start | bytes 3145736 | tf_op jit(solution)/shard_map/ppermute | solution.py:17
  21.1 0.6 pad_add_fusion.1.meta.refs_0_
  21.7 5.5 %margin_left.1 = (bf16[5,2,4,128,256]{4,3,2,1,0:T(8,128)(2,1)}, bf16[2,1,2,128,256]{4,3,2,1,0:T(8,128)(2,1)}, bf16[2,1,2,128,256]{4,3,2,1,0:T(8,128)(2,1)}) custom-call(s32[2]{0:T(128)} %pad_add_fusion.1.meta.refs_0_, s32[4,8]{1,0:T(4,128)} %cols_a.1, s32[4,8]{1,0:T(4,128)} %copy-done.12, f32[4,8,128,128]{3,2,1,0:T(8,128)} %table_a.1, ...), custom_call_target="tpu_custom_call" | custom-call | tf_op jit(solution)/shard_map/margin_left/pallas_call | solution.py:252
  27.2 10.2 %collective-permute-done.refs_8_.refs_7_ = f32[2056,128]{1,0:T(8,128)S(1)} collective-permute-done((f32[2056,128]{1,0:T(8,128)S(1)}, f32[2056,128]{1,0:T(8,128)S(1)}, u32[]{:S(2)}, u32[]{:S(2)}) %collective-permute-start) | collective-permute-done | bytes 1052704 | tf_op jit(solution)/shard_map/ppermute | solution.py:17
  37.4 6.9 %collective-permute-start.5 = (f32[2056,128]{1,0:T(8,128)}, f32[2056,128]{1,0:T(8,128)}, u32[]{:S(2)}, u32[]{:S(2)}) collective-permute-start(f32[2056,128]{1,0:T(8,128)} %collective-permute-done.1.refs_10_.refs_11_), channel_id=1, source_target_pairs={{0,126},{2,0},{4,2},{6,4},{8,6},{10,8},{12,10},{14,12},{16,14},{18... | collective-permute-start | bytes 3158024 | tf_op jit(solution)/shard_map/ppermute | solution.py:17
  44.3 15.7 %collective-permute-done.6.refs_9_.refs_8_ = f32[2048,128]{1,0:T(8,128)} collective-permute-done((f32[2048,128]{1,0:T(8,128)S(1)}, f32[2048,128]{1,0:T(8,128)}, u32[]{:S(2)}, u32[]{:S(2)}) %collective-permute-start.6) | collective-permute-done | bytes 1048608 | tf_op jit(solution)/shard_map/ppermute | solution.py:17
  60.0 6.9 %collective-permute-start.9 = (f32[2048,128]{1,0:T(8,128)}, f32[2048,128]{1,0:T(8,128)S(1)}, u32[]{:S(2)}, u32[]{:S(2)}) collective-permute-start(f32[2048,128]{1,0:T(8,128)} %collective-permute-done.8.refs_11_.refs_12_), channel_id=1, source_target_pairs={{0,126},{2,0},{4,2},{6,4},{8,6},{10,8},{12,10},{14,12},{16,14},{18... | collective-permute-start | bytes 3145736 | tf_op jit(solution)/shard_map/ppermute | solution.py:17
  66.9 1.3 slice_convert_fusion.refs_4_.refs_3_
  68.1 0.6 slice_convert_fusion.1.refs_3_.refs_1_.refs_2_
  68.7 16.3 %product_near.1 = (f32[2,24,128,128]{3,2,1,0:T(8,128)}, f32[2,24,128,128]{3,2,1,0:T(8,128)}) custom-call(s32[2]{0:T(128)} %pad_add_fusion.1.meta.refs_0_, s32[4,24]{1,0:T(4,128)} %refs_1_.12, s32[2,40]{1,0:T(2,128)} %get-tuple-element.73.refs_2_, s32[2,40]{1,0:T(2,128)} %slice_convert_fusion.1.refs_3_.refs_1_.refs_2_, ...), custom_call_target="tpu_custom_call" | custom-call | tf_op jit(solution)/shard_map/product_near/pallas_call | solution.py:227
  85.0 1.2 slice_convert_fusion.2.refs_3_.refs_4_
  86.3 1.3 slice_convert_fusion.3.refs_2_.refs_0_
  87.5 11.8 %product_far0.1 = (f32[1,24,128,128]{3,2,1,0:T(8,128)}, f32[1,24,128,128]{3,2,1,0:T(8,128)}, f32[1,24,128,128]{3,2,1,0:T(8,128)}, f32[1,24,128,128]{3,2,1,0:T(8,128)}) custom-call(s32[2]{0:T(128)} %pad_add_fusion.1.meta.refs_0_, s32[4,24]{1,0:T(4,128)} %refs_1_.12, s32[2,40]{1,0:T(2,128)} %slice_convert_fusion.3.refs_2_.refs_0_, ...), custom_call_target="tpu_custom_call" | custom-call | tf_op jit(solution)/shard_map/product_far0/pallas_call | solution.py:227
  99.3 5.6 %collective-permute-done.7.refs_5_.refs_6_ = f32[2048,128]{1,0:T(8,128)S(1)} collective-permute-done((f32[2048,128]{1,0:T(8,128)}, f32[2048,128]{1,0:T(8,128)S(1)}, u32[]{:S(2)}, u32[]{:S(2)}) %collective-permute-start.7) | collective-permute-done | bytes 1048608 | tf_op jit(solution)/shard_map/ppermute | solution.py:17
  104.9 1.0 copy-done.2
  106.2 7.5 %product_far1.3 = (f32[1,24,128,128]{3,2,1,0:T(8,128)}, f32[1,24,128,128]{3,2,1,0:T(8,128)}) custom-call(s32[2]{0:T(128)} %pad_add_fusion.1.meta.refs_0_, s32[4,24]{1,0:T(4,128)} %refs_1_.12, s32[2,40]{1,0:T(2,128)} %slice_convert_fusion.3.refs_2_.refs_0_, s32[2,40]{1,0:T(2,128)} %slice_convert_fusion.2.refs_3_.refs_4_, ...), custom_call_target="tpu_custom_call" | custom-call | tf_op jit(solution)/shard_map/product_far1/pallas_call | solution.py:227
  113.7 0.6 collective-permute-start.13
  114.3 7.5 %product_far1.2 = (f32[1,24,128,128]{3,2,1,0:T(8,128)}, f32[1,24,128,128]{3,2,1,0:T(8,128)}) custom-call(s32[2]{0:T(128)} %pad_add_fusion.1.meta.refs_0_, s32[4,24]{1,0:T(4,128)} %refs_1_.12, s32[2,40]{1,0:T(2,128)} %slice_convert_fusion.3.refs_2_.refs_0_, s32[2,40]{1,0:T(2,128)} %slice_convert_fusion.2.refs_3_.refs_4_, ...), custom_call_target="tpu_custom_call" | custom-call | tf_op jit(solution)/shard_map/product_far1/pallas_call | solution.py:227
  121.9 2.8 add.37
  124.8 6.9 %collective-permute-start.18 = (f32[3072,128]{1,0:T(8,128)}, f32[3072,128]{1,0:T(8,128)}, u32[]{:S(2)}, u32[]{:S(2)}) collective-permute-start(f32[3072,128]{1,0:T(8,128)} %bitcast.5.refs_4_), channel_id=1, source_target_pairs={{0,126},{2,0},{4,2},{6,4},{8,6},{10,8},{12,10},{14,12},{16,14},{18... | collective-permute-start | bytes 4718600 | tf_op jit(solution)/shard_map/ppermute | solution.py:17
  131.7 1.4 add.36
  133.1 1.5 fusion
  134.6 1.1 collective-permute-start.14
  135.7 6.9 %collective-permute-start.12 = (f32[3072,128]{1,0:T(8,128)}, f32[3072,128]{1,0:T(8,128)}, u32[]{:S(2)}, u32[]{:S(2)}) collective-permute-start(f32[3072,128]{1,0:T(8,128)} %bitcast.4.refs_5_), channel_id=1, source_target_pairs={{0,126},{2,0},{4,2},{6,4},{8,6},{10,8},{12,10},{14,12},{16,14},{18... | collective-permute-start | bytes 4718600 | tf_op jit(solution)/shard_map/ppermute | solution.py:17
  142.6 11.4 %factor_left.1 = (bf16[5,2,4,128,256]{4,3,2,1,0:T(8,128)(2,1)}, bf16[2,1,2,128,256]{4,3,2,1,0:T(8,128)(2,1)}, bf16[2,1,2,128,256]{4,3,2,1,0:T(8,128)(2,1)}) custom-call(s32[2]{0:T(128)} %pad_add_fusion.1.meta.refs_0_, s32[2,40]{1,0:T(2,128)} %slice_convert_fusion.3.refs_2_.refs_0_, s32[2,40]{1,0:T(2,128)} %slice_convert_fusion.1.refs_3_.refs_1_.refs_2_, ...), custom_call_target="tpu_custom_call" | custom-call | tf_op jit(solution)/shard_map/factor_left/pallas_call | solution.py:252
  154.0 11.6 %metric_own.1 = (f32[4,12,128,128]{3,2,1,0:T(8,128)}, f32[4,12,128,128]{3,2,1,0:T(8,128)}) custom-call(s32[2]{0:T(128)} %pad_add_fusion.1.meta.refs_0_, s32[4,24]{1,0:T(4,128)} %refs_1_.17, s32[2,40]{1,0:T(2,128)} %get-tuple-element.73.refs_2_, bf16[5,2,4,128,256]{4,3,2,1,0:T(8,128)(2,1)} %get-tuple-element.56.refs_3_.refs_4_, f32[3072,128]{1,0:T(8,128)} %bitcast.5.refs_4_, ...), custom_call_target="tpu_custom_call" | custom-call | tf_op jit(solution)/shard_map/metric_own/pallas_call | solution.py:227
  166.0 6.9 %collective-permute-start.20 = (f32[3072,128]{1,0:T(8,128)}, f32[3072,128]{1,0:T(8,128)}, u32[]{:S(2)}, u32[]{:S(2)}) collective-permute-start(f32[3072,128]{1,0:T(8,128)} %collective-permute-done.18.refs_7_), channel_id=1, source_target_pairs={{0,126},{2,0},{4,2},{6,4},{8,6},{10,8},{12,10},{14,12},{16,14},{18... | collective-permute-start | bytes 4718600 | tf_op jit(solution)/shard_map/ppermute | solution.py:17
  172.9 2.4 broadcast_select_fusion.1
  175.3 2.0 pad_maximum_fusion
  177.4 22.3 %collective-permute-done.11.refs_6_ = f32[3072,128]{1,0:T(8,128)} collective-permute-done((f32[3072,128]{1,0:T(8,128)}, f32[3072,128]{1,0:T(8,128)}, u32[]{:S(2)}, u32[]{:S(2)}) %collective-permute-start.11) | collective-permute-done | bytes 1572896 | tf_op jit(solution)/shard_map/ppermute | solution.py:17
  199.7 6.9 %collective-permute-start.16 = (f32[3072,128]{1,0:T(8,128)}, f32[3072,128]{1,0:T(8,128)S(1)}, u32[]{:S(2)}, u32[]{:S(2)}) collective-permute-start(f32[3072,128]{1,0:T(8,128)} %collective-permute-done.12.refs_8_), channel_id=1, source_target_pairs={{0,126},{2,0},{4,2},{6,4},{8,6},{10,8},{12,10},{14,12},{16,14},{18... | collective-permute-start | bytes 4718600 | tf_op jit(solution)/shard_map/ppermute | solution.py:17
  206.6 18.8 %metric_near.1 = (f32[4,12,128,128]{3,2,1,0:T(8,128)}, f32[4,12,128,128]{3,2,1,0:T(8,128)}) custom-call(s32[2]{0:T(128)} %pad_add_fusion.1.meta.refs_0_, s32[4,24]{1,0:T(4,128)} %refs_1_.17, s32[2,40]{1,0:T(2,128)} %slice_convert_fusion.1.refs_3_.refs_1_.refs_2_, s32[2,40]{1,0:T(2,128)} %slice_convert_fusion.refs_4_.refs_3_, ...), custom_call_target="tpu_custom_call" | custom-call | tf_op jit(solution)/shard_map/metric_near/pallas_call | solution.py:227
  225.4 8.0 %collective-permute-done.19.refs_5_ = f32[3072,128]{1,0:T(8,128)} collective-permute-done((f32[3072,128]{1,0:T(8,128)}, f32[3072,128]{1,0:T(8,128)}, u32[]{:S(2)}, u32[]{:S(2)}) %collective-permute-start.19) | collective-permute-done | bytes 1572896 | tf_op jit(solution)/shard_map/ppermute | solution.py:17
  233.4 13.8 %metric_far0.1 = (f32[2,12,128,128]{3,2,1,0:T(8,128)}, f32[2,12,128,128]{3,2,1,0:T(8,128)}, f32[2,12,128,128]{3,2,1,0:T(8,128)}, f32[2,12,128,128]{3,2,1,0:T(8,128)}) custom-call(s32[2]{0:T(128)} %pad_add_fusion.1.meta.refs_0_, s32[4,24]{1,0:T(4,128)} %refs_1_.17, s32[2,40]{1,0:T(2,128)} %slice_convert_fusion.3.refs_2_.refs_0_, ...), custom_call_target="tpu_custom_call" | custom-call | tf_op jit(solution)/shard_map/metric_far0/pallas_call | solution.py:227
  247.2 19.8 %collective-permute-done.15.refs_5_ = f32[3072,128]{1,0:T(8,128)S(1)} collective-permute-done((f32[3072,128]{1,0:T(8,128)}, f32[3072,128]{1,0:T(8,128)S(1)}, u32[]{:S(2)}, u32[]{:S(2)}) %collective-permute-start.15) | collective-permute-done | bytes 1572896 | tf_op jit(solution)/shard_map/ppermute | solution.py:17
  267.0 1.1 copy-done.4
  268.7 9.0 %metric_far1.2 = (f32[2,12,128,128]{3,2,1,0:T(8,128)}, f32[2,12,128,128]{3,2,1,0:T(8,128)}) custom-call(s32[2]{0:T(128)} %pad_add_fusion.1.meta.refs_0_, s32[4,24]{1,0:T(4,128)} %refs_1_.17, s32[2,40]{1,0:T(2,128)} %slice_convert_fusion.3.refs_2_.refs_0_, s32[2,40]{1,0:T(2,128)} %slice_convert_fusion.2.refs_3_.refs_4_, ...), custom_call_target="tpu_custom_call" | custom-call | tf_op jit(solution)/shard_map/metric_far1/pallas_call | solution.py:227
  277.7 1.3 collective-permute-start.21
  279.0 9.1 %metric_far1.3 = (f32[2,12,128,128]{3,2,1,0:T(8,128)}, f32[2,12,128,128]{3,2,1,0:T(8,128)}) custom-call(s32[2]{0:T(128)} %pad_add_fusion.1.meta.refs_0_, s32[4,24]{1,0:T(4,128)} %refs_1_.17, s32[2,40]{1,0:T(2,128)} %slice_convert_fusion.3.refs_2_.refs_0_, s32[2,40]{1,0:T(2,128)} %slice_convert_fusion.2.refs_3_.refs_4_, ...), custom_call_target="tpu_custom_call" | custom-call | tf_op jit(solution)/shard_map/metric_far1/pallas_call | solution.py:227
  288.4 3.4 %collective-permute-done.22 = f32[2,12,128,128]{3,2,1,0:T(8,128)S(1)} collective-permute-done((f32[2,12,128,128]{3,2,1,0:T(8,128)}, f32[2,12,128,128]{3,2,1,0:T(8,128)S(1)}, u32[]{:S(2)}, u32[]{:S(2)}) %collective-permute-start.22) | collective-permute-done | bytes 1572896 | tf_op jit(solution)/shard_map/ppermute | solution.py:21
  291.9 2.0 pad_maximum_fusion.1
  (52 shorter events, 2.2 us)
Async XLA Ops:
  0.6 21.1 %collective-permute-start.3 = (f32[4,8,128,128]{3,2,1,0:T(8,128)}, f32[4,8,128,128]{3,2,1,0:T(8,128)}, u32[]{:S(2)}, u32[]{:S(2)}) collective-permute-start(f32[4,8,128,128]{3,2,1,0:T(8,128)} %table_a.1), channel_id=1, source_target_pairs={{0,1},{1,0},{2,3},{3,2},{4,5},{5,4},{6,7},{7,6},{8,9},{9,8},{10,11... | collective-permute-start | bytes 6291464 | tf_op jit(solution)/shard_map/ppermute | solution.py:21
  5.2 22.1 %copy-start.1 = (f32[1,16,128,128]{3,2,1,0:T(8,128)}, f32[1,16,128,128]{3,2,1,0:T(8,128)S(1)}, u32[]{:S(2)}) copy-start(f32[1,16,128,128]{3,2,1,0:T(8,128)S(1)} %get-tuple-element.76) | copy-start | bytes 3145732
  5.2 8.7 %copy-start.11 = (s32[4,8]{1,0:T(4,128)S(1)}, s32[4,8]{1,0:T(4,128)}, u32[]{:S(2)}) copy-start(s32[4,8]{1,0:T(4,128)} %cols_a.1) | copy-start | bytes 388
  5.3 22.0 %copy-start = (f32[2056,128]{1,0:T(8,128)}, f32[2056,128]{1,0:T(8,128)S(1)}, u32[]{:S(2)}) copy-start(f32[2056,128]{1,0:T(8,128)S(1)} %select_maximum_fusion.refs_6_.refs_9_) | copy-start | bytes 3158020
  5.3 32.2 %collective-permute-start = (f32[2056,128]{1,0:T(8,128)S(1)}, f32[2056,128]{1,0:T(8,128)S(1)}, u32[]{:S(2)}, u32[]{:S(2)}) collective-permute-start(f32[2056,128]{1,0:T(8,128)S(1)} %select_maximum_fusion.refs_6_.refs_9_), channel_id=1, source_target_pairs={{0,2},{2,4},{4,6},{6,8},{8,10},{10,12},{12,14},{14,16},{16,18},{18... | collective-permute-start | bytes 3158024 | tf_op jit(solution)/shard_map/ppermute | solution.py:17
  6.6 30.8 %collective-permute-start.1 = (f32[2056,128]{1,0:T(8,128)S(1)}, f32[2056,128]{1,0:T(8,128)}, u32[]{:S(2)}, u32[]{:S(2)}) collective-permute-start(f32[2056,128]{1,0:T(8,128)S(1)} %select_maximum_fusion.refs_6_.refs_9_), channel_id=1, source_target_pairs={{0,126},{2,0},{4,2},{6,4},{8,6},{10,8},{12,10},{14,12},{16,14},{18... | collective-permute-start | bytes 3158024 | tf_op jit(solution)/shard_map/ppermute | solution.py:17
  13.9 1.2 collective-permute-start.2
  14.2 45.8 %collective-permute-start.6 = (f32[2048,128]{1,0:T(8,128)S(1)}, f32[2048,128]{1,0:T(8,128)}, u32[]{:S(2)}, u32[]{:S(2)}) collective-permute-start(f32[2048,128]{1,0:T(8,128)S(1)} %bitcast.6), channel_id=1, source_target_pairs={{0,2},{2,4},{4,6},{6,8},{8,10},{10,12},{12,14},{14,16},{16,18},{18... | collective-permute-start | bytes 3145736 | tf_op jit(solution)/shard_map/ppermute | solution.py:17
  15.1 6.7 %copy-start.12 = (s32[4,8]{1,0:T(4,128)}, s32[4,8]{1,0:T(4,128)S(1)}, u32[]{:S(2)}) copy-start(s32[4,8]{1,0:T(4,128)S(1)} %collective-permute-done.2.cols_b) | copy-start | bytes 388
  15.1 44.9 %collective-permute-start.8 = (f32[2048,128]{1,0:T(8,128)S(1)}, f32[2048,128]{1,0:T(8,128)}, u32[]{:S(2)}, u32[]{:S(2)}) collective-permute-start(f32[2048,128]{1,0:T(8,128)S(1)} %bitcast.7), channel_id=1, source_target_pairs={{0,126},{2,0},{4,2},{6,4},{8,6},{10,8},{12,10},{14,12},{16,14},{18... | collective-permute-start | bytes 3145736 | tf_op jit(solution)/shard_map/ppermute | solution.py:17
  37.4 31.3 %copy-start.6 = (f32[2056,128]{1,0:T(8,128)}, f32[2056,128]{1,0:T(8,128)S(1)}, u32[]{:S(2)}) copy-start(f32[2056,128]{1,0:T(8,128)S(1)} %collective-permute-done.refs_8_.refs_7_) | copy-start | bytes 3158020
  37.4 47.6 %collective-permute-start.5 = (f32[2056,128]{1,0:T(8,128)}, f32[2056,128]{1,0:T(8,128)}, u32[]{:S(2)}, u32[]{:S(2)}) collective-permute-start(f32[2056,128]{1,0:T(8,128)} %collective-permute-done.1.refs_10_.refs_11_), channel_id=1, source_target_pairs={{0,126},{2,0},{4,2},{6,4},{8,6},{10,8},{12,10},{14,12},{16,14},{18... | collective-permute-start | bytes 3158024 | tf_op jit(solution)/shard_map/ppermute | solution.py:17
  44.3 42.0 %collective-permute-start.4 = (f32[2056,128]{1,0:T(8,128)S(1)}, f32[2056,128]{1,0:T(8,128)}, u32[]{:S(2)}, u32[]{:S(2)}) collective-permute-start(f32[2056,128]{1,0:T(8,128)S(1)} %collective-permute-done.refs_8_.refs_7_), channel_id=1, source_target_pairs={{0,2},{2,4},{4,6},{6,8},{8,10},{10,12},{12,14},{14,16},{16,18},{18... | collective-permute-start | bytes 3158024 | tf_op jit(solution)/shard_map/ppermute | solution.py:17
  60.0 44.9 %collective-permute-start.7 = (f32[2048,128]{1,0:T(8,128)}, f32[2048,128]{1,0:T(8,128)S(1)}, u32[]{:S(2)}, u32[]{:S(2)}) collective-permute-start(f32[2048,128]{1,0:T(8,128)} %collective-permute-done.6.refs_9_.refs_8_), channel_id=1, source_target_pairs={{0,2},{2,4},{4,6},{6,8},{8,10},{10,12},{12,14},{14,16},{16,18},{18... | collective-permute-start | bytes 3145736 | tf_op jit(solution)/shard_map/ppermute | solution.py:17
  60.0 44.9 %collective-permute-start.9 = (f32[2048,128]{1,0:T(8,128)}, f32[2048,128]{1,0:T(8,128)S(1)}, u32[]{:S(2)}, u32[]{:S(2)}) collective-permute-start(f32[2048,128]{1,0:T(8,128)} %collective-permute-done.8.refs_11_.refs_12_), channel_id=1, source_target_pairs={{0,126},{2,0},{4,2},{6,4},{8,6},{10,8},{12,10},{14,12},{16,14},{18... | collective-permute-start | bytes 3145736 | tf_op jit(solution)/shard_map/ppermute | solution.py:17
  104.9 1.0 copy-start.2
  104.9 1.3 copy-start.3
  113.7 8.2 %collective-permute-start.13 = (f32[1,24,128,128]{3,2,1,0:T(8,128)}, f32[1,24,128,128]{3,2,1,0:T(8,128)}, u32[]{:S(2)}, u32[]{:S(2)}) collective-permute-start(f32[1,24,128,128]{3,2,1,0:T(8,128)} %get-tuple-element.51), channel_id=1, source_target_pairs={{0,1},{1,0},{2,3},{3,2},{4,5},{5,4},{6,7},{7,6},{8,9},{9,8},{10,11... | collective-permute-start | bytes 4718600 | tf_op jit(solution)/shard_map/ppermute | solution.py:21
  114.3 7.6 %copy-start.8 = (f32[1,24,128,128]{3,2,1,0:T(8,128)S(1)}, f32[1,24,128,128]{3,2,1,0:T(8,128)}, u32[]{:S(2)}) copy-start(f32[1,24,128,128]{3,2,1,0:T(8,128)} %get-tuple-element.50) | copy-start | bytes 4718596
  121.9 9.8 %collective-permute-start.10 = (f32[1,24,128,128]{3,2,1,0:T(8,128)}, f32[1,24,128,128]{3,2,1,0:T(8,128)S(1)}, u32[]{:S(2)}, u32[]{:S(2)}) collective-permute-start(f32[1,24,128,128]{3,2,1,0:T(8,128)} %get-tuple-element.47), channel_id=1, source_target_pairs={{0,1},{1,0},{2,3},{3,2},{4,5},{5,4},{6,7},{7,6},{8,9},{9,8},{10,11... | collective-permute-start | bytes 4718600 | tf_op jit(solution)/shard_map/ppermute | solution.py:21
  121.9 9.8 %copy-start.7 = (f32[1,24,128,128]{3,2,1,0:T(8,128)S(1)}, f32[1,24,128,128]{3,2,1,0:T(8,128)}, u32[]{:S(2)}) copy-start(f32[1,24,128,128]{3,2,1,0:T(8,128)} %get-tuple-element.46) | copy-start | bytes 4718596
  124.8 41.2 %collective-permute-start.17 = (f32[3072,128]{1,0:T(8,128)}, f32[3072,128]{1,0:T(8,128)}, u32[]{:S(2)}, u32[]{:S(2)}) collective-permute-start(f32[3072,128]{1,0:T(8,128)} %bitcast.5.refs_4_), channel_id=1, source_target_pairs={{0,2},{2,4},{4,6},{6,8},{8,10},{10,12},{12,14},{14,16},{16,18},{18... | collective-permute-start | bytes 4718600 | tf_op jit(solution)/shard_map/ppermute | solution.py:17
  124.8 41.2 %collective-permute-start.18 = (f32[3072,128]{1,0:T(8,128)}, f32[3072,128]{1,0:T(8,128)}, u32[]{:S(2)}, u32[]{:S(2)}) collective-permute-start(f32[3072,128]{1,0:T(8,128)} %bitcast.5.refs_4_), channel_id=1, source_target_pairs={{0,126},{2,0},{4,2},{6,4},{8,6},{10,8},{12,10},{14,12},{16,14},{18... | collective-permute-start | bytes 4718600 | tf_op jit(solution)/shard_map/ppermute | solution.py:17
  134.6 38.3 %collective-permute-start.14 = (f32[2,12,128,128]{3,2,1,0:T(8,128)S(1)}, f32[2,12,128,128]{3,2,1,0:T(8,128)S(1)}, u32[]{:S(2)}, u32[]{:S(2)}) collective-permute-start(f32[2,12,128,128]{3,2,1,0:T(8,128)S(1)} %fusion), channel_id=1, source_target_pairs={{0,1},{1,0},{2,3},{3,2},{4,5},{5,4},{6,7},{7,6},{8,9},{9,8},{10,11... | collective-permute-start | bytes 4718600 | tf_op jit(solution)/shard_map/ppermute | solution.py:21
  135.7 64.0 %collective-permute-start.11 = (f32[3072,128]{1,0:T(8,128)}, f32[3072,128]{1,0:T(8,128)}, u32[]{:S(2)}, u32[]{:S(2)}) collective-permute-start(f32[3072,128]{1,0:T(8,128)} %bitcast.4.refs_5_), channel_id=1, source_target_pairs={{0,2},{2,4},{4,6},{6,8},{8,10},{10,12},{12,14},{14,16},{16,18},{18... | collective-permute-start | bytes 4718600 | tf_op jit(solution)/shard_map/ppermute | solution.py:17
  135.7 64.0 %collective-permute-start.12 = (f32[3072,128]{1,0:T(8,128)}, f32[3072,128]{1,0:T(8,128)}, u32[]{:S(2)}, u32[]{:S(2)}) collective-permute-start(f32[3072,128]{1,0:T(8,128)} %bitcast.4.refs_5_), channel_id=1, source_target_pairs={{0,126},{2,0},{4,2},{6,4},{8,6},{10,8},{12,10},{14,12},{16,14},{18... | collective-permute-start | bytes 4718600 | tf_op jit(solution)/shard_map/ppermute | solution.py:17
  166.0 67.4 %collective-permute-start.19 = (f32[3072,128]{1,0:T(8,128)}, f32[3072,128]{1,0:T(8,128)}, u32[]{:S(2)}, u32[]{:S(2)}) collective-permute-start(f32[3072,128]{1,0:T(8,128)} %collective-permute-done.17.refs_5_), channel_id=1, source_target_pairs={{0,2},{2,4},{4,6},{6,8},{8,10},{10,12},{12,14},{14,16},{16,18},{18... | collective-permute-start | bytes 4718600 | tf_op jit(solution)/shard_map/ppermute | solution.py:17
  166.0 67.4 %collective-permute-start.20 = (f32[3072,128]{1,0:T(8,128)}, f32[3072,128]{1,0:T(8,128)}, u32[]{:S(2)}, u32[]{:S(2)}) collective-permute-start(f32[3072,128]{1,0:T(8,128)} %collective-permute-done.18.refs_7_), channel_id=1, source_target_pairs={{0,126},{2,0},{4,2},{6,4},{8,6},{10,8},{12,10},{14,12},{16,14},{18... | collective-permute-start | bytes 4718600 | tf_op jit(solution)/shard_map/ppermute | solution.py:17
  199.7 67.3 %collective-permute-start.15 = (f32[3072,128]{1,0:T(8,128)}, f32[3072,128]{1,0:T(8,128)S(1)}, u32[]{:S(2)}, u32[]{:S(2)}) collective-permute-start(f32[3072,128]{1,0:T(8,128)} %collective-permute-done.11.refs_6_), channel_id=1, source_target_pairs={{0,2},{2,4},{4,6},{6,8},{8,10},{10,12},{12,14},{14,16},{16,18},{18... | collective-permute-start | bytes 4718600 | tf_op jit(solution)/shard_map/ppermute | solution.py:17
  199.7 67.3 %collective-permute-start.16 = (f32[3072,128]{1,0:T(8,128)}, f32[3072,128]{1,0:T(8,128)S(1)}, u32[]{:S(2)}, u32[]{:S(2)}) collective-permute-start(f32[3072,128]{1,0:T(8,128)} %collective-permute-done.12.refs_8_), channel_id=1, source_target_pairs={{0,126},{2,0},{4,2},{6,4},{8,6},{10,8},{12,10},{14,12},{16,14},{18... | collective-permute-start | bytes 4718600 | tf_op jit(solution)/shard_map/ppermute | solution.py:17
  267.0 1.1 copy-start.4
  267.0 1.7 copy-start.5
  277.7 10.5 %collective-permute-start.21 = (f32[2,12,128,128]{3,2,1,0:T(8,128)}, f32[2,12,128,128]{3,2,1,0:T(8,128)S(1)}, u32[]{:S(2)}, u32[]{:S(2)}) collective-permute-start(f32[2,12,128,128]{3,2,1,0:T(8,128)} %get-tuple-element.66), channel_id=1, source_target_pairs={{0,1},{1,0},{2,3},{3,2},{4,5},{5,4},{6,7},{7,6},{8,9},{9,8},{10,11... | collective-permute-start | bytes 4718600 | tf_op jit(solution)/shard_map/ppermute | solution.py:21
  279.0 9.1 %copy-start.9 = (f32[2,12,128,128]{3,2,1,0:T(8,128)S(1)}, f32[2,12,128,128]{3,2,1,0:T(8,128)}, u32[]{:S(2)}) copy-start(f32[2,12,128,128]{3,2,1,0:T(8,128)} %get-tuple-element.65) | copy-start | bytes 4718596
  288.1 3.6 %collective-permute-start.22 = (f32[2,12,128,128]{3,2,1,0:T(8,128)}, f32[2,12,128,128]{3,2,1,0:T(8,128)S(1)}, u32[]{:S(2)}, u32[]{:S(2)}) collective-permute-start(f32[2,12,128,128]{3,2,1,0:T(8,128)} %get-tuple-element.71), channel_id=1, source_target_pairs={{0,1},{1,0},{2,3},{3,2},{4,5},{5,4},{6,7},{7,6},{8,9},{9,8},{10,11... | collective-permute-start | bytes 4718600 | tf_op jit(solution)/shard_map/ppermute | solution.py:21
  288.1 3.6 %copy-start.10 = (f32[2,12,128,128]{3,2,1,0:T(8,128)S(1)}, f32[2,12,128,128]{3,2,1,0:T(8,128)}, u32[]{:S(2)}) copy-start(f32[2,12,128,128]{3,2,1,0:T(8,128)} %get-tuple-element.70) | copy-start | bytes 4718596

commit v3 on v2

--- a/solution.py
+++ b/solution.py
@@ -108,21 +108,37 @@
     copy_last(out, (part_a, part_b), lambda part, row: 2 * part + row)
 
 
-def stage_kernel(gs, crs, pieces, starts, counts, total, by_rows, row0, col0, has_acc, *refs):
+def stage_kernel(gs, crs, pieces, starts, counts, total, by_rows, row0, col0, has_acc, portions, *refs):
     count, depth = len(gs), len(crs)
     meta, outcols = refs[:2]
     patterns = refs[2 : 2 + count]
     refs = refs[2 + count :]
     lefts, refs = refs[0], list(refs[1:])
-    tables = []
+    sources = [refs.pop(0) for _ in range(sum(pieces))]
+    acc_sources = [refs.pop(0) for _ in range(2 if has_acc else 0)]
+    results = [refs.pop(0) for _ in range(2 * portions)]
+    right_high, right_low, dense, left_held, sems = refs[:5]
+    refs = refs[5:]
+    held = [refs.pop(0) for _ in sources]
+    acc = [refs.pop(0) for _ in acc_sources]
+    outs = refs
+    copies = []
+
+    def start(source, target):
+        copies.append(pltpu.make_async_copy(source, target, sems.at[len(copies)]))
+        copies[-1].start()
+        return copies[-1]
+
+    arriving = [start(source.at[pl.ds(0, target.shape[0])], target) for source, target in zip(sources, held)]
+    left_copies = []
+    for gi, g in enumerate(gs):
+        for ci, c in enumerate(crs):
+            source = lefts.at[g + 2, c] if lefts.shape[0] == 5 else lefts.at[gi, 0]
+            left_copies.append(start(source, left_held.at[gi, ci]))
+    acc_copies = [start(source, target) for source, target in zip(acc_sources, acc)]
+    tables, held = [], list(zip(held, arriving))
     for number in pieces:
-        tables.append([refs.pop(0) for _ in range(number)])
-    acc = None
-    if has_acc:
-        acc, refs = refs[:2], refs[2:]
-    right_high, right_low, dense = refs[-3:]
-    outs = refs[:-3]
-    portions = len(outs) // 2
+        tables.append([held.pop(0) for _ in range(number)])
     core = meta[1]
     base = 4 * meta[0] - 16
     rows = dense.shape[1]
@@ -130,9 +146,11 @@
     for gi in range(count):
         clear(right_high.at[gi], 0, counts[gi])
         clear(right_low.at[gi], 0, counts[gi])
+    for gi in range(count):
         for ci, c in enumerate(crs):
             cols, first = patterns[gi], col0
-            for table in tables[gi * depth + ci]:
+            for table, copy in tables[gi * depth + ci]:
+                copy.wait()
 
                 def right_body(m, carry, gi=gi, ci=ci, c=c, cols=cols, table=table, first=first):
                     rel = wrap(cols[c, first + m] - base, total) - starts[gi]
@@ -150,61 +168,61 @@
             [ref[gi, at + j].reshape(128 * depth, 128) for j in range(4)], axis=1
         )
 
-    done = (0, 0)
-    for gi, g in enumerate(gs):
-        if lefts.shape[0] == 5:
-            left = [lefts[g + 2, c].reshape(rows * 128, 256) for c in crs]
-        else:
-            left = [lefts[gi, 0].reshape(rows * 128, 256)]
+    for copy in left_copies:
+        copy.wait()
+    lefts_of = []
+    for gi in range(count):
+        left = [left_held[gi, ci].reshape(rows * 128, 256) for ci in range(depth)]
         highs = [part[:, :128] for part in left]
         lows = [part[:, 128:] for part in left]
-        left = jnp.concatenate(highs + lows + highs, axis=1)
-
-        def body(q, carry, gi=gi, left=left, add=False):
-            rh, rl = rights(right_high, gi, 4 * q), rights(right_low, gi, 4 * q)
-            out = jnp.dot(left, jnp.concatenate([rh, rh, rl], axis=0), preferred_element_type=F32)
-            to = starts[gi] + 4 * q
+        lefts_of.append(highs + lows + highs)
+
+    edges = sorted({0, WINDOW} | set(starts) | {s + c for s, c in zip(starts, counts)})
+    for first, last in zip(edges, edges[1:]):
+        active = [gi for gi in range(count) if starts[gi] <= first and last <= starts[gi] + counts[gi]]
+        if not active:
+            clear(dense, first, last)
+            continue
+        left = jnp.concatenate([part for gi in active for part in lefts_of[gi]], axis=1)
+
+        def body(q, carry, active=active, left=left):
+            right = []
+            for gi in active:
+                rh = rights(right_high, gi, 4 * q - starts[gi])
+                right += [rh, rh, rights(right_low, gi, 4 * q - starts[gi])]
+            out = jnp.dot(left, jnp.concatenate(right, axis=0), preferred_element_type=F32)
             for j in range(4):
-                value = out[:, 128 * j : 128 * j + 128].reshape(rows, 128, 128)
-                dense[to + j] = dense[to + j] + value if add else value
+                dense[4 * q + j] = out[:, 128 * j : 128 * j + 128].reshape(rows, 128, 128)
             return carry
 
-        start, stop = starts[gi], starts[gi] + counts[gi]
-        low, high = max(start, done[0]), min(stop, done[1])
-        if low >= high:
-            spans = [(start, stop, False)]
-        else:
-            spans = [(start, low, False), (low, high, True), (high, stop, False)]
-        for first, last, add in spans:
-            if last > first:
-                lax.fori_loop(
-                    (first - start) // 4, (last - start) // 4, functools.partial(body, add=add), 0, unroll=2
-                )
-        done = (start, stop) if gi == 0 else (min(start, done[0]), max(stop, done[1]))
-    clear(dense, 0, done[0])
-    clear(dense, done[1], WINDOW)
-    kept_rows, kept_cols = outs[0].shape[0] * portions, outs[0].shape[1]
-    each = outs[0].shape[0]
-    for which in range(2):
+        lax.fori_loop(first // 4, last // 4, body, 0, unroll=2)
+    for copy in acc_copies:
+        copy.wait()
+    each, kept_cols = outs[0].shape[:2]
+    leaving = []
+    for which in (1, 0):
         side = core if which == 0 else 1 - core
-        for row in range(kept_rows):
-            source = side * kept_rows + row if by_rows else row
+        for row in range(each * portions):
+            source = side * each * portions + row if by_rows else row
             at_row = 2 * side + row0 + row if by_rows else row0 + row
             at_col = 0 if by_rows else kept_cols * side
-
-            def out_body(y, carry, which=which, row=row, source=source, at_row=at_row, at_col=at_col):
-                rel = wrap(outcols[at_row, at_col + y] - base, total)
-                value = dense[rel, source]
-                if acc is not None:
-                    value = value + acc[which][row, y]
-                outs[which * portions + row // each][row % each, y] = value
+            portion = which * portions + row // each
+            own, sum_in = outs[portion].at[row % each], acc[which].at[row] if acc else None
+
+            def out_body(y, carry, own=own, sum_in=sum_in, source=source, at_row=at_row, at_col=at_col):
+                value = dense[wrap(outcols[at_row, at_col + y] - base, total), source]
+                own[y] = value if sum_in is None else value + sum_in[y]
                 return carry
 
             lax.fori_loop(0, kept_cols, out_body, 0, unroll=4)
+            leaving.append(start(own, results[portion].at[row % each]))
+    for copy in leaving:
+        copy.wait()
 
 
 SMEM = pl.BlockSpec(memory_space=pltpu.SMEM)
 VMEM = pl.BlockSpec(memory_space=pltpu.VMEM)
+HERE = pl.BlockSpec(memory_space=pl.ANY)
 PARAMS = pltpu.CompilerParams(vmem_limit_bytes=60 << 20)
 
 
@@ -219,7 +237,7 @@
         row0, rows = 2 * (part or 0), out[0]
     tables = [tables[g][c] for g in gs for c in crs]
     kernel = functools.partial(
-        stage_kernel, gs, crs, [len(t) for t in tables], starts, counts, total, by_rows, row0, col0, bool(acc)
+        stage_kernel, gs, crs, [len(t) for t in tables], starts, counts, total, by_rows, row0, col0, bool(acc), portions
     )
     shape = jax.ShapeDtypeStruct((out[0] // portions,) + out[1:], F32)
     blocks = [piece for table in tables for piece in table]
@@ -228,13 +246,18 @@
         kernel,
         name=name,
         out_shape=[shape] * (2 * portions),
-        in_specs=[SMEM] * (2 + len(gs)) + [VMEM] * (1 + len(blocks) + len(acc)),
-        out_specs=[VMEM] * (2 * portions),
+        in_specs=[SMEM] * (2 + len(gs)) + [HERE] * (1 + len(blocks) + len(acc)),
+        out_specs=[HERE] * (2 * portions),
         scratch_shapes=[
             pltpu.VMEM((len(gs), window + 1, len(crs), 128, 128), BF16),
             pltpu.VMEM((len(gs), window + 1, len(crs), 128, 128), BF16),
             pltpu.VMEM((WINDOW, rows, 128, 128), F32),
-        ],
+            pltpu.VMEM((len(gs), len(crs), rows, 128, 256), BF16),
+            pltpu.SemaphoreType.DMA((len(blocks) + len(gs) * len(crs) + len(acc) + 2 * out[0],)),
+        ]
+        + [pltpu.VMEM((b.shape[0] // 128 * 128, 128), F32) for b in blocks]
+        + [pltpu.VMEM(a.shape, F32) for a in acc]
+        + [pltpu.VMEM(shape.shape, F32)] * (2 * portions),
         compiler_params=PARAMS,
         cost_estimate=pl.CostEstimate(
             flops=0,

time: 294 us -> 289 us (0.983)
  Pallas kernels: 122 us -> 99.6 us
  waiting for transfers between devices: 86.2 us -> 103 us
    pallas_call x9, Pallas kernels: 106 us -> 82.7 us  [stage(): pl.pallas_call(kernel, name=name, out_shape=[shape] * (2 * portions), in_...]
    ppermute x16, waiting for transfers between devices: 82 us -> 98.6 us  [ring(): lax.ppermute(array, 'rows', [(i, (i + by) % devices) for i in range(devic...]
  transfers between devices with their start and end apart: 23 -> 23, of which waited for: 9 -> 9; matrix products, arithmetic and copies ran while one was open for 6% -> 6% of each run, Pallas kernels for 36% -> 30%
where the time goes in v3:
time: 289 us; the launch traced here: 288 us
  waiting for transfers between devices  103 us (36%)
  Pallas kernels  99.6 us (34%)
  starting transfers between devices  61.3 us (21%)
  other arithmetic  18.9 us (7%)
  local copies, waits for them, and re-layouts  4.7 us (2%)
    ppermute x16, waiting for transfers between devices, ring(): lax.ppermute(array, 'rows', [(i, (i + by) % devices) for i in range(devic...  98.6 us
    pallas_call x9, Pallas kernels, stage(): pl.pallas_call(kernel, name=name, out_shape=[shape] * (2 * portions), in_...  82.7 us
    ppermute x16, starting transfers between devices, ring(): lax.ppermute(array, 'rows', [(i, (i + by) % devices) for i in range(devic...  56.1 us
    pallas_call x2, Pallas kernels, left_call(): pl.pallas_call(kernel, name=name, out_shape=[out, last, last], in_specs=[...  16.9 us
  transfers between devices with their start and end apart: 23, of which 9 were waited for; matrix products, arithmetic and copies ran while one was open for 6% of the time, Pallas kernels for 30%

profile of v3, /device:TPU:1, one launch (start us, length us, event | category | flops | bytes accessed | tf_op | source)
XLA Modules:
  0.0 288.2 jit_solution(13708759902643377786)
XLA Ops:
  0.6 1.5 collective-permute-start.3
  2.1 0.8 pad_add_fusion
  3.5 1.7 constant_dynamic-slice_fusion
  5.3 1.4 collective-permute-start
  6.6 7.3 %collective-permute-start.1 = (f32[2056,128]{1,0:T(8,128)S(1)}, f32[2056,128]{1,0:T(8,128)}, u32[]{:S(2)}, u32[]{:S(2)}) collective-permute-start(f32[2056,128]{1,0:T(8,128)S(1)} %select_maximum_fusion.refs_6_.refs_9_), channel_id=1, source_target_pairs={{0,126},{2,0},{4,2},{6,4},{8,6},{10,8},{12,10},{14,12},{16,14},{18... | collective-permute-start | bytes 3158024 | tf_op jit(solution)/shard_map/ppermute | solution.py:17
  14.2 0.8 collective-permute-done.2.cols_b
  15.1 6.0 %collective-permute-start.8 = (f32[2048,128]{1,0:T(8,128)S(1)}, f32[2048,128]{1,0:T(8,128)}, u32[]{:S(2)}, u32[]{:S(2)}) collective-permute-start(f32[2048,128]{1,0:T(8,128)S(1)} %bitcast.7), channel_id=1, source_target_pairs={{0,126},{2,0},{4,2},{6,4},{8,6},{10,8},{12,10},{14,12},{16,14},{18... | collective-permute-start | bytes 3145736 | tf_op jit(solution)/shard_map/ppermute | solution.py:17
  21.1 0.6 pad_add_fusion.1.meta.refs_0_
  21.7 5.5 %margin_left.1 = (bf16[5,2,4,128,256]{4,3,2,1,0:T(8,128)(2,1)}, bf16[2,1,2,128,256]{4,3,2,1,0:T(8,128)(2,1)}, bf16[2,1,2,128,256]{4,3,2,1,0:T(8,128)(2,1)}) custom-call(s32[2]{0:T(128)} %pad_add_fusion.1.meta.refs_0_, s32[4,8]{1,0:T(4,128)} %cols_a.1, s32[4,8]{1,0:T(4,128)} %copy-done.12, f32[4,8,128,128]{3,2,1,0:T(8,128)} %table_a.1, ...), custom_call_target="tpu_custom_call" | custom-call | tf_op jit(solution)/shard_map/margin_left/pallas_call | solution.py:275
  27.3 10.2 %collective-permute-done.refs_8_.refs_7_ = f32[2056,128]{1,0:T(8,128)S(1)} collective-permute-done((f32[2056,128]{1,0:T(8,128)S(1)}, f32[2056,128]{1,0:T(8,128)S(1)}, u32[]{:S(2)}, u32[]{:S(2)}) %collective-permute-start) | collective-permute-done | bytes 1052704 | tf_op jit(solution)/shard_map/ppermute | solution.py:17
  37.4 6.9 %collective-permute-start.5 = (f32[2056,128]{1,0:T(8,128)}, f32[2056,128]{1,0:T(8,128)}, u32[]{:S(2)}, u32[]{:S(2)}) collective-permute-start(f32[2056,128]{1,0:T(8,128)} %collective-permute-done.1.refs_10_.refs_11_), channel_id=1, source_target_pairs={{0,126},{2,0},{4,2},{6,4},{8,6},{10,8},{12,10},{14,12},{16,14},{18... | collective-permute-start | bytes 3158024 | tf_op jit(solution)/shard_map/ppermute | solution.py:17
  44.3 15.7 %collective-permute-done.6.refs_9_.refs_8_ = f32[2048,128]{1,0:T(8,128)} collective-permute-done((f32[2048,128]{1,0:T(8,128)S(1)}, f32[2048,128]{1,0:T(8,128)}, u32[]{:S(2)}, u32[]{:S(2)}) %collective-permute-start.6) | collective-permute-done | bytes 1048608 | tf_op jit(solution)/shard_map/ppermute | solution.py:17
  60.0 6.9 %collective-permute-start.9 = (f32[2048,128]{1,0:T(8,128)}, f32[2048,128]{1,0:T(8,128)S(1)}, u32[]{:S(2)}, u32[]{:S(2)}) collective-permute-start(f32[2048,128]{1,0:T(8,128)} %collective-permute-done.8.refs_11_.refs_12_), channel_id=1, source_target_pairs={{0,126},{2,0},{4,2},{6,4},{8,6},{10,8},{12,10},{14,12},{16,14},{18... | collective-permute-start | bytes 3145736 | tf_op jit(solution)/shard_map/ppermute | solution.py:17
  66.9 1.3 slice_convert_fusion.refs_4_.refs_3_
  68.1 0.6 slice_convert_fusion.1.refs_3_.refs_1_.refs_2_
  68.7 13.3 %product_near.1 = (f32[2,24,128,128]{3,2,1,0:T(8,128)}, f32[2,24,128,128]{3,2,1,0:T(8,128)}) custom-call(s32[2]{0:T(128)} %pad_add_fusion.1.meta.refs_0_, s32[4,24]{1,0:T(4,128)} %refs_1_.12, s32[2,40]{1,0:T(2,128)} %get-tuple-element.73.refs_2_, s32[2,40]{1,0:T(2,128)} %slice_convert_fusion.1.refs_3_.refs_1_.refs_2_, ...), custom_call_target="tpu_custom_call" | custom-call | tf_op jit(solution)/shard_map/product_near/pallas_call | solution.py:245
  82.1 1.2 slice_convert_fusion.2.refs_3_.refs_4_
  83.3 1.3 slice_convert_fusion.3.refs_2_.refs_0_
  84.5 8.7 %product_far0.1 = (f32[1,24,128,128]{3,2,1,0:T(8,128)}, f32[1,24,128,128]{3,2,1,0:T(8,128)}, f32[1,24,128,128]{3,2,1,0:T(8,128)}, f32[1,24,128,128]{3,2,1,0:T(8,128)}) custom-call(s32[2]{0:T(128)} %pad_add_fusion.1.meta.refs_0_, s32[4,24]{1,0:T(4,128)} %refs_1_.12, s32[2,40]{1,0:T(2,128)} %slice_convert_fusion.3.refs_2_.refs_0_, ...), custom_call_target="tpu_custom_call" | custom-call | tf_op jit(solution)/shard_map/product_far0/pallas_call | solution.py:245
  93.3 11.6 %collective-permute-done.7.refs_5_.refs_6_ = f32[2048,128]{1,0:T(8,128)S(1)} collective-permute-done((f32[2048,128]{1,0:T(8,128)}, f32[2048,128]{1,0:T(8,128)S(1)}, u32[]{:S(2)}, u32[]{:S(2)}) %collective-permute-start.7) | collective-permute-done | bytes 1048608 | tf_op jit(solution)/shard_map/ppermute | solution.py:17
  104.9 1.0 copy-done.2
  106.2 6.5 %product_far1.3 = (f32[1,24,128,128]{3,2,1,0:T(8,128)}, f32[1,24,128,128]{3,2,1,0:T(8,128)}) custom-call(s32[2]{0:T(128)} %pad_add_fusion.1.meta.refs_0_, s32[4,24]{1,0:T(4,128)} %refs_1_.12, s32[2,40]{1,0:T(2,128)} %slice_convert_fusion.3.refs_2_.refs_0_, s32[2,40]{1,0:T(2,128)} %slice_convert_fusion.2.refs_3_.refs_4_, ...), custom_call_target="tpu_custom_call" | custom-call | tf_op jit(solution)/shard_map/product_far1/pallas_call | solution.py:245
  112.7 0.7 collective-permute-start.13
  113.4 6.6 %product_far1.2 = (f32[1,24,128,128]{3,2,1,0:T(8,128)}, f32[1,24,128,128]{3,2,1,0:T(8,128)}) custom-call(s32[2]{0:T(128)} %pad_add_fusion.1.meta.refs_0_, s32[4,24]{1,0:T(4,128)} %refs_1_.12, s32[2,40]{1,0:T(2,128)} %slice_convert_fusion.3.refs_2_.refs_0_, s32[2,40]{1,0:T(2,128)} %slice_convert_fusion.2.refs_3_.refs_4_, ...), custom_call_target="tpu_custom_call" | custom-call | tf_op jit(solution)/shard_map/product_far1/pallas_call | solution.py:245
  120.1 2.8 add.37
  123.0 6.9 %collective-permute-start.18 = (f32[3072,128]{1,0:T(8,128)}, f32[3072,128]{1,0:T(8,128)}, u32[]{:S(2)}, u32[]{:S(2)}) collective-permute-start(f32[3072,128]{1,0:T(8,128)} %bitcast.5.refs_4_), channel_id=1, source_target_pairs={{0,126},{2,0},{4,2},{6,4},{8,6},{10,8},{12,10},{14,12},{16,14},{18... | collective-permute-start | bytes 4718600 | tf_op jit(solution)/shard_map/ppermute | solution.py:17
  129.9 1.4 add.36
  131.3 1.5 fusion
  132.7 1.1 collective-permute-start.14
  133.9 6.9 %collective-permute-start.12 = (f32[3072,128]{1,0:T(8,128)}, f32[3072,128]{1,0:T(8,128)}, u32[]{:S(2)}, u32[]{:S(2)}) collective-permute-start(f32[3072,128]{1,0:T(8,128)} %bitcast.4.refs_5_), channel_id=1, source_target_pairs={{0,126},{2,0},{4,2},{6,4},{8,6},{10,8},{12,10},{14,12},{16,14},{18... | collective-permute-start | bytes 4718600 | tf_op jit(solution)/shard_map/ppermute | solution.py:17
  140.8 11.4 %factor_left.1 = (bf16[5,2,4,128,256]{4,3,2,1,0:T(8,128)(2,1)}, bf16[2,1,2,128,256]{4,3,2,1,0:T(8,128)(2,1)}, bf16[2,1,2,128,256]{4,3,2,1,0:T(8,128)(2,1)}) custom-call(s32[2]{0:T(128)} %pad_add_fusion.1.meta.refs_0_, s32[2,40]{1,0:T(2,128)} %slice_convert_fusion.3.refs_2_.refs_0_, s32[2,40]{1,0:T(2,128)} %slice_convert_fusion.1.refs_3_.refs_1_.refs_2_, ...), custom_call_target="tpu_custom_call" | custom-call | tf_op jit(solution)/shard_map/factor_left/pallas_call | solution.py:275
  152.1 10.1 %metric_own.1 = (f32[4,12,128,128]{3,2,1,0:T(8,128)}, f32[4,12,128,128]{3,2,1,0:T(8,128)}) custom-call(s32[2]{0:T(128)} %pad_add_fusion.1.meta.refs_0_, s32[4,24]{1,0:T(4,128)} %refs_1_.17, s32[2,40]{1,0:T(2,128)} %get-tuple-element.73.refs_2_, bf16[5,2,4,128,256]{4,3,2,1,0:T(8,128)(2,1)} %get-tuple-element.56.refs_3_.refs_4_, f32[3072,128]{1,0:T(8,128)} %bitcast.5.refs_4_, ...), custom_call_target="tpu_custom_call" | custom-call | tf_op jit(solution)/shard_map/metric_own/pallas_call | solution.py:245
  162.3 1.9 collective-permute-done.17.refs_5_
  164.2 6.9 %collective-permute-start.20 = (f32[3072,128]{1,0:T(8,128)}, f32[3072,128]{1,0:T(8,128)}, u32[]{:S(2)}, u32[]{:S(2)}) collective-permute-start(f32[3072,128]{1,0:T(8,128)} %collective-permute-done.18.refs_7_), channel_id=1, source_target_pairs={{0,126},{2,0},{4,2},{6,4},{8,6},{10,8},{12,10},{14,12},{16,14},{18... | collective-permute-start | bytes 4718600 | tf_op jit(solution)/shard_map/ppermute | solution.py:17
  171.1 2.4 broadcast_select_fusion.1
  173.5 2.0 pad_maximum_fusion
  175.6 22.3 %collective-permute-done.11.refs_6_ = f32[3072,128]{1,0:T(8,128)} collective-permute-done((f32[3072,128]{1,0:T(8,128)}, f32[3072,128]{1,0:T(8,128)}, u32[]{:S(2)}, u32[]{:S(2)}) %collective-permute-start.11) | collective-permute-done | bytes 1572896 | tf_op jit(solution)/shard_map/ppermute | solution.py:17
  197.9 6.9 %collective-permute-start.16 = (f32[3072,128]{1,0:T(8,128)}, f32[3072,128]{1,0:T(8,128)S(1)}, u32[]{:S(2)}, u32[]{:S(2)}) collective-permute-start(f32[3072,128]{1,0:T(8,128)} %collective-permute-done.12.refs_8_), channel_id=1, source_target_pairs={{0,126},{2,0},{4,2},{6,4},{8,6},{10,8},{12,10},{14,12},{16,14},{18... | collective-permute-start | bytes 4718600 | tf_op jit(solution)/shard_map/ppermute | solution.py:17
  204.8 14.1 %metric_near.1 = (f32[4,12,128,128]{3,2,1,0:T(8,128)}, f32[4,12,128,128]{3,2,1,0:T(8,128)}) custom-call(s32[2]{0:T(128)} %pad_add_fusion.1.meta.refs_0_, s32[4,24]{1,0:T(4,128)} %refs_1_.17, s32[2,40]{1,0:T(2,128)} %slice_convert_fusion.1.refs_3_.refs_1_.refs_2_, s32[2,40]{1,0:T(2,128)} %slice_convert_fusion.refs_4_.refs_3_, ...), custom_call_target="tpu_custom_call" | custom-call | tf_op jit(solution)/shard_map/metric_near/pallas_call | solution.py:245
  218.9 12.7 %collective-permute-done.19.refs_5_ = f32[3072,128]{1,0:T(8,128)} collective-permute-done((f32[3072,128]{1,0:T(8,128)}, f32[3072,128]{1,0:T(8,128)}, u32[]{:S(2)}, u32[]{:S(2)}) %collective-permute-start.19) | collective-permute-done | bytes 1572896 | tf_op jit(solution)/shard_map/ppermute | solution.py:17
  231.6 9.4 %metric_far0.1 = (f32[2,12,128,128]{3,2,1,0:T(8,128)}, f32[2,12,128,128]{3,2,1,0:T(8,128)}, f32[2,12,128,128]{3,2,1,0:T(8,128)}, f32[2,12,128,128]{3,2,1,0:T(8,128)}) custom-call(s32[2]{0:T(128)} %pad_add_fusion.1.meta.refs_0_, s32[4,24]{1,0:T(4,128)} %refs_1_.17, s32[2,40]{1,0:T(2,128)} %slice_convert_fusion.3.refs_2_.refs_0_, ...), custom_call_target="tpu_custom_call" | custom-call | tf_op jit(solution)/shard_map/metric_far0/pallas_call | solution.py:245
  241.0 24.2 %collective-permute-done.15.refs_5_ = f32[3072,128]{1,0:T(8,128)S(1)} collective-permute-done((f32[3072,128]{1,0:T(8,128)}, f32[3072,128]{1,0:T(8,128)S(1)}, u32[]{:S(2)}, u32[]{:S(2)}) %collective-permute-start.15) | collective-permute-done | bytes 1572896 | tf_op jit(solution)/shard_map/ppermute | solution.py:17
  265.2 1.1 copy-done.4
  266.9 7.0 %metric_far1.2 = (f32[2,12,128,128]{3,2,1,0:T(8,128)}, f32[2,12,128,128]{3,2,1,0:T(8,128)}) custom-call(s32[2]{0:T(128)} %pad_add_fusion.1.meta.refs_0_, s32[4,24]{1,0:T(4,128)} %refs_1_.17, s32[2,40]{1,0:T(2,128)} %slice_convert_fusion.3.refs_2_.refs_0_, s32[2,40]{1,0:T(2,128)} %slice_convert_fusion.2.refs_3_.refs_4_, ...), custom_call_target="tpu_custom_call" | custom-call | tf_op jit(solution)/shard_map/metric_far1/pallas_call | solution.py:245
  273.8 1.4 collective-permute-start.21
  275.2 7.0 %metric_far1.3 = (f32[2,12,128,128]{3,2,1,0:T(8,128)}, f32[2,12,128,128]{3,2,1,0:T(8,128)}) custom-call(s32[2]{0:T(128)} %pad_add_fusion.1.meta.refs_0_, s32[4,24]{1,0:T(4,128)} %refs_1_.17, s32[2,40]{1,0:T(2,128)} %slice_convert_fusion.3.refs_2_.refs_0_, s32[2,40]{1,0:T(2,128)} %slice_convert_fusion.2.refs_3_.refs_4_, ...), custom_call_target="tpu_custom_call" | custom-call | tf_op jit(solution)/shard_map/metric_far1/pallas_call | solution.py:245
  282.6 3.4 %collective-permute-done.22 = f32[2,12,128,128]{3,2,1,0:T(8,128)S(1)} collective-permute-done((f32[2,12,128,128]{3,2,1,0:T(8,128)}, f32[2,12,128,128]{3,2,1,0:T(8,128)S(1)}, u32[]{:S(2)}, u32[]{:S(2)}) %collective-permute-start.22) | collective-permute-done | bytes 1572896 | tf_op jit(solution)/shard_map/ppermute | solution.py:21
  286.1 2.0 pad_maximum_fusion.1
  (52 shorter events, 2.5 us)
Async XLA Ops:
  0.6 21.1 %collective-permute-start.3 = (f32[4,8,128,128]{3,2,1,0:T(8,128)}, f32[4,8,128,128]{3,2,1,0:T(8,128)}, u32[]{:S(2)}, u32[]{:S(2)}) collective-permute-start(f32[4,8,128,128]{3,2,1,0:T(8,128)} %table_a.1), channel_id=1, source_target_pairs={{0,1},{1,0},{2,3},{3,2},{4,5},{5,4},{6,7},{7,6},{8,9},{9,8},{10,11... | collective-permute-start | bytes 6291464 | tf_op jit(solution)/shard_map/ppermute | solution.py:21
  5.2 22.1 %copy-start.1 = (f32[1,16,128,128]{3,2,1,0:T(8,128)}, f32[1,16,128,128]{3,2,1,0:T(8,128)S(1)}, u32[]{:S(2)}) copy-start(f32[1,16,128,128]{3,2,1,0:T(8,128)S(1)} %get-tuple-element.76) | copy-start | bytes 3145732
  5.2 8.7 %copy-start.11 = (s32[4,8]{1,0:T(4,128)S(1)}, s32[4,8]{1,0:T(4,128)}, u32[]{:S(2)}) copy-start(s32[4,8]{1,0:T(4,128)} %cols_a.1) | copy-start | bytes 388
  5.3 22.0 %copy-start = (f32[2056,128]{1,0:T(8,128)}, f32[2056,128]{1,0:T(8,128)S(1)}, u32[]{:S(2)}) copy-start(f32[2056,128]{1,0:T(8,128)S(1)} %select_maximum_fusion.refs_6_.refs_9_) | copy-start | bytes 3158020
  5.3 32.2 %collective-permute-start = (f32[2056,128]{1,0:T(8,128)S(1)}, f32[2056,128]{1,0:T(8,128)S(1)}, u32[]{:S(2)}, u32[]{:S(2)}) collective-permute-start(f32[2056,128]{1,0:T(8,128)S(1)} %select_maximum_fusion.refs_6_.refs_9_), channel_id=1, source_target_pairs={{0,2},{2,4},{4,6},{6,8},{8,10},{10,12},{12,14},{14,16},{16,18},{18... | collective-permute-start | bytes 3158024 | tf_op jit(solution)/shard_map/ppermute | solution.py:17
  6.6 30.8 %collective-permute-start.1 = (f32[2056,128]{1,0:T(8,128)S(1)}, f32[2056,128]{1,0:T(8,128)}, u32[]{:S(2)}, u32[]{:S(2)}) collective-permute-start(f32[2056,128]{1,0:T(8,128)S(1)} %select_maximum_fusion.refs_6_.refs_9_), channel_id=1, source_target_pairs={{0,126},{2,0},{4,2},{6,4},{8,6},{10,8},{12,10},{14,12},{16,14},{18... | collective-permute-start | bytes 3158024 | tf_op jit(solution)/shard_map/ppermute | solution.py:17
  13.9 1.2 collective-permute-start.2
  14.2 45.8 %collective-permute-start.6 = (f32[2048,128]{1,0:T(8,128)S(1)}, f32[2048,128]{1,0:T(8,128)}, u32[]{:S(2)}, u32[]{:S(2)}) collective-permute-start(f32[2048,128]{1,0:T(8,128)S(1)} %bitcast.6), channel_id=1, source_target_pairs={{0,2},{2,4},{4,6},{6,8},{8,10},{10,12},{12,14},{14,16},{16,18},{18... | collective-permute-start | bytes 3145736 | tf_op jit(solution)/shard_map/ppermute | solution.py:17
  15.1 6.7 %copy-start.12 = (s32[4,8]{1,0:T(4,128)}, s32[4,8]{1,0:T(4,128)S(1)}, u32[]{:S(2)}) copy-start(s32[4,8]{1,0:T(4,128)S(1)} %collective-permute-done.2.cols_b) | copy-start | bytes 388
  15.1 44.9 %collective-permute-start.8 = (f32[2048,128]{1,0:T(8,128)S(1)}, f32[2048,128]{1,0:T(8,128)}, u32[]{:S(2)}, u32[]{:S(2)}) collective-permute-start(f32[2048,128]{1,0:T(8,128)S(1)} %bitcast.7), channel_id=1, source_target_pairs={{0,126},{2,0},{4,2},{6,4},{8,6},{10,8},{12,10},{14,12},{16,14},{18... | collective-permute-start | bytes 3145736 | tf_op jit(solution)/shard_map/ppermute | solution.py:17
  37.4 31.3 %copy-start.6 = (f32[2056,128]{1,0:T(8,128)}, f32[2056,128]{1,0:T(8,128)S(1)}, u32[]{:S(2)}) copy-start(f32[2056,128]{1,0:T(8,128)S(1)} %collective-permute-done.refs_8_.refs_7_) | copy-start | bytes 3158020
  37.4 44.6 %collective-permute-start.5 = (f32[2056,128]{1,0:T(8,128)}, f32[2056,128]{1,0:T(8,128)}, u32[]{:S(2)}, u32[]{:S(2)}) collective-permute-start(f32[2056,128]{1,0:T(8,128)} %collective-permute-done.1.refs_10_.refs_11_), channel_id=1, source_target_pairs={{0,126},{2,0},{4,2},{6,4},{8,6},{10,8},{12,10},{14,12},{16,14},{18... | collective-permute-start | bytes 3158024 | tf_op jit(solution)/shard_map/ppermute | solution.py:17
  44.3 39.0 %collective-permute-start.4 = (f32[2056,128]{1,0:T(8,128)S(1)}, f32[2056,128]{1,0:T(8,128)}, u32[]{:S(2)}, u32[]{:S(2)}) collective-permute-start(f32[2056,128]{1,0:T(8,128)S(1)} %collective-permute-done.refs_8_.refs_7_), channel_id=1, source_target_pairs={{0,2},{2,4},{4,6},{6,8},{8,10},{10,12},{12,14},{14,16},{16,18},{18... | collective-permute-start | bytes 3158024 | tf_op jit(solution)/shard_map/ppermute | solution.py:17
  60.0 44.9 %collective-permute-start.7 = (f32[2048,128]{1,0:T(8,128)}, f32[2048,128]{1,0:T(8,128)S(1)}, u32[]{:S(2)}, u32[]{:S(2)}) collective-permute-start(f32[2048,128]{1,0:T(8,128)} %collective-permute-done.6.refs_9_.refs_8_), channel_id=1, source_target_pairs={{0,2},{2,4},{4,6},{6,8},{8,10},{10,12},{12,14},{14,16},{16,18},{18... | collective-permute-start | bytes 3145736 | tf_op jit(solution)/shard_map/ppermute | solution.py:17
  60.0 44.9 %collective-permute-start.9 = (f32[2048,128]{1,0:T(8,128)}, f32[2048,128]{1,0:T(8,128)S(1)}, u32[]{:S(2)}, u32[]{:S(2)}) collective-permute-start(f32[2048,128]{1,0:T(8,128)} %collective-permute-done.8.refs_11_.refs_12_), channel_id=1, source_target_pairs={{0,126},{2,0},{4,2},{6,4},{8,6},{10,8},{12,10},{14,12},{16,14},{18... | collective-permute-start | bytes 3145736 | tf_op jit(solution)/shard_map/ppermute | solution.py:17
  104.9 1.0 copy-start.2
  104.9 1.3 copy-start.3
  112.7 7.4 %collective-permute-start.13 = (f32[1,24,128,128]{3,2,1,0:T(8,128)}, f32[1,24,128,128]{3,2,1,0:T(8,128)}, u32[]{:S(2)}, u32[]{:S(2)}) collective-permute-start(f32[1,24,128,128]{3,2,1,0:T(8,128)} %get-tuple-element.51), channel_id=1, source_target_pairs={{0,1},{1,0},{2,3},{3,2},{4,5},{5,4},{6,7},{7,6},{8,9},{9,8},{10,11... | collective-permute-start | bytes 4718600 | tf_op jit(solution)/shard_map/ppermute | solution.py:21
  113.4 6.7 %copy-start.8 = (f32[1,24,128,128]{3,2,1,0:T(8,128)S(1)}, f32[1,24,128,128]{3,2,1,0:T(8,128)}, u32[]{:S(2)}) copy-start(f32[1,24,128,128]{3,2,1,0:T(8,128)} %get-tuple-element.50) | copy-start | bytes 4718596
  120.0 9.9 %collective-permute-start.10 = (f32[1,24,128,128]{3,2,1,0:T(8,128)}, f32[1,24,128,128]{3,2,1,0:T(8,128)S(1)}, u32[]{:S(2)}, u32[]{:S(2)}) collective-permute-start(f32[1,24,128,128]{3,2,1,0:T(8,128)} %get-tuple-element.47), channel_id=1, source_target_pairs={{0,1},{1,0},{2,3},{3,2},{4,5},{5,4},{6,7},{7,6},{8,9},{9,8},{10,11... | collective-permute-start | bytes 4718600 | tf_op jit(solution)/shard_map/ppermute | solution.py:21
  120.1 9.8 %copy-start.7 = (f32[1,24,128,128]{3,2,1,0:T(8,128)S(1)}, f32[1,24,128,128]{3,2,1,0:T(8,128)}, u32[]{:S(2)}) copy-start(f32[1,24,128,128]{3,2,1,0:T(8,128)} %get-tuple-element.46) | copy-start | bytes 4718596
  123.0 41.2 %collective-permute-start.17 = (f32[3072,128]{1,0:T(8,128)}, f32[3072,128]{1,0:T(8,128)}, u32[]{:S(2)}, u32[]{:S(2)}) collective-permute-start(f32[3072,128]{1,0:T(8,128)} %bitcast.5.refs_4_), channel_id=1, source_target_pairs={{0,2},{2,4},{4,6},{6,8},{8,10},{10,12},{12,14},{14,16},{16,18},{18... | collective-permute-start | bytes 4718600 | tf_op jit(solution)/shard_map/ppermute | solution.py:17
  123.0 41.2 %collective-permute-start.18 = (f32[3072,128]{1,0:T(8,128)}, f32[3072,128]{1,0:T(8,128)}, u32[]{:S(2)}, u32[]{:S(2)}) collective-permute-start(f32[3072,128]{1,0:T(8,128)} %bitcast.5.refs_4_), channel_id=1, source_target_pairs={{0,126},{2,0},{4,2},{6,4},{8,6},{10,8},{12,10},{14,12},{16,14},{18... | collective-permute-start | bytes 4718600 | tf_op jit(solution)/shard_map/ppermute | solution.py:17
  132.7 38.3 %collective-permute-start.14 = (f32[2,12,128,128]{3,2,1,0:T(8,128)S(1)}, f32[2,12,128,128]{3,2,1,0:T(8,128)S(1)}, u32[]{:S(2)}, u32[]{:S(2)}) collective-permute-start(f32[2,12,128,128]{3,2,1,0:T(8,128)S(1)} %fusion), channel_id=1, source_target_pairs={{0,1},{1,0},{2,3},{3,2},{4,5},{5,4},{6,7},{7,6},{8,9},{9,8},{10,11... | collective-permute-start | bytes 4718600 | tf_op jit(solution)/shard_map/ppermute | solution.py:21
  133.9 64.0 %collective-permute-start.11 = (f32[3072,128]{1,0:T(8,128)}, f32[3072,128]{1,0:T(8,128)}, u32[]{:S(2)}, u32[]{:S(2)}) collective-permute-start(f32[3072,128]{1,0:T(8,128)} %bitcast.4.refs_5_), channel_id=1, source_target_pairs={{0,2},{2,4},{4,6},{6,8},{8,10},{10,12},{12,14},{14,16},{16,18},{18... | collective-permute-start | bytes 4718600 | tf_op jit(solution)/shard_map/ppermute | solution.py:17
  133.9 64.0 %collective-permute-start.12 = (f32[3072,128]{1,0:T(8,128)}, f32[3072,128]{1,0:T(8,128)}, u32[]{:S(2)}, u32[]{:S(2)}) collective-permute-start(f32[3072,128]{1,0:T(8,128)} %bitcast.4.refs_5_), channel_id=1, source_target_pairs={{0,126},{2,0},{4,2},{6,4},{8,6},{10,8},{12,10},{14,12},{16,14},{18... | collective-permute-start | bytes 4718600 | tf_op jit(solution)/shard_map/ppermute | solution.py:17
  164.2 67.4 %collective-permute-start.19 = (f32[3072,128]{1,0:T(8,128)}, f32[3072,128]{1,0:T(8,128)}, u32[]{:S(2)}, u32[]{:S(2)}) collective-permute-start(f32[3072,128]{1,0:T(8,128)} %collective-permute-done.17.refs_5_), channel_id=1, source_target_pairs={{0,2},{2,4},{4,6},{6,8},{8,10},{10,12},{12,14},{14,16},{16,18},{18... | collective-permute-start | bytes 4718600 | tf_op jit(solution)/shard_map/ppermute | solution.py:17
  164.2 67.4 %collective-permute-start.20 = (f32[3072,128]{1,0:T(8,128)}, f32[3072,128]{1,0:T(8,128)}, u32[]{:S(2)}, u32[]{:S(2)}) collective-permute-start(f32[3072,128]{1,0:T(8,128)} %collective-permute-done.18.refs_7_), channel_id=1, source_target_pairs={{0,126},{2,0},{4,2},{6,4},{8,6},{10,8},{12,10},{14,12},{16,14},{18... | collective-permute-start | bytes 4718600 | tf_op jit(solution)/shard_map/ppermute | solution.py:17
  197.9 67.3 %collective-permute-start.15 = (f32[3072,128]{1,0:T(8,128)}, f32[3072,128]{1,0:T(8,128)S(1)}, u32[]{:S(2)}, u32[]{:S(2)}) collective-permute-start(f32[3072,128]{1,0:T(8,128)} %collective-permute-done.11.refs_6_), channel_id=1, source_target_pairs={{0,2},{2,4},{4,6},{6,8},{8,10},{10,12},{12,14},{14,16},{16,18},{18... | collective-permute-start | bytes 4718600 | tf_op jit(solution)/shard_map/ppermute | solution.py:17
  197.9 67.3 %collective-permute-start.16 = (f32[3072,128]{1,0:T(8,128)}, f32[3072,128]{1,0:T(8,128)S(1)}, u32[]{:S(2)}, u32[]{:S(2)}) collective-permute-start(f32[3072,128]{1,0:T(8,128)} %collective-permute-done.12.refs_8_), channel_id=1, source_target_pairs={{0,126},{2,0},{4,2},{6,4},{8,6},{10,8},{12,10},{14,12},{16,14},{18... | collective-permute-start | bytes 4718600 | tf_op jit(solution)/shard_map/ppermute | solution.py:17
  265.2 1.1 copy-start.4
  265.2 1.7 copy-start.5
  273.8 8.5 %collective-permute-start.21 = (f32[2,12,128,128]{3,2,1,0:T(8,128)}, f32[2,12,128,128]{3,2,1,0:T(8,128)S(1)}, u32[]{:S(2)}, u32[]{:S(2)}) collective-permute-start(f32[2,12,128,128]{3,2,1,0:T(8,128)} %get-tuple-element.66), channel_id=1, source_target_pairs={{0,1},{1,0},{2,3},{3,2},{4,5},{5,4},{6,7},{7,6},{8,9},{9,8},{10,11... | collective-permute-start | bytes 4718600 | tf_op jit(solution)/shard_map/ppermute | solution.py:21
  275.2 7.2 %copy-start.9 = (f32[2,12,128,128]{3,2,1,0:T(8,128)S(1)}, f32[2,12,128,128]{3,2,1,0:T(8,128)}, u32[]{:S(2)}) copy-start(f32[2,12,128,128]{3,2,1,0:T(8,128)} %get-tuple-element.65) | copy-start | bytes 4718596
  282.3 3.7 %collective-permute-start.22 = (f32[2,12,128,128]{3,2,1,0:T(8,128)}, f32[2,12,128,128]{3,2,1,0:T(8,128)S(1)}, u32[]{:S(2)}, u32[]{:S(2)}) collective-permute-start(f32[2,12,128,128]{3,2,1,0:T(8,128)} %get-tuple-element.71), channel_id=1, source_target_pairs={{0,1},{1,0},{2,3},{3,2},{4,5},{5,4},{6,7},{7,6},{8,9},{9,8},{10,11... | collective-permute-start | bytes 4718600 | tf_op jit(solution)/shard_map/ppermute | solution.py:21
  282.4 3.6 %copy-start.10 = (f32[2,12,128,128]{3,2,1,0:T(8,128)S(1)}, f32[2,12,128,128]{3,2,1,0:T(8,128)}, u32[]{:S(2)}) copy-start(f32[2,12,128,128]{3,2,1,0:T(8,128)} %get-tuple-element.70) | copy-start | bytes 4718596

commit v4 on v3

--- a/solution.py
+++ b/solution.py
@@ -1,4 +1,5 @@
 import functools
+import math
 
 import jax
 import jax.numpy as jnp
@@ -114,14 +115,16 @@
     patterns = refs[2 : 2 + count]
     refs = refs[2 + count :]
     lefts, refs = refs[0], list(refs[1:])
+    direct = lefts.shape[0] != 5
     sources = [refs.pop(0) for _ in range(sum(pieces))]
     acc_sources = [refs.pop(0) for _ in range(2 if has_acc else 0)]
     results = [refs.pop(0) for _ in range(2 * portions)]
+    straight = portions == 2 or direct
     right_high, right_low, dense, left_held, sems = refs[:5]
     refs = refs[5:]
-    held = [refs.pop(0) for _ in sources]
-    acc = [refs.pop(0) for _ in acc_sources]
-    outs = refs
+    held = sources if direct else [refs.pop(0) for _ in sources]
+    acc = acc_sources if direct else [refs.pop(0) for _ in acc_sources]
+    outs = results if straight else refs
     copies = []
 
     def start(source, target):
@@ -129,13 +132,13 @@
         copies[-1].start()
         return copies[-1]
 
-    arriving = [start(source.at[pl.ds(0, target.shape[0])], target) for source, target in zip(sources, held)]
+    arriving = [None if direct else start(source.at[pl.ds(0, target.shape[0])], target) for source, target in zip(sources, held)]
     left_copies = []
     for gi, g in enumerate(gs):
         for ci, c in enumerate(crs):
             source = lefts.at[g + 2, c] if lefts.shape[0] == 5 else lefts.at[gi, 0]
             left_copies.append(start(source, left_held.at[gi, ci]))
-    acc_copies = [start(source, target) for source, target in zip(acc_sources, acc)]
+    acc_copies = [] if direct else [start(source, target) for source, target in zip(acc_sources, acc)]
     tables, held = [], list(zip(held, arriving))
     for number in pieces:
         tables.append([held.pop(0) for _ in range(number)])
@@ -150,7 +153,8 @@
         for ci, c in enumerate(crs):
             cols, first = patterns[gi], col0
             for table, copy in tables[gi * depth + ci]:
-                copy.wait()
+                if copy is not None:
+                    copy.wait()
 
                 def right_body(m, carry, gi=gi, ci=ci, c=c, cols=cols, table=table, first=first):
                     rel = wrap(cols[c, first + m] - base, total) - starts[gi]
@@ -215,7 +219,8 @@
                 return carry
 
             lax.fori_loop(0, kept_cols, out_body, 0, unroll=4)
-            leaving.append(start(own, results[portion].at[row % each]))
+            if not straight:
+                leaving.append(start(own, results[portion].at[row % each]))
     for copy in leaving:
         copy.wait()
 
@@ -241,29 +246,36 @@
     )
     shape = jax.ShapeDtypeStruct((out[0] // portions,) + out[1:], F32)
     blocks = [piece for table in tables for piece in table]
+    if part is not None:
+        blocks = [pltpu.with_memory_space_constraint(b, pltpu.VMEM) for b in blocks]
+        acc = [pltpu.with_memory_space_constraint(a, pltpu.VMEM) for a in acc]
+    straight = portions == 2 or part is not None
     window = max(counts)
+    wide = pltpu.VMEM((len(gs), window + 1, len(crs), 128, 128), BF16)
+    scratch = [
+        wide,
+        wide,
+        pltpu.VMEM((WINDOW, rows, 128, 128), F32),
+        pltpu.VMEM((len(gs), len(crs), rows, 128, 256), BF16),
+    ]
+    if part is None:
+        held = [pltpu.VMEM((b.shape[0] // 128 * 128, 128), F32) for b in blocks]
+        held += [pltpu.VMEM(a.shape, F32) for a in acc]
+    else:
+        held = []
+    if not straight:
+        held += [pltpu.VMEM(shape.shape, F32)] * (2 * portions)
+    used = sum(math.prod(ref.shape) * jnp.dtype(ref.dtype).itemsize for ref in scratch + held)
+    copies = len(blocks) + len(gs) * len(crs) + len(acc) + 2 * out[0]
     return pl.pallas_call(
         kernel,
         name=name,
-        out_shape=[shape] * (2 * portions),
-        in_specs=[SMEM] * (2 + len(gs)) + [HERE] * (1 + len(blocks) + len(acc)),
-        out_specs=[HERE] * (2 * portions),
-        scratch_shapes=[
-            pltpu.VMEM((len(gs), window + 1, len(crs), 128, 128), BF16),
-            pltpu.VMEM((len(gs), window + 1, len(crs), 128, 128), BF16),
-            pltpu.VMEM((WINDOW, rows, 128, 128), F32),
-            pltpu.VMEM((len(gs), len(crs), rows, 128, 256), BF16),
-            pltpu.SemaphoreType.DMA((len(blocks) + len(gs) * len(crs) + len(acc) + 2 * out[0],)),
-        ]
-        + [pltpu.VMEM((b.shape[0] // 128 * 128, 128), F32) for b in blocks]
-        + [pltpu.VMEM(a.shape, F32) for a in acc]
-        + [pltpu.VMEM(shape.shape, F32)] * (2 * portions),
-        compiler_params=PARAMS,
-        cost_estimate=pl.CostEstimate(
-            flops=0,
-            transcendentals=0,
-            bytes_accessed=0,
-        ),
+        out_shape=[pltpu.VMEM(shape.shape, F32) if straight else shape] * (2 * portions),
+        in_specs=[SMEM] * (2 + len(gs)) + [HERE] + [HERE if part is None else VMEM] * (len(blocks) + len(acc)),
+        out_specs=[VMEM if straight else HERE] * (2 * portions),
+        scratch_shapes=scratch + [pltpu.SemaphoreType.DMA((copies,))] + held,
+        compiler_params=pltpu.CompilerParams(vmem_limit_bytes=used + (6 << 20)),
+        cost_estimate=pl.CostEstimate(flops=0, transcendentals=0, bytes_accessed=0),
     )(
         meta, outcols, *[patterns[g] for g in gs], left[0 if part is None else 1 + part], *blocks, *acc
     )

time: 289 us -> 276 us (0.955)
  Pallas kernels: 99.6 us -> 79.5 us
  waiting for transfers between devices: 103 us -> 113 us
  other arithmetic: 18.9 us -> 12.9 us
  local copies, waits for them, and re-layouts: 4.7 us -> 8.3 us
    pallas_call x9, Pallas kernels: 82.7 us -> 62.5 us  [stage(): pl.pallas_call(kernel, name=name, out_shape=[pltpu.VMEM(shape.shape, F32)...]
    ppermute x16, waiting for transfers between devices: 98.6 us -> 109 us  [ring(): lax.ppermute(array, 'rows', [(i, (i + by) % devices) for i in range(devic...]
    convert_element_type x4, other arithmetic: 4.32 us -> 0.68 us  [shards(): factors[g][0][0][slots * 128:slots * 128 + 2, :pattern.shape[1]]]
    unnamed x26 -> x72, local copies, waits for them, and re-layouts: 3.02 us -> 6.62 us
  transfers between devices with their start and end apart: 23 -> 23, of which waited for: 9 -> 11; matrix products, arithmetic and copies ran while one was open for 6% -> 4% of each run, Pallas kernels for 30% -> 26%
where the time goes in v4:
time: 276 us
  waiting for transfers between devices  113 us (41%)
  Pallas kernels  79.5 us (29%)
  starting transfers between devices  61.1 us (22%)
  other arithmetic  12.9 us (5%)
  local copies, waits for them, and re-layouts  8.3 us (3%)
    ppermute x16, waiting for transfers between devices, ring(): lax.ppermute(array, 'rows', [(i, (i + by) % devices) for i in range(devic...  109 us
    pallas_call x9, Pallas kernels, stage(): pl.pallas_call(kernel, name=name, out_shape=[pltpu.VMEM(shape.shape, F32)...  62.5 us
    ppermute x16, starting transfers between devices, ring(): lax.ppermute(array, 'rows', [(i, (i + by) % devices) for i in range(devic...  56.2 us
    pallas_call x2, Pallas kernels, left_call(): pl.pallas_call(kernel, name=name, out_shape=[out, last, last], in_specs=[...  17 us
    unnamed x72, local copies, waits for them, and re-layouts  6.62 us
  transfers between devices with their start and end apart: 23, of which 11 were waited for; matrix products, arithmetic and copies ran while one was open for 4% of the time, Pallas kernels for 26%

profile of v4, /device:TPU:1, one launch (start us, length us, event | category | flops | bytes accessed | tf_op | source)
XLA Modules:
  0.0 275.9 jit_solution(5231247430185077266)
XLA Ops:
  0.6 1.5 collective-permute-start.3
  2.1 0.8 pad_add_fusion
  2.9 1.7 constant_dynamic-slice_fusion
  4.7 1.4 collective-permute-start
  6.1 7.3 %collective-permute-start.1 = (f32[2056,128]{1,0:T(8,128)S(1)}, f32[2056,128]{1,0:T(8,128)}, u32[]{:S(2)}, u32[]{:S(2)}) collective-permute-start(f32[2056,128]{1,0:T(8,128)S(1)} %select_maximum_fusion.refs_6_.refs_9_), channel_id=1, source_target_pairs={{0,126},{2,0},{4,2},{6,4},{8,6},{10,8},{12,10},{14,12},{16,14},{18... | collective-permute-start | bytes 3158024 | tf_op jit(solution)/shard_map/ppermute | solution.py:18
  13.7 0.8 collective-permute-done.2.cols_b
  14.5 6.0 %collective-permute-start.8 = (f32[2048,128]{1,0:T(8,128)S(1)}, f32[2048,128]{1,0:T(8,128)}, u32[]{:S(2)}, u32[]{:S(2)}) collective-permute-start(f32[2048,128]{1,0:T(8,128)S(1)} %bitcast.13), channel_id=1, source_target_pairs={{0,126},{2,0},{4,2},{6,4},{8,6},{10,8},{12,10},{14,12},{16,14},{18... | collective-permute-start | bytes 3145736 | tf_op jit(solution)/shard_map/ppermute | solution.py:18
  21.2 5.5 %margin_left.1 = (bf16[5,2,4,128,256]{4,3,2,1,0:T(8,128)(2,1)}, bf16[2,1,2,128,256]{4,3,2,1,0:T(8,128)(2,1)}, bf16[2,1,2,128,256]{4,3,2,1,0:T(8,128)(2,1)}) custom-call(s32[2]{0:T(128)} %pad_add_fusion.1.meta.refs_0_, s32[4,8]{1,0:T(4,128)} %cols_a.1, s32[4,8]{1,0:T(4,128)} %copy-done.35, f32[4,8,128,128]{3,2,1,0:T(8,128)} %table_a.1, ...), custom_call_target="tpu_custom_call" | custom-call | tf_op jit(solution)/shard_map/margin_left/pallas_call | solution.py:287
  26.7 10.2 %collective-permute-done.refs_8_.refs_7_ = f32[2056,128]{1,0:T(8,128)S(1)} collective-permute-done((f32[2056,128]{1,0:T(8,128)S(1)}, f32[2056,128]{1,0:T(8,128)S(1)}, u32[]{:S(2)}, u32[]{:S(2)}) %collective-permute-start) | collective-permute-done | bytes 1052704 | tf_op jit(solution)/shard_map/ppermute | solution.py:18
  36.9 6.9 %collective-permute-start.5 = (f32[2056,128]{1,0:T(8,128)}, f32[2056,128]{1,0:T(8,128)S(1)}, u32[]{:S(2)}, u32[]{:S(2)}) collective-permute-start(f32[2056,128]{1,0:T(8,128)} %collective-permute-done.1.refs_10_.refs_11_), channel_id=1, source_target_pairs={{0,126},{2,0},{4,2},{6,4},{8,6},{10,8},{12,10},{14,12},{16,14},{18... | collective-permute-start | bytes 3158024 | tf_op jit(solution)/shard_map/ppermute | solution.py:18
  43.7 15.7 %collective-permute-done.6.refs_9_.refs_8_ = f32[2048,128]{1,0:T(8,128)} collective-permute-done((f32[2048,128]{1,0:T(8,128)S(1)}, f32[2048,128]{1,0:T(8,128)}, u32[]{:S(2)}, u32[]{:S(2)}) %collective-permute-start.6) | collective-permute-done | bytes 1048608 | tf_op jit(solution)/shard_map/ppermute | solution.py:18
  59.5 6.9 %collective-permute-start.9 = (f32[2048,128]{1,0:T(8,128)}, f32[2048,128]{1,0:T(8,128)S(1)}, u32[]{:S(2)}, u32[]{:S(2)}) collective-permute-start(f32[2048,128]{1,0:T(8,128)} %collective-permute-done.8.refs_11_.refs_12_), channel_id=1, source_target_pairs={{0,126},{2,0},{4,2},{6,4},{8,6},{10,8},{12,10},{14,12},{16,14},{18... | collective-permute-start | bytes 3145736 | tf_op jit(solution)/shard_map/ppermute | solution.py:18
  66.3 0.7 slice_convert_fusion.refs_4_.refs_3_
  67.1 1.7 copy-done.2
  68.8 10.5 %product_near.1 = (f32[2,24,128,128]{3,2,1,0:T(8,128)S(1)}, f32[2,24,128,128]{3,2,1,0:T(8,128)S(1)}) custom-call(s32[2]{0:T(128)S(1)} %copy-done.24, s32[4,24]{1,0:T(4,128)S(1)} %copy-done.26, s32[2,40]{1,0:T(2,128)S(1)} %get-tuple-element.73.refs_2_, s32[2,40]{1,0:T(2,128)S(1)} %slice_convert_fusion.1.refs_3_.refs_1_.refs_2_, ...), custom_call_target="tpu_custom_call" | custom-call | tf_op jit(solution)/shard_map/product_near/pallas_call | solution.py:270
  79.3 1.8 collective-permute-done.5.refs_6_.refs_13_
  81.2 0.7 collective-permute-done.4.refs_5_
  81.9 6.1 %product_far0.1 = (f32[1,24,128,128]{3,2,1,0:T(8,128)S(1)}, f32[1,24,128,128]{3,2,1,0:T(8,128)S(1)}, f32[1,24,128,128]{3,2,1,0:T(8,128)S(1)}, f32[1,24,128,128]{3,2,1,0:T(8,128)S(1)}) custom-call(s32[2]{0:T(128)S(1)} %copy-done.24, s32[4,24]{1,0:T(4,128)S(1)} %copy-done.26, s32[2,40]{1,0:T(2,128)S(1)} %slice_convert_fusion.3.refs_2_.refs_0_, ...), custom_call_target="tpu_custom_call" | custom-call | tf_op jit(solution)/shard_map/product_far0/pallas_call | solution.py:270
  88.1 16.3 %collective-permute-done.7.refs_5_.refs_6_ = f32[2048,128]{1,0:T(8,128)S(1)} collective-permute-done((f32[2048,128]{1,0:T(8,128)}, f32[2048,128]{1,0:T(8,128)S(1)}, u32[]{:S(2)}, u32[]{:S(2)}) %collective-permute-start.7) | collective-permute-done | bytes 1048608 | tf_op jit(solution)/shard_map/ppermute | solution.py:18
  104.4 4.1 %product_far1.3 = (f32[1,24,128,128]{3,2,1,0:T(8,128)S(1)}, f32[1,24,128,128]{3,2,1,0:T(8,128)S(1)}) custom-call(s32[2]{0:T(128)S(1)} %copy-done.24, s32[4,24]{1,0:T(4,128)S(1)} %copy-done.26, s32[2,40]{1,0:T(2,128)S(1)} %slice_convert_fusion.3.refs_2_.refs_0_, s32[2,40]{1,0:T(2,128)S(1)} %slice_convert_fusion.2.refs_3_.refs_4_, ...), custom_call_target="tpu_custom_call" | custom-call | tf_op jit(solution)/shard_map/product_far1/pallas_call | solution.py:270
  108.5 0.7 collective-permute-start.13
  109.2 5.3 %product_far1.2 = (f32[1,24,128,128]{3,2,1,0:T(8,128)S(1)}, f32[1,24,128,128]{3,2,1,0:T(8,128)}) custom-call(s32[2]{0:T(128)S(1)} %copy-done.24, s32[4,24]{1,0:T(4,128)S(1)} %copy-done.26, s32[2,40]{1,0:T(2,128)S(1)} %slice_convert_fusion.3.refs_2_.refs_0_, s32[2,40]{1,0:T(2,128)S(1)} %slice_convert_fusion.2.refs_3_.refs_4_, ...), custom_call_target="tpu_custom_call" | custom-call | tf_op jit(solution)/shard_map/product_far1/pallas_call | solution.py:270
  114.6 1.1 copy-done.14
  115.7 1.7 add.37
  117.5 7.0 %collective-permute-start.18 = (f32[3072,128]{1,0:T(8,128)S(1)}, f32[3072,128]{1,0:T(8,128)}, u32[]{:S(2)}, u32[]{:S(2)}) collective-permute-start(f32[3072,128]{1,0:T(8,128)S(1)} %bitcast.7), channel_id=1, source_target_pairs={{0,126},{2,0},{4,2},{6,4},{8,6},{10,8},{12,10},{14,12},{16,14},{18... | collective-permute-start | bytes 4718600 | tf_op jit(solution)/shard_map/ppermute | solution.py:18
  124.5 1.6 add.36
  126.2 1.3 fusion
  127.4 0.9 collective-permute-start.14
  128.3 6.9 %collective-permute-start.12 = (f32[3072,128]{1,0:T(8,128)S(1)}, f32[3072,128]{1,0:T(8,128)}, u32[]{:S(2)}, u32[]{:S(2)}) collective-permute-start(f32[3072,128]{1,0:T(8,128)S(1)} %bitcast.10), channel_id=1, source_target_pairs={{0,126},{2,0},{4,2},{6,4},{8,6},{10,8},{12,10},{14,12},{16,14},{18... | collective-permute-start | bytes 4718600 | tf_op jit(solution)/shard_map/ppermute | solution.py:18
  135.2 11.4 %factor_left.1 = (bf16[5,2,4,128,256]{4,3,2,1,0:T(8,128)(2,1)}, bf16[2,1,2,128,256]{4,3,2,1,0:T(8,128)(2,1)}, bf16[2,1,2,128,256]{4,3,2,1,0:T(8,128)(2,1)}) custom-call(s32[2]{0:T(128)} %pad_add_fusion.1.meta.refs_0_, s32[2,40]{1,0:T(2,128)} %copy-done.22, s32[2,40]{1,0:T(2,128)} %copy-done.32, s32[2,40]{1,0:T(2,128)} %copy-done.28, s32[2,40]{1,0:T(2,128)} %copy-done.30, ...), custom_call_target="tpu_custom_call" | custom-call | tf_op jit(solution)/shard_map/factor_left/pallas_call | solution.py:287
  146.7 1.7 copy-done
  148.4 7.6 %metric_own.1 = (f32[4,12,128,128]{3,2,1,0:T(8,128)S(1)}, f32[4,12,128,128]{3,2,1,0:T(8,128)S(1)}) custom-call(s32[2]{0:T(128)S(1)} %copy-done.25, s32[4,24]{1,0:T(4,128)S(1)} %copy-done.27, s32[2,40]{1,0:T(2,128)S(1)} %copy-done.29, bf16[5,2,4,128,256]{4,3,2,1,0:T(8,128)(2,1)S(1)} %copy-done, f32[3072,128]{1,0:T(8,128)S(1)} %bitcast.8, f32[3072,128]{1,0:T(8,128)S(1)} %bitcast.11), custom_call_target="tpu_custom_call" | custom-call | tf_op jit(solution)/shard_map/metric_own/pallas_call | solution.py:270
  156.0 2.7 collective-permute-done.17.refs_5_
  158.7 6.9 %collective-permute-start.20 = (f32[3072,128]{1,0:T(8,128)}, f32[3072,128]{1,0:T(8,128)}, u32[]{:S(2)}, u32[]{:S(2)}) collective-permute-start(f32[3072,128]{1,0:T(8,128)} %collective-permute-done.18.refs_7_), channel_id=1, source_target_pairs={{0,126},{2,0},{4,2},{6,4},{8,6},{10,8},{12,10},{14,12},{16,14},{18... | collective-permute-start | bytes 4718600 | tf_op jit(solution)/shard_map/ppermute | solution.py:18
  165.6 1.7 broadcast_select_fusion.1
  167.3 2.0 pad_maximum_fusion
  169.4 23.0 %collective-permute-done.11.refs_6_ = f32[3072,128]{1,0:T(8,128)} collective-permute-done((f32[3072,128]{1,0:T(8,128)S(1)}, f32[3072,128]{1,0:T(8,128)}, u32[]{:S(2)}, u32[]{:S(2)}) %collective-permute-start.11) | collective-permute-done | bytes 1572896 | tf_op jit(solution)/shard_map/ppermute | solution.py:18
  192.4 6.9 %collective-permute-start.16 = (f32[3072,128]{1,0:T(8,128)}, f32[3072,128]{1,0:T(8,128)S(1)}, u32[]{:S(2)}, u32[]{:S(2)}) collective-permute-start(f32[3072,128]{1,0:T(8,128)} %collective-permute-done.12.refs_8_), channel_id=1, source_target_pairs={{0,126},{2,0},{4,2},{6,4},{8,6},{10,8},{12,10},{14,12},{16,14},{18... | collective-permute-start | bytes 4718600 | tf_op jit(solution)/shard_map/ppermute | solution.py:18
  199.3 12.9 %metric_near.1 = (f32[4,12,128,128]{3,2,1,0:T(8,128)S(1)}, f32[4,12,128,128]{3,2,1,0:T(8,128)}) custom-call(s32[2]{0:T(128)S(1)} %copy-done.25, s32[4,24]{1,0:T(4,128)S(1)} %copy-done.27, s32[2,40]{1,0:T(2,128)S(1)} %copy-done.33, s32[2,40]{1,0:T(2,128)S(1)} %copy-done.31, bf16[5,2,4,128,256]{4,3,2,1,0:T(8,128)(2,1)S(1)} %copy-done.1, ...), custom_call_target="tpu_custom_call" | custom-call | tf_op jit(solution)/shard_map/metric_near/pallas_call | solution.py:270
  212.2 13.8 %collective-permute-done.19.refs_5_ = f32[3072,128]{1,0:T(8,128)S(1)} collective-permute-done((f32[3072,128]{1,0:T(8,128)}, f32[3072,128]{1,0:T(8,128)S(1)}, u32[]{:S(2)}, u32[]{:S(2)}) %collective-permute-start.19) | collective-permute-done | bytes 1572896 | tf_op jit(solution)/shard_map/ppermute | solution.py:18
  226.0 1.9 copy-done.13
  227.9 7.0 %metric_far0.1 = (f32[2,12,128,128]{3,2,1,0:T(8,128)S(1)}, f32[2,12,128,128]{3,2,1,0:T(8,128)S(1)}, f32[2,12,128,128]{3,2,1,0:T(8,128)S(1)}, f32[2,12,128,128]{3,2,1,0:T(8,128)S(1)}) custom-call(s32[2]{0:T(128)S(1)} %copy-done.25, s32[4,24]{1,0:T(4,128)S(1)} %copy-done.27, s32[2,40]{1,0:T(2,128)S(1)} %copy-done.23, s32[2,40]{1,0:T(2,128)S(1)} %copy-done.21, ...), custom_call_target="tpu_custom_call" | custom-call | tf_op jit(solution)/shard_map/metric_far0/pallas_call | solution.py:270
  234.9 24.8 %collective-permute-done.15.refs_5_ = f32[3072,128]{1,0:T(8,128)S(1)} collective-permute-done((f32[3072,128]{1,0:T(8,128)}, f32[3072,128]{1,0:T(8,128)S(1)}, u32[]{:S(2)}, u32[]{:S(2)}) %collective-permute-start.15) | collective-permute-done | bytes 1572896 | tf_op jit(solution)/shard_map/ppermute | solution.py:18
  259.7 4.5 %metric_far1.2 = (f32[2,12,128,128]{3,2,1,0:T(8,128)S(1)}, f32[2,12,128,128]{3,2,1,0:T(8,128)S(1)}) custom-call(s32[2]{0:T(128)S(1)} %copy-done.25, s32[4,24]{1,0:T(4,128)S(1)} %copy-done.27, s32[2,40]{1,0:T(2,128)S(1)} %copy-done.23, s32[2,40]{1,0:T(2,128)S(1)} %copy-done.21, bf16[2,1,2,128,256]{4,3,2,1,0:T(8,128)(2,1)S(1)} %copy-done.17, ...), custom_call_target="tpu_custom_call" | custom-call | tf_op jit(solution)/shard_map/metric_far1/pallas_call | solution.py:270
  264.2 1.3 collective-permute-start.21
  265.6 4.6 %metric_far1.3 = (f32[2,12,128,128]{3,2,1,0:T(8,128)S(1)}, f32[2,12,128,128]{3,2,1,0:T(8,128)S(1)}) custom-call(s32[2]{0:T(128)S(1)} %copy-done.25, s32[4,24]{1,0:T(4,128)S(1)} %copy-done.27, s32[2,40]{1,0:T(2,128)S(1)} %copy-done.23, s32[2,40]{1,0:T(2,128)S(1)} %copy-done.21, bf16[2,1,2,128,256]{4,3,2,1,0:T(8,128)(2,1)S(1)} %copy-done.16, ...), custom_call_target="tpu_custom_call" | custom-call | tf_op jit(solution)/shard_map/metric_far1/pallas_call | solution.py:270
  270.5 3.2 %collective-permute-done.22 = f32[2,12,128,128]{3,2,1,0:T(8,128)S(1)} collective-permute-done((f32[2,12,128,128]{3,2,1,0:T(8,128)S(1)}, f32[2,12,128,128]{3,2,1,0:T(8,128)S(1)}, u32[]{:S(2)}, u32[]{:S(2)}) %collective-permute-start.22) | collective-permute-done | bytes 1572896 | tf_op jit(solution)/shard_map/ppermute | solution.py:22
  273.9 2.0 pad_maximum_fusion.1
  (98 shorter events, 1.8 us)
Async XLA Ops:
  0.6 20.5 %collective-permute-start.3 = (f32[4,8,128,128]{3,2,1,0:T(8,128)}, f32[4,8,128,128]{3,2,1,0:T(8,128)}, u32[]{:S(2)}, u32[]{:S(2)}) collective-permute-start(f32[4,8,128,128]{3,2,1,0:T(8,128)} %table_a.1), channel_id=1, source_target_pairs={{0,1},{1,0},{2,3},{3,2},{4,5},{5,4},{6,7},{7,6},{8,9},{9,8},{10,11... | collective-permute-start | bytes 6291464 | tf_op jit(solution)/shard_map/ppermute | solution.py:22
  2.9 64.1 %copy-start.28 = (s32[2,40]{1,0:T(2,128)}, s32[2,40]{1,0:T(2,128)S(1)}, u32[]{:S(2)}) copy-start(s32[2,40]{1,0:T(2,128)S(1)} %get-tuple-element.73.refs_2_) | copy-start | bytes 964
  4.6 62.4 %copy-start.5 = (f32[1,16,128,128]{3,2,1,0:T(8,128)}, f32[1,16,128,128]{3,2,1,0:T(8,128)S(1)}, u32[]{:S(2)}) copy-start(f32[1,16,128,128]{3,2,1,0:T(8,128)S(1)} %get-tuple-element.76) | copy-start | bytes 3145732
  4.6 8.7 %copy-start.34 = (s32[4,8]{1,0:T(4,128)S(1)}, s32[4,8]{1,0:T(4,128)}, u32[]{:S(2)}) copy-start(s32[4,8]{1,0:T(4,128)} %cols_a.1) | copy-start | bytes 388
  4.7 62.3 %copy-start.4 = (f32[2056,128]{1,0:T(8,128)}, f32[2056,128]{1,0:T(8,128)S(1)}, u32[]{:S(2)}) copy-start(f32[2056,128]{1,0:T(8,128)S(1)} %select_maximum_fusion.refs_6_.refs_9_) | copy-start | bytes 3158020
  4.7 32.2 %collective-permute-start = (f32[2056,128]{1,0:T(8,128)S(1)}, f32[2056,128]{1,0:T(8,128)S(1)}, u32[]{:S(2)}, u32[]{:S(2)}) collective-permute-start(f32[2056,128]{1,0:T(8,128)S(1)} %select_maximum_fusion.refs_6_.refs_9_), channel_id=1, source_target_pairs={{0,2},{2,4},{4,6},{6,8},{8,10},{10,12},{12,14},{14,16},{16,18},{18... | collective-permute-start | bytes 3158024 | tf_op jit(solution)/shard_map/ppermute | solution.py:18
  6.1 30.8 %collective-permute-start.1 = (f32[2056,128]{1,0:T(8,128)S(1)}, f32[2056,128]{1,0:T(8,128)}, u32[]{:S(2)}, u32[]{:S(2)}) collective-permute-start(f32[2056,128]{1,0:T(8,128)S(1)} %select_maximum_fusion.refs_6_.refs_9_), channel_id=1, source_target_pairs={{0,126},{2,0},{4,2},{6,4},{8,6},{10,8},{12,10},{14,12},{16,14},{18... | collective-permute-start | bytes 3158024 | tf_op jit(solution)/shard_map/ppermute | solution.py:18
  13.4 1.2 collective-permute-start.2
  13.7 45.8 %collective-permute-start.6 = (f32[2048,128]{1,0:T(8,128)S(1)}, f32[2048,128]{1,0:T(8,128)}, u32[]{:S(2)}, u32[]{:S(2)}) collective-permute-start(f32[2048,128]{1,0:T(8,128)S(1)} %bitcast.12), channel_id=1, source_target_pairs={{0,2},{2,4},{4,6},{6,8},{8,10},{10,12},{12,14},{14,16},{16,18},{18... | collective-permute-start | bytes 3145736 | tf_op jit(solution)/shard_map/ppermute | solution.py:18
  14.5 44.9 %collective-permute-start.8 = (f32[2048,128]{1,0:T(8,128)S(1)}, f32[2048,128]{1,0:T(8,128)}, u32[]{:S(2)}, u32[]{:S(2)}) collective-permute-start(f32[2048,128]{1,0:T(8,128)S(1)} %bitcast.13), channel_id=1, source_target_pairs={{0,126},{2,0},{4,2},{6,4},{8,6},{10,8},{12,10},{14,12},{16,14},{18... | collective-permute-start | bytes 3145736 | tf_op jit(solution)/shard_map/ppermute | solution.py:18
  21.1 45.9 %copy-start.24 = (s32[2]{0:T(128)S(1)}, s32[2]{0:T(128)}, u32[]{:S(2)}) copy-start(s32[2]{0:T(128)} %pad_add_fusion.1.meta.refs_0_) | copy-start | bytes 28
  21.1 45.9 %copy-start.26 = (s32[4,24]{1,0:T(4,128)S(1)}, s32[4,24]{1,0:T(4,128)}, u32[]{:S(2)}) copy-start(s32[4,24]{1,0:T(4,128)} %refs_1_.12) | copy-start | bytes 1156
  36.9 42.4 %copy-start.8 = (f32[2056,128]{1,0:T(8,128)}, f32[2056,128]{1,0:T(8,128)S(1)}, u32[]{:S(2)}) copy-start(f32[2056,128]{1,0:T(8,128)S(1)} %collective-permute-done.refs_8_.refs_7_) | copy-start | bytes 3158020
  36.9 44.3 %collective-permute-start.5 = (f32[2056,128]{1,0:T(8,128)}, f32[2056,128]{1,0:T(8,128)S(1)}, u32[]{:S(2)}, u32[]{:S(2)}) collective-permute-start(f32[2056,128]{1,0:T(8,128)} %collective-permute-done.1.refs_10_.refs_11_), channel_id=1, source_target_pairs={{0,126},{2,0},{4,2},{6,4},{8,6},{10,8},{12,10},{14,12},{16,14},{18... | collective-permute-start | bytes 3158024 | tf_op jit(solution)/shard_map/ppermute | solution.py:18
  43.7 38.2 %collective-permute-start.4 = (f32[2056,128]{1,0:T(8,128)S(1)}, f32[2056,128]{1,0:T(8,128)S(1)}, u32[]{:S(2)}, u32[]{:S(2)}) collective-permute-start(f32[2056,128]{1,0:T(8,128)S(1)} %collective-permute-done.refs_8_.refs_7_), channel_id=1, source_target_pairs={{0,2},{2,4},{4,6},{6,8},{8,10},{10,12},{12,14},{14,16},{16,18},{18... | collective-permute-start | bytes 3158024 | tf_op jit(solution)/shard_map/ppermute | solution.py:18
  59.4 44.9 %collective-permute-start.7 = (f32[2048,128]{1,0:T(8,128)}, f32[2048,128]{1,0:T(8,128)S(1)}, u32[]{:S(2)}, u32[]{:S(2)}) collective-permute-start(f32[2048,128]{1,0:T(8,128)} %collective-permute-done.6.refs_9_.refs_8_), channel_id=1, source_target_pairs={{0,2},{2,4},{4,6},{6,8},{8,10},{10,12},{12,14},{14,16},{16,18},{18... | collective-permute-start | bytes 3145736 | tf_op jit(solution)/shard_map/ppermute | solution.py:18
  59.5 44.9 %collective-permute-start.9 = (f32[2048,128]{1,0:T(8,128)}, f32[2048,128]{1,0:T(8,128)S(1)}, u32[]{:S(2)}, u32[]{:S(2)}) collective-permute-start(f32[2048,128]{1,0:T(8,128)} %collective-permute-done.8.refs_11_.refs_12_), channel_id=1, source_target_pairs={{0,126},{2,0},{4,2},{6,4},{8,6},{10,8},{12,10},{14,12},{16,14},{18... | collective-permute-start | bytes 3145736 | tf_op jit(solution)/shard_map/ppermute | solution.py:18
  67.0 12.3 %copy-start.30 = (s32[2,40]{1,0:T(2,128)}, s32[2,40]{1,0:T(2,128)S(1)}, u32[]{:S(2)}) copy-start(s32[2,40]{1,0:T(2,128)S(1)} %slice_convert_fusion.refs_4_.refs_3_) | copy-start | bytes 964
  67.0 12.3 %copy-start.32 = (s32[2,40]{1,0:T(2,128)}, s32[2,40]{1,0:T(2,128)S(1)}, u32[]{:S(2)}) copy-start(s32[2,40]{1,0:T(2,128)S(1)} %slice_convert_fusion.1.refs_3_.refs_1_.refs_2_) | copy-start | bytes 964
  68.8 13.1 %copy-start.3 = (bf16[5,2,4,128,256]{4,3,2,1,0:T(8,128)(2,1)S(1)}, bf16[5,2,4,128,256]{4,3,2,1,0:T(8,128)(2,1)}, u32[]{:S(2)}) copy-start(bf16[5,2,4,128,256]{4,3,2,1,0:T(8,128)(2,1)} %get-tuple-element.37.refs_5_.refs_4_) | copy-start | bytes 7864324
  81.2 28.1 %copy-start.20 = (s32[2,40]{1,0:T(2,128)}, s32[2,40]{1,0:T(2,128)S(1)}, u32[]{:S(2)}) copy-start(s32[2,40]{1,0:T(2,128)S(1)} %slice_convert_fusion.2.refs_3_.refs_4_) | copy-start | bytes 964
  81.9 27.3 %copy-start.22 = (s32[2,40]{1,0:T(2,128)}, s32[2,40]{1,0:T(2,128)S(1)}, u32[]{:S(2)}) copy-start(s32[2,40]{1,0:T(2,128)S(1)} %slice_convert_fusion.3.refs_2_.refs_0_) | copy-start | bytes 964
  81.9 22.5 %copy-start.19 = (bf16[2,1,2,128,256]{4,3,2,1,0:T(8,128)(2,1)S(1)}, bf16[2,1,2,128,256]{4,3,2,1,0:T(8,128)(2,1)}, u32[]{:S(2)}) copy-start(bf16[2,1,2,128,256]{4,3,2,1,0:T(8,128)(2,1)} %get-tuple-element.38.refs_4_) | copy-start | bytes 786436
  108.5 7.2 %collective-permute-start.13 = (f32[1,24,128,128]{3,2,1,0:T(8,128)S(1)}, f32[1,24,128,128]{3,2,1,0:T(8,128)}, u32[]{:S(2)}, u32[]{:S(2)}) collective-permute-start(f32[1,24,128,128]{3,2,1,0:T(8,128)S(1)} %get-tuple-element.51), channel_id=1, source_target_pairs={{0,1},{1,0},{2,3},{3,2},{4,5},{5,4},{6,7},{7,6},{8,9},{9,8},{10,11... | collective-permute-start | bytes 4718600 | tf_op jit(solution)/shard_map/ppermute | solution.py:22
  115.7 8.9 %collective-permute-start.10 = (f32[1,24,128,128]{3,2,1,0:T(8,128)}, f32[1,24,128,128]{3,2,1,0:T(8,128)}, u32[]{:S(2)}, u32[]{:S(2)}) collective-permute-start(f32[1,24,128,128]{3,2,1,0:T(8,128)} %get-tuple-element.47), channel_id=1, source_target_pairs={{0,1},{1,0},{2,3},{3,2},{4,5},{5,4},{6,7},{7,6},{8,9},{9,8},{10,11... | collective-permute-start | bytes 4718600 | tf_op jit(solution)/shard_map/ppermute | solution.py:22
  115.7 8.8 %copy-start.15 = (f32[1,24,128,128]{3,2,1,0:T(8,128)S(1)}, f32[1,24,128,128]{3,2,1,0:T(8,128)}, u32[]{:S(2)}) copy-start(f32[1,24,128,128]{3,2,1,0:T(8,128)} %copy-done.14) | copy-start | bytes 4718596
  117.4 41.2 %collective-permute-start.17 = (f32[3072,128]{1,0:T(8,128)S(1)}, f32[3072,128]{1,0:T(8,128)}, u32[]{:S(2)}, u32[]{:S(2)}) collective-permute-start(f32[3072,128]{1,0:T(8,128)S(1)} %bitcast.6), channel_id=1, source_target_pairs={{0,2},{2,4},{4,6},{6,8},{8,10},{10,12},{12,14},{14,16},{16,18},{18... | collective-permute-start | bytes 4718600 | tf_op jit(solution)/shard_map/ppermute | solution.py:18
  117.5 41.1 %collective-permute-start.18 = (f32[3072,128]{1,0:T(8,128)S(1)}, f32[3072,128]{1,0:T(8,128)}, u32[]{:S(2)}, u32[]{:S(2)}) collective-permute-start(f32[3072,128]{1,0:T(8,128)S(1)} %bitcast.7), channel_id=1, source_target_pairs={{0,126},{2,0},{4,2},{6,4},{8,6},{10,8},{12,10},{14,12},{16,14},{18... | collective-permute-start | bytes 4718600 | tf_op jit(solution)/shard_map/ppermute | solution.py:18
  127.4 38.1 %collective-permute-start.14 = (f32[2,12,128,128]{3,2,1,0:T(8,128)}, f32[2,12,128,128]{3,2,1,0:T(8,128)}, u32[]{:S(2)}, u32[]{:S(2)}) collective-permute-start(f32[2,12,128,128]{3,2,1,0:T(8,128)} %fusion), channel_id=1, source_target_pairs={{0,1},{1,0},{2,3},{3,2},{4,5},{5,4},{6,7},{7,6},{8,9},{9,8},{10,11... | collective-permute-start | bytes 4718600 | tf_op jit(solution)/shard_map/ppermute | solution.py:22
  128.3 64.0 %collective-permute-start.11 = (f32[3072,128]{1,0:T(8,128)S(1)}, f32[3072,128]{1,0:T(8,128)}, u32[]{:S(2)}, u32[]{:S(2)}) collective-permute-start(f32[3072,128]{1,0:T(8,128)S(1)} %bitcast.9), channel_id=1, source_target_pairs={{0,2},{2,4},{4,6},{6,8},{8,10},{10,12},{12,14},{14,16},{16,18},{18... | collective-permute-start | bytes 4718600 | tf_op jit(solution)/shard_map/ppermute | solution.py:18
  128.3 64.0 %collective-permute-start.12 = (f32[3072,128]{1,0:T(8,128)S(1)}, f32[3072,128]{1,0:T(8,128)}, u32[]{:S(2)}, u32[]{:S(2)}) collective-permute-start(f32[3072,128]{1,0:T(8,128)S(1)} %bitcast.10), channel_id=1, source_target_pairs={{0,126},{2,0},{4,2},{6,4},{8,6},{10,8},{12,10},{14,12},{16,14},{18... | collective-permute-start | bytes 4718600 | tf_op jit(solution)/shard_map/ppermute | solution.py:18
  135.2 11.4 %copy-start.25 = (s32[2]{0:T(128)S(1)}, s32[2]{0:T(128)}, u32[]{:S(2)}) copy-start(s32[2]{0:T(128)} %pad_add_fusion.1.meta.refs_0_) | copy-start | bytes 28
  135.2 11.4 %copy-start.27 = (s32[4,24]{1,0:T(4,128)S(1)}, s32[4,24]{1,0:T(4,128)}, u32[]{:S(2)}) copy-start(s32[4,24]{1,0:T(4,128)} %refs_1_.17) | copy-start | bytes 1156
  135.2 11.4 %copy-start.29 = (s32[2,40]{1,0:T(2,128)S(1)}, s32[2,40]{1,0:T(2,128)}, u32[]{:S(2)}) copy-start(s32[2,40]{1,0:T(2,128)} %copy-done.28) | copy-start | bytes 964
  156.0 11.3 %copy-start.11 = (f32[4,12,128,128]{3,2,1,0:T(8,128)}, f32[4,12,128,128]{3,2,1,0:T(8,128)S(1)}, u32[]{:S(2)}) copy-start(f32[4,12,128,128]{3,2,1,0:T(8,128)S(1)} %get-tuple-element.57.refs_9_) | copy-start | bytes 9437188
  156.0 11.3 %copy-start.12 = (f32[4,12,128,128]{3,2,1,0:T(8,128)}, f32[4,12,128,128]{3,2,1,0:T(8,128)S(1)}, u32[]{:S(2)}) copy-start(f32[4,12,128,128]{3,2,1,0:T(8,128)S(1)} %get-tuple-element.58.refs_10_) | copy-start | bytes 9437188
  158.7 67.3 %collective-permute-start.19 = (f32[3072,128]{1,0:T(8,128)}, f32[3072,128]{1,0:T(8,128)S(1)}, u32[]{:S(2)}, u32[]{:S(2)}) collective-permute-start(f32[3072,128]{1,0:T(8,128)} %collective-permute-done.17.refs_5_), channel_id=1, source_target_pairs={{0,2},{2,4},{4,6},{6,8},{8,10},{10,12},{12,14},{14,16},{16,18},{18... | collective-permute-start | bytes 4718600 | tf_op jit(solution)/shard_map/ppermute | solution.py:18
  158.7 67.3 %collective-permute-start.20 = (f32[3072,128]{1,0:T(8,128)}, f32[3072,128]{1,0:T(8,128)}, u32[]{:S(2)}, u32[]{:S(2)}) collective-permute-start(f32[3072,128]{1,0:T(8,128)} %collective-permute-done.18.refs_7_), channel_id=1, source_target_pairs={{0,126},{2,0},{4,2},{6,4},{8,6},{10,8},{12,10},{14,12},{16,14},{18... | collective-permute-start | bytes 4718600 | tf_op jit(solution)/shard_map/ppermute | solution.py:18
  167.3 32.0 %copy-start.1 = (bf16[5,2,4,128,256]{4,3,2,1,0:T(8,128)(2,1)S(1)}, bf16[5,2,4,128,256]{4,3,2,1,0:T(8,128)(2,1)}, u32[]{:S(2)}) copy-start(bf16[5,2,4,128,256]{4,3,2,1,0:T(8,128)(2,1)} %get-tuple-element.56.refs_3_.refs_4_) | copy-start | bytes 7864324
  167.3 32.0 %copy-start.31 = (s32[2,40]{1,0:T(2,128)S(1)}, s32[2,40]{1,0:T(2,128)}, u32[]{:S(2)}) copy-start(s32[2,40]{1,0:T(2,128)} %copy-done.30) | copy-start | bytes 964
  167.3 32.0 %copy-start.33 = (s32[2,40]{1,0:T(2,128)S(1)}, s32[2,40]{1,0:T(2,128)}, u32[]{:S(2)}) copy-start(s32[2,40]{1,0:T(2,128)} %copy-done.32) | copy-start | bytes 964
  169.4 56.6 %copy-start.21 = (s32[2,40]{1,0:T(2,128)S(1)}, s32[2,40]{1,0:T(2,128)}, u32[]{:S(2)}) copy-start(s32[2,40]{1,0:T(2,128)} %copy-done.20) | copy-start | bytes 964
  169.4 56.6 %copy-start.23 = (s32[2,40]{1,0:T(2,128)S(1)}, s32[2,40]{1,0:T(2,128)}, u32[]{:S(2)}) copy-start(s32[2,40]{1,0:T(2,128)} %copy-done.22) | copy-start | bytes 964
  192.4 67.3 %collective-permute-start.15 = (f32[3072,128]{1,0:T(8,128)}, f32[3072,128]{1,0:T(8,128)S(1)}, u32[]{:S(2)}, u32[]{:S(2)}) collective-permute-start(f32[3072,128]{1,0:T(8,128)} %collective-permute-done.11.refs_6_), channel_id=1, source_target_pairs={{0,2},{2,4},{4,6},{6,8},{8,10},{10,12},{12,14},{14,16},{16,18},{18... | collective-permute-start | bytes 4718600 | tf_op jit(solution)/shard_map/ppermute | solution.py:18
  192.4 67.3 %collective-permute-start.16 = (f32[3072,128]{1,0:T(8,128)}, f32[3072,128]{1,0:T(8,128)S(1)}, u32[]{:S(2)}, u32[]{:S(2)}) collective-permute-start(f32[3072,128]{1,0:T(8,128)} %collective-permute-done.12.refs_8_), channel_id=1, source_target_pairs={{0,126},{2,0},{4,2},{6,4},{8,6},{10,8},{12,10},{14,12},{16,14},{18... | collective-permute-start | bytes 4718600 | tf_op jit(solution)/shard_map/ppermute | solution.py:18
  227.9 31.8 %copy-start.17 = (bf16[2,1,2,128,256]{4,3,2,1,0:T(8,128)(2,1)S(1)}, bf16[2,1,2,128,256]{4,3,2,1,0:T(8,128)(2,1)}, u32[]{:S(2)}) copy-start(bf16[2,1,2,128,256]{4,3,2,1,0:T(8,128)(2,1)} %get-tuple-element.53.refs_4_) | copy-start | bytes 786436
  264.2 6.0 %collective-permute-start.21 = (f32[2,12,128,128]{3,2,1,0:T(8,128)S(1)}, f32[2,12,128,128]{3,2,1,0:T(8,128)S(1)}, u32[]{:S(2)}, u32[]{:S(2)}) collective-permute-start(f32[2,12,128,128]{3,2,1,0:T(8,128)S(1)} %get-tuple-element.66), channel_id=1, source_target_pairs={{0,1},{1,0},{2,3},{3,2},{4,5},{5,4},{6,7},{7,6},{8,9},{9,8},{10,11... | collective-permute-start | bytes 4718600 | tf_op jit(solution)/shard_map/ppermute | solution.py:22
  270.1 3.5 %collective-permute-start.22 = (f32[2,12,128,128]{3,2,1,0:T(8,128)S(1)}, f32[2,12,128,128]{3,2,1,0:T(8,128)S(1)}, u32[]{:S(2)}, u32[]{:S(2)}) collective-permute-start(f32[2,12,128,128]{3,2,1,0:T(8,128)S(1)} %get-tuple-element.71), channel_id=1, source_target_pairs={{0,1},{1,0},{2,3},{3,2},{4,5},{5,4},{6,7},{7,6},{8,9},{9,8},{10,11... | collective-permute-start | bytes 4718600 | tf_op jit(solution)/shard_map/ppermute | solution.py:22
  (11 other events, 46.7 us)

commit v5 on v4

--- a/solution.py
+++ b/solution.py
@@ -50,7 +50,7 @@
 def copy_last(out, parts, row_of):
     for part, ref in enumerate(parts):
         for gi, group in enumerate((0, 4)):
-            for row in range(2):
+            for row in range(ref.shape[2]):
                 ref[gi, 0, row] = out[group, 1, row_of(part, row)]
 
 
@@ -106,7 +106,7 @@
 
                 lax.fori_loop(0, table.shape[0] // 128, body, 0)
                 first += table.shape[0] // 128
-    copy_last(out, (part_a, part_b), lambda part, row: 2 * part + row)
+    copy_last(out, (part_a, part_b), lambda part, row: 3 * part + row)
 
 
 def stage_kernel(gs, crs, pieces, starts, counts, total, by_rows, row0, col0, has_acc, portions, *refs):
@@ -118,8 +118,8 @@
     direct = lefts.shape[0] != 5
     sources = [refs.pop(0) for _ in range(sum(pieces))]
     acc_sources = [refs.pop(0) for _ in range(2 if has_acc else 0)]
-    results = [refs.pop(0) for _ in range(2 * portions)]
-    straight = portions == 2 or direct
+    results = [refs.pop(0) for _ in range(2 * len(portions))]
+    straight = len(portions) == 2 or direct
     right_high, right_low, dense, left_held, sems = refs[:5]
     refs = refs[5:]
     held = sources if direct else [refs.pop(0) for _ in sources]
@@ -202,16 +202,17 @@
         lax.fori_loop(first // 4, last // 4, body, 0, unroll=2)
     for copy in acc_copies:
         copy.wait()
-    each, kept_cols = outs[0].shape[:2]
+    kept_cols = outs[0].shape[1]
+    places = [(portion, row) for portion, number in enumerate(portions) for row in range(number)]
     leaving = []
     for which in (1, 0):
         side = core if which == 0 else 1 - core
-        for row in range(each * portions):
-            source = side * each * portions + row if by_rows else row
+        for row, (portion, local) in enumerate(places):
+            source = side * len(places) + row if by_rows else row
             at_row = 2 * side + row0 + row if by_rows else row0 + row
             at_col = 0 if by_rows else kept_cols * side
-            portion = which * portions + row // each
-            own, sum_in = outs[portion].at[row % each], acc[which].at[row] if acc else None
+            portion = which * len(portions) + portion
+            own, sum_in = outs[portion].at[local], acc[which].at[row] if acc else None
 
             def out_body(y, carry, own=own, sum_in=sum_in, source=source, at_row=at_row, at_col=at_col):
                 value = dense[wrap(outcols[at_row, at_col + y] - base, total), source]
@@ -220,7 +221,7 @@
 
             lax.fori_loop(0, kept_cols, out_body, 0, unroll=4)
             if not straight:
-                leaving.append(start(own, results[portion].at[row % each]))
+                leaving.append(start(own, results[portion].at[local]))
     for copy in leaving:
         copy.wait()
 
@@ -231,25 +232,26 @@
 PARAMS = pltpu.CompilerParams(vmem_limit_bytes=60 << 20)
 
 
-def stage(name, gs, crs, by_rows, part, total, meta, outcols, patterns, left, tables, acc, col0, portions=1):
+def stage(name, gs, crs, by_rows, part, total, meta, outcols, patterns, left, tables, acc, col0, halves=None):
     if by_rows:
         starts, counts = [4 * (g + 2) for g in gs], [20] * len(gs)
         out = (2 if part is None else 1, outcols.shape[1], 128, 128)
         row0, rows = part or 0, 2 * out[0]
     else:
         starts, counts = [max(0, 4 * g) for g in gs], [WINDOW - 4 * abs(g) for g in gs]
-        out = (4 if part is None else 2, outcols.shape[1] // 2, 128, 128)
-        row0, rows = 2 * (part or 0), out[0]
+        out = ((3, 1, 4)[2 if part is None else part], outcols.shape[1] // 2, 128, 128)
+        row0, rows = 3 * (part or 0), out[0]
+    portions = ((1, 1) if by_rows else (3, 1)) if halves else (out[0],)
     tables = [tables[g][c] for g in gs for c in crs]
     kernel = functools.partial(
         stage_kernel, gs, crs, [len(t) for t in tables], starts, counts, total, by_rows, row0, col0, bool(acc), portions
     )
-    shape = jax.ShapeDtypeStruct((out[0] // portions,) + out[1:], F32)
+    shapes = [(number,) + out[1:] for number in portions] * 2
     blocks = [piece for table in tables for piece in table]
     if part is not None:
         blocks = [pltpu.with_memory_space_constraint(b, pltpu.VMEM) for b in blocks]
         acc = [pltpu.with_memory_space_constraint(a, pltpu.VMEM) for a in acc]
-    straight = portions == 2 or part is not None
+    straight = halves or part is not None
     window = max(counts)
     wide = pltpu.VMEM((len(gs), window + 1, len(crs), 128, 128), BF16)
     scratch = [
@@ -264,15 +266,15 @@
     else:
         held = []
     if not straight:
-        held += [pltpu.VMEM(shape.shape, F32)] * (2 * portions)
+        held += [pltpu.VMEM(shape, F32) for shape in shapes]
     used = sum(math.prod(ref.shape) * jnp.dtype(ref.dtype).itemsize for ref in scratch + held)
     copies = len(blocks) + len(gs) * len(crs) + len(acc) + 2 * out[0]
     return pl.pallas_call(
         kernel,
         name=name,
-        out_shape=[pltpu.VMEM(shape.shape, F32) if straight else shape] * (2 * portions),
+        out_shape=[pltpu.VMEM(shape, F32) if straight else jax.ShapeDtypeStruct(shape, F32) for shape in shapes],
         in_specs=[SMEM] * (2 + len(gs)) + [HERE] + [HERE if part is None else VMEM] * (len(blocks) + len(acc)),
-        out_specs=[VMEM if straight else HERE] * (2 * portions),
+        out_specs=[VMEM if straight else HERE] * len(shapes),
         scratch_shapes=scratch + [pltpu.SemaphoreType.DMA((copies,))] + held,
         compiler_params=pltpu.CompilerParams(vmem_limit_bytes=used + (6 << 20)),
         cost_estimate=pl.CostEstimate(flops=0, transcendentals=0, bytes_accessed=0),
@@ -281,13 +283,13 @@
     )
 
 
-def left_call(kernel, name, scalars, arrays):
+def left_call(kernel, name, scalars, arrays, parts):
     out = jax.ShapeDtypeStruct((5, 2, 4, 128, 256), BF16)
-    last = jax.ShapeDtypeStruct((2, 1, 2, 128, 256), BF16)
+    last = [jax.ShapeDtypeStruct((2, 1, rows, 128, 256), BF16) for rows in parts]
     return pl.pallas_call(
         kernel,
         name=name,
-        out_shape=[out, last, last],
+        out_shape=[out, *last],
         in_specs=[SMEM] * len(scalars) + [VMEM] * len(arrays),
         out_specs=[VMEM] * 3,
         compiler_params=PARAMS,
@@ -323,7 +325,7 @@
     own[0] = jnp.concatenate([own[0], columns], axis=0)
     margin_left = left_call(
         functools.partial(margin_left_kernel, total), "margin_left",
-        [meta, margin_cols, swap(margin_cols)], [margin_blocks, swap(margin_blocks)],
+        [meta, margin_cols, swap(margin_cols)], [margin_blocks, swap(margin_blocks)], (2, 2),
     )
 
     def after_margin(below, above):
@@ -335,7 +337,7 @@
         patterns[g] = factors[g][0][0][slots * 128 : slots * 128 + 2, : pattern.shape[1]].astype(jnp.int32)
     part = lambda name, gs, crs, which, acc: stage(
         name, gs, crs, True, which, total, meta, product_cols, patterns, margin_left, factors, acc, 0,
-        2 if gs == (-2, 2) and which is None else 1,
+        gs == (-2, 2) and which is None,
     )
     acc = part("product_near", (0, -1, 1), (0, 1), None, ())
     acc = part("product_far0", (-2, 2), (0,), None, acc)
@@ -351,12 +353,12 @@
     blocks = [factors[g][c] for g in range(-2, 3) for c in range(2)]
     factor_left = left_call(
         functools.partial(factor_left_kernel, [len(b) for b in blocks], total), "factor_left",
-        [meta] + [patterns[g] for g in range(-2, 3)], [piece for b in blocks for piece in b],
+        [meta] + [patterns[g] for g in range(-2, 3)], [piece for b in blocks for piece in b], (3, 1),
     )
     products = {0: [(row,) for row in rows]}
     part = lambda name, gs, crs, which, acc: stage(
         name, gs, crs, False, which, total, meta, metric_cols, patterns, factor_left, products, acc, slots,
-        2 if gs == (-2, 2) and which is None else 1,
+        gs == (-2, 2) and which is None,
     )
     own_acc = part("metric_own", (0,), (0, 1), None, ())
 
@@ -371,7 +373,9 @@
     acc = part("metric_near", (-1, 1), (0, 1), None, own_acc)
     acc = part("metric_far0", (-2, 2), (0,), None, acc)
     finals = [part("metric_far1", (-2, 2), (1,), which, acc[which::2]) for which in range(2)]
-    metric = jnp.concatenate([kept + swap(sent) for kept, sent in finals], axis=0)
+    first, last = [kept + swap(sent) for kept, sent in finals]
+    metric = lax.optimization_barrier(jnp.pad(first, ((0, last.shape[0]), (0, 0), (0, 0), (0, 0))))
+    metric = lax.dynamic_update_slice_in_dim(metric, last, first.shape[0], 0)
     return (made[0], metric)
 
 

time: 276 us -> 275 us (level)
  local copies, waits for them, and re-layouts: 8.3 us -> 12.8 us
  waiting for transfers between devices: 113 us -> 109 us
    unnamed x72 -> x78, local copies, waits for them, and re-layouts: 6.62 us -> 10.8 us
  transfers between devices with their start and end apart: 23 -> 23, of which waited for: 11 -> 12; matrix products, arithmetic and copies ran while one was open for 4% -> 5% of each run, Pallas kernels for 26% -> 25%
where the time goes in v5:
time: 275 us; the launch traced here: 274 us
  waiting for transfers between devices  109 us (40%)
  Pallas kernels  79.5 us (29%)
  starting transfers between devices  61.1 us (22%)
  local copies, waits for them, and re-layouts  12.8 us (5%)
  other arithmetic  10.9 us (4%)
    ppermute x16, waiting for transfers between devices, ring(): lax.ppermute(array, 'rows', [(i, (i + by) % devices) for i in range(devic...  106 us
    pallas_call x9, Pallas kernels, stage(): pl.pallas_call(kernel, name=name, out_shape=[pltpu.VMEM(shape, F32) if st...  62.6 us
    ppermute x16, starting transfers between devices, ring(): lax.ppermute(array, 'rows', [(i, (i + by) % devices) for i in range(devic...  56.2 us
    pallas_call x2, Pallas kernels, left_call(): pl.pallas_call(kernel, name=name, out_shape=[out, *last], in_specs=[SMEM]...  16.9 us
    unnamed x78, local copies, waits for them, and re-layouts  10.8 us
  transfers between devices with their start and end apart: 23, of which 12 were waited for; matrix products, arithmetic and copies ran while one was open for 5% of the time, Pallas kernels for 25%

profile of v5, /device:TPU:1, one launch (start us, length us, event | category | flops | bytes accessed | tf_op | source)
XLA Modules:
  0.0 274.3 jit_solution(10358436537800813988)
XLA Ops:
  0.6 1.5 collective-permute-start.3
  2.1 0.8 pad_add_fusion
  2.9 1.7 constant_dynamic-slice_fusion
  4.7 1.4 collective-permute-start
  6.1 7.3 %collective-permute-start.1 = (f32[2056,128]{1,0:T(8,128)S(1)}, f32[2056,128]{1,0:T(8,128)}, u32[]{:S(2)}, u32[]{:S(2)}) collective-permute-start(f32[2056,128]{1,0:T(8,128)S(1)} %select_maximum_fusion.refs_6_.refs_9_), channel_id=1, source_target_pairs={{0,126},{2,0},{4,2},{6,4},{8,6},{10,8},{12,10},{14,12},{16,14},{18... | collective-permute-start | bytes 3158024 | tf_op jit(solution)/shard_map/ppermute | solution.py:18
  13.7 0.8 collective-permute-done.2.cols_b
  14.5 6.0 %collective-permute-start.8 = (f32[2048,128]{1,0:T(8,128)S(1)}, f32[2048,128]{1,0:T(8,128)}, u32[]{:S(2)}, u32[]{:S(2)}) collective-permute-start(f32[2048,128]{1,0:T(8,128)S(1)} %bitcast.13), channel_id=1, source_target_pairs={{0,126},{2,0},{4,2},{6,4},{8,6},{10,8},{12,10},{14,12},{16,14},{18... | collective-permute-start | bytes 3145736 | tf_op jit(solution)/shard_map/ppermute | solution.py:18
  21.2 5.5 %margin_left.1 = (bf16[5,2,4,128,256]{4,3,2,1,0:T(8,128)(2,1)}, bf16[2,1,2,128,256]{4,3,2,1,0:T(8,128)(2,1)}, bf16[2,1,2,128,256]{4,3,2,1,0:T(8,128)(2,1)}) custom-call(s32[2]{0:T(128)} %pad_add_fusion.1.meta.refs_0_, s32[4,8]{1,0:T(4,128)} %cols_a.1, s32[4,8]{1,0:T(4,128)} %copy-done.38, f32[4,8,128,128]{3,2,1,0:T(8,128)} %table_a.1, ...), custom_call_target="tpu_custom_call" | custom-call | tf_op jit(solution)/shard_map/margin_left/pallas_call | solution.py:289
  26.7 10.2 %collective-permute-done.refs_8_.refs_7_ = f32[2056,128]{1,0:T(8,128)S(1)} collective-permute-done((f32[2056,128]{1,0:T(8,128)S(1)}, f32[2056,128]{1,0:T(8,128)S(1)}, u32[]{:S(2)}, u32[]{:S(2)}) %collective-permute-start) | collective-permute-done | bytes 1052704 | tf_op jit(solution)/shard_map/ppermute | solution.py:18
  36.9 6.9 %collective-permute-start.5 = (f32[2056,128]{1,0:T(8,128)}, f32[2056,128]{1,0:T(8,128)S(1)}, u32[]{:S(2)}, u32[]{:S(2)}) collective-permute-start(f32[2056,128]{1,0:T(8,128)} %collective-permute-done.1.refs_10_.refs_11_), channel_id=1, source_target_pairs={{0,126},{2,0},{4,2},{6,4},{8,6},{10,8},{12,10},{14,12},{16,14},{18... | collective-permute-start | bytes 3158024 | tf_op jit(solution)/shard_map/ppermute | solution.py:18
  43.7 15.7 %collective-permute-done.6.refs_9_.refs_8_ = f32[2048,128]{1,0:T(8,128)} collective-permute-done((f32[2048,128]{1,0:T(8,128)S(1)}, f32[2048,128]{1,0:T(8,128)}, u32[]{:S(2)}, u32[]{:S(2)}) %collective-permute-start.6) | collective-permute-done | bytes 1048608 | tf_op jit(solution)/shard_map/ppermute | solution.py:18
  59.5 6.9 %collective-permute-start.9 = (f32[2048,128]{1,0:T(8,128)}, f32[2048,128]{1,0:T(8,128)S(1)}, u32[]{:S(2)}, u32[]{:S(2)}) collective-permute-start(f32[2048,128]{1,0:T(8,128)} %collective-permute-done.8.refs_11_.refs_12_), channel_id=1, source_target_pairs={{0,126},{2,0},{4,2},{6,4},{8,6},{10,8},{12,10},{14,12},{16,14},{18... | collective-permute-start | bytes 3145736 | tf_op jit(solution)/shard_map/ppermute | solution.py:18
  67.1 1.7 copy-done.2
  68.8 10.5 %product_near.1 = (f32[2,24,128,128]{3,2,1,0:T(8,128)S(1)}, f32[2,24,128,128]{3,2,1,0:T(8,128)S(1)}) custom-call(s32[2]{0:T(128)S(1)} %copy-done.26, s32[4,24]{1,0:T(4,128)S(1)} %copy-done.28, s32[2,40]{1,0:T(2,128)S(1)} %get-tuple-element.73.refs_2_, s32[2,40]{1,0:T(2,128)S(1)} %slice_convert_fusion.1.refs_3_.refs_1_.refs_2_, ...), custom_call_target="tpu_custom_call" | custom-call | tf_op jit(solution)/shard_map/product_near/pallas_call | solution.py:272
  79.3 1.8 collective-permute-done.5.refs_6_.refs_13_
  81.2 0.7 collective-permute-done.4.refs_5_
  81.9 6.1 %product_far0.1 = (f32[1,24,128,128]{3,2,1,0:T(8,128)S(1)}, f32[1,24,128,128]{3,2,1,0:T(8,128)S(1)}, f32[1,24,128,128]{3,2,1,0:T(8,128)S(1)}, f32[1,24,128,128]{3,2,1,0:T(8,128)S(1)}) custom-call(s32[2]{0:T(128)S(1)} %copy-done.26, s32[4,24]{1,0:T(4,128)S(1)} %copy-done.28, s32[2,40]{1,0:T(2,128)S(1)} %slice_convert_fusion.3.refs_2_.refs_0_, ...), custom_call_target="tpu_custom_call" | custom-call | tf_op jit(solution)/shard_map/product_far0/pallas_call | solution.py:272
  88.1 16.3 %collective-permute-done.7.refs_5_.refs_6_ = f32[2048,128]{1,0:T(8,128)S(1)} collective-permute-done((f32[2048,128]{1,0:T(8,128)}, f32[2048,128]{1,0:T(8,128)S(1)}, u32[]{:S(2)}, u32[]{:S(2)}) %collective-permute-start.7) | collective-permute-done | bytes 1048608 | tf_op jit(solution)/shard_map/ppermute | solution.py:18
  104.4 4.1 %product_far1.3 = (f32[1,24,128,128]{3,2,1,0:T(8,128)S(1)}, f32[1,24,128,128]{3,2,1,0:T(8,128)S(1)}) custom-call(s32[2]{0:T(128)S(1)} %copy-done.26, s32[4,24]{1,0:T(4,128)S(1)} %copy-done.28, s32[2,40]{1,0:T(2,128)S(1)} %slice_convert_fusion.3.refs_2_.refs_0_, s32[2,40]{1,0:T(2,128)S(1)} %slice_convert_fusion.2.refs_3_.refs_4_, ...), custom_call_target="tpu_custom_call" | custom-call | tf_op jit(solution)/shard_map/product_far1/pallas_call | solution.py:272
  109.2 5.3 %product_far1.2 = (f32[1,24,128,128]{3,2,1,0:T(8,128)S(1)}, f32[1,24,128,128]{3,2,1,0:T(8,128)}) custom-call(s32[2]{0:T(128)S(1)} %copy-done.26, s32[4,24]{1,0:T(4,128)S(1)} %copy-done.28, s32[2,40]{1,0:T(2,128)S(1)} %slice_convert_fusion.3.refs_2_.refs_0_, s32[2,40]{1,0:T(2,128)S(1)} %slice_convert_fusion.2.refs_3_.refs_4_, ...), custom_call_target="tpu_custom_call" | custom-call | tf_op jit(solution)/shard_map/product_far1/pallas_call | solution.py:272
  114.6 1.1 copy-done.14
  115.7 1.7 add.39
  117.5 7.0 %collective-permute-start.18 = (f32[3072,128]{1,0:T(8,128)S(1)}, f32[3072,128]{1,0:T(8,128)}, u32[]{:S(2)}, u32[]{:S(2)}) collective-permute-start(f32[3072,128]{1,0:T(8,128)S(1)} %bitcast.7), channel_id=1, source_target_pairs={{0,126},{2,0},{4,2},{6,4},{8,6},{10,8},{12,10},{14,12},{16,14},{18... | collective-permute-start | bytes 4718600 | tf_op jit(solution)/shard_map/ppermute | solution.py:18
  124.5 1.6 add.38
  126.2 1.3 fusion
  127.4 0.9 collective-permute-start.14
  128.3 6.9 %collective-permute-start.12 = (f32[3072,128]{1,0:T(8,128)S(1)}, f32[3072,128]{1,0:T(8,128)}, u32[]{:S(2)}, u32[]{:S(2)}) collective-permute-start(f32[3072,128]{1,0:T(8,128)S(1)} %bitcast.10), channel_id=1, source_target_pairs={{0,126},{2,0},{4,2},{6,4},{8,6},{10,8},{12,10},{14,12},{16,14},{18... | collective-permute-start | bytes 4718600 | tf_op jit(solution)/shard_map/ppermute | solution.py:18
  135.2 11.4 %factor_left.1 = (bf16[5,2,4,128,256]{4,3,2,1,0:T(8,128)(2,1)}, bf16[2,1,3,128,256]{4,3,2,1,0:T(8,128)(2,1)}, bf16[2,1,1,128,256]{4,3,2,1,0:T(8,128)(2,1)}) custom-call(s32[2]{0:T(128)} %pad_add_fusion.1.meta.refs_0_, s32[2,40]{1,0:T(2,128)} %copy-done.24, s32[2,40]{1,0:T(2,128)} %copy-done.34, s32[2,40]{1,0:T(2,128)} %copy-done.30, s32[2,40]{1,0:T(2,128)} %copy-done.32, ...), custom_call_target="tpu_custom_call" | custom-call | tf_op jit(solution)/shard_map/factor_left/pallas_call | solution.py:289
  146.7 1.7 copy-done
  148.4 7.6 %metric_own.1 = (f32[4,12,128,128]{3,2,1,0:T(8,128)S(1)}, f32[4,12,128,128]{3,2,1,0:T(8,128)S(1)}) custom-call(s32[2]{0:T(128)S(1)} %copy-done.27, s32[4,24]{1,0:T(4,128)S(1)} %copy-done.29, s32[2,40]{1,0:T(2,128)S(1)} %copy-done.31, bf16[5,2,4,128,256]{4,3,2,1,0:T(8,128)(2,1)S(1)} %copy-done, f32[3072,128]{1,0:T(8,128)S(1)} %bitcast.8, f32[3072,128]{1,0:T(8,128)S(1)} %bitcast.11), custom_call_target="tpu_custom_call" | custom-call | tf_op jit(solution)/shard_map/metric_own/pallas_call | solution.py:272
  156.0 2.7 collective-permute-done.17.refs_5_
  158.7 6.9 %collective-permute-start.20 = (f32[3072,128]{1,0:T(8,128)}, f32[3072,128]{1,0:T(8,128)}, u32[]{:S(2)}, u32[]{:S(2)}) collective-permute-start(f32[3072,128]{1,0:T(8,128)} %collective-permute-done.18.refs_7_), channel_id=1, source_target_pairs={{0,126},{2,0},{4,2},{6,4},{8,6},{10,8},{12,10},{14,12},{16,14},{18... | collective-permute-start | bytes 4718600 | tf_op jit(solution)/shard_map/ppermute | solution.py:18
  165.6 1.7 broadcast_select_fusion.1
  167.3 2.0 pad_maximum_fusion
  169.4 23.0 %collective-permute-done.11.refs_6_ = f32[3072,128]{1,0:T(8,128)} collective-permute-done((f32[3072,128]{1,0:T(8,128)S(1)}, f32[3072,128]{1,0:T(8,128)}, u32[]{:S(2)}, u32[]{:S(2)}) %collective-permute-start.11) | collective-permute-done | bytes 1572896 | tf_op jit(solution)/shard_map/ppermute | solution.py:18
  192.4 6.9 %collective-permute-start.16 = (f32[3072,128]{1,0:T(8,128)}, f32[3072,128]{1,0:T(8,128)S(1)}, u32[]{:S(2)}, u32[]{:S(2)}) collective-permute-start(f32[3072,128]{1,0:T(8,128)} %collective-permute-done.12.refs_8_), channel_id=1, source_target_pairs={{0,126},{2,0},{4,2},{6,4},{8,6},{10,8},{12,10},{14,12},{16,14},{18... | collective-permute-start | bytes 4718600 | tf_op jit(solution)/shard_map/ppermute | solution.py:18
  199.3 12.9 %metric_near.1 = (f32[4,12,128,128]{3,2,1,0:T(8,128)S(1)}, f32[4,12,128,128]{3,2,1,0:T(8,128)}) custom-call(s32[2]{0:T(128)S(1)} %copy-done.27, s32[4,24]{1,0:T(4,128)S(1)} %copy-done.29, s32[2,40]{1,0:T(2,128)S(1)} %copy-done.35, s32[2,40]{1,0:T(2,128)S(1)} %copy-done.33, bf16[5,2,4,128,256]{4,3,2,1,0:T(8,128)(2,1)S(1)} %copy-done.1, ...), custom_call_target="tpu_custom_call" | custom-call | tf_op jit(solution)/shard_map/metric_near/pallas_call | solution.py:272
  212.2 13.8 %collective-permute-done.19.refs_5_ = f32[3072,128]{1,0:T(8,128)S(1)} collective-permute-done((f32[3072,128]{1,0:T(8,128)}, f32[3072,128]{1,0:T(8,128)S(1)}, u32[]{:S(2)}, u32[]{:S(2)}) %collective-permute-start.19) | collective-permute-done | bytes 1572896 | tf_op jit(solution)/shard_map/ppermute | solution.py:18
  226.0 1.1 copy-done.16
  227.1 1.9 copy-done.13
  229.0 1.4 copy-done.17
  230.4 7.0 %metric_far0.1 = (f32[3,12,128,128]{3,2,1,0:T(8,128)S(1)}, f32[1,12,128,128]{3,2,1,0:T(8,128)S(1)}, f32[3,12,128,128]{3,2,1,0:T(8,128)S(1)}, f32[1,12,128,128]{3,2,1,0:T(8,128)S(1)}) custom-call(s32[2]{0:T(128)S(1)} %copy-done.27, s32[4,24]{1,0:T(4,128)S(1)} %copy-done.29, s32[2,40]{1,0:T(2,128)S(1)} %copy-done.25, s32[2,40]{1,0:T(2,128)S(1)} %copy-done.23, ...), custom_call_target="tpu_custom_call" | custom-call | tf_op jit(solution)/shard_map/metric_far0/pallas_call | solution.py:272
  237.4 22.3 %collective-permute-done.15.refs_5_ = f32[3072,128]{1,0:T(8,128)S(1)} collective-permute-done((f32[3072,128]{1,0:T(8,128)}, f32[3072,128]{1,0:T(8,128)S(1)}, u32[]{:S(2)}, u32[]{:S(2)}) %collective-permute-start.15) | collective-permute-done | bytes 1572896 | tf_op jit(solution)/shard_map/ppermute | solution.py:18
  259.7 5.7 %metric_far1.2 = (f32[3,12,128,128]{3,2,1,0:T(8,128)S(1)}, f32[3,12,128,128]{3,2,1,0:T(8,128)S(1)}) custom-call(s32[2]{0:T(128)S(1)} %copy-done.27, s32[4,24]{1,0:T(4,128)S(1)} %copy-done.29, s32[2,40]{1,0:T(2,128)S(1)} %copy-done.25, s32[2,40]{1,0:T(2,128)S(1)} %copy-done.23, bf16[2,1,3,128,256]{4,3,2,1,0:T(8,128)(2,1)S(1)} %copy-done.18, ...), custom_call_target="tpu_custom_call" | custom-call | tf_op jit(solution)/shard_map/metric_far1/pallas_call | solution.py:272
  265.4 1.3 collective-permute-start.21
  266.7 3.4 %metric_far1.3 = (f32[1,12,128,128]{3,2,1,0:T(8,128)S(1)}, f32[1,12,128,128]{3,2,1,0:T(8,128)S(1)}) custom-call(s32[2]{0:T(128)S(1)} %copy-done.27, s32[4,24]{1,0:T(4,128)S(1)} %copy-done.29, s32[2,40]{1,0:T(2,128)S(1)} %copy-done.25, s32[2,40]{1,0:T(2,128)S(1)} %copy-done.23, bf16[2,1,1,128,256]{4,3,2,1,0:T(8,128)(2,1)S(1)} %copy-done.21, ...), custom_call_target="tpu_custom_call" | custom-call | tf_op jit(solution)/shard_map/metric_far1/pallas_call | solution.py:272
  271.6 1.0 collective-permute-done.22
  272.7 1.7 copy-done.36
  (104 shorter events, 4.2 us)
Async XLA Ops:
  0.6 20.5 %collective-permute-start.3 = (f32[4,8,128,128]{3,2,1,0:T(8,128)}, f32[4,8,128,128]{3,2,1,0:T(8,128)}, u32[]{:S(2)}, u32[]{:S(2)}) collective-permute-start(f32[4,8,128,128]{3,2,1,0:T(8,128)} %table_a.1), channel_id=1, source_target_pairs={{0,1},{1,0},{2,3},{3,2},{4,5},{5,4},{6,7},{7,6},{8,9},{9,8},{10,11... | collective-permute-start | bytes 6291464 | tf_op jit(solution)/shard_map/ppermute | solution.py:22
  2.9 64.1 %copy-start.30 = (s32[2,40]{1,0:T(2,128)}, s32[2,40]{1,0:T(2,128)S(1)}, u32[]{:S(2)}) copy-start(s32[2,40]{1,0:T(2,128)S(1)} %get-tuple-element.73.refs_2_) | copy-start | bytes 964
  4.6 62.4 %copy-start.5 = (f32[1,16,128,128]{3,2,1,0:T(8,128)}, f32[1,16,128,128]{3,2,1,0:T(8,128)S(1)}, u32[]{:S(2)}) copy-start(f32[1,16,128,128]{3,2,1,0:T(8,128)S(1)} %get-tuple-element.76) | copy-start | bytes 3145732
  4.6 8.7 %copy-start.37 = (s32[4,8]{1,0:T(4,128)S(1)}, s32[4,8]{1,0:T(4,128)}, u32[]{:S(2)}) copy-start(s32[4,8]{1,0:T(4,128)} %cols_a.1) | copy-start | bytes 388
  4.7 62.4 %copy-start.4 = (f32[2056,128]{1,0:T(8,128)}, f32[2056,128]{1,0:T(8,128)S(1)}, u32[]{:S(2)}) copy-start(f32[2056,128]{1,0:T(8,128)S(1)} %select_maximum_fusion.refs_6_.refs_9_) | copy-start | bytes 3158020
  4.7 32.2 %collective-permute-start = (f32[2056,128]{1,0:T(8,128)S(1)}, f32[2056,128]{1,0:T(8,128)S(1)}, u32[]{:S(2)}, u32[]{:S(2)}) collective-permute-start(f32[2056,128]{1,0:T(8,128)S(1)} %select_maximum_fusion.refs_6_.refs_9_), channel_id=1, source_target_pairs={{0,2},{2,4},{4,6},{6,8},{8,10},{10,12},{12,14},{14,16},{16,18},{18... | collective-permute-start | bytes 3158024 | tf_op jit(solution)/shard_map/ppermute | solution.py:18
  6.1 30.8 %collective-permute-start.1 = (f32[2056,128]{1,0:T(8,128)S(1)}, f32[2056,128]{1,0:T(8,128)}, u32[]{:S(2)}, u32[]{:S(2)}) collective-permute-start(f32[2056,128]{1,0:T(8,128)S(1)} %select_maximum_fusion.refs_6_.refs_9_), channel_id=1, source_target_pairs={{0,126},{2,0},{4,2},{6,4},{8,6},{10,8},{12,10},{14,12},{16,14},{18... | collective-permute-start | bytes 3158024 | tf_op jit(solution)/shard_map/ppermute | solution.py:18
  13.4 1.2 collective-permute-start.2
  13.7 45.8 %collective-permute-start.6 = (f32[2048,128]{1,0:T(8,128)S(1)}, f32[2048,128]{1,0:T(8,128)}, u32[]{:S(2)}, u32[]{:S(2)}) collective-permute-start(f32[2048,128]{1,0:T(8,128)S(1)} %bitcast.12), channel_id=1, source_target_pairs={{0,2},{2,4},{4,6},{6,8},{8,10},{10,12},{12,14},{14,16},{16,18},{18... | collective-permute-start | bytes 3145736 | tf_op jit(solution)/shard_map/ppermute | solution.py:18
  14.5 44.9 %collective-permute-start.8 = (f32[2048,128]{1,0:T(8,128)S(1)}, f32[2048,128]{1,0:T(8,128)}, u32[]{:S(2)}, u32[]{:S(2)}) collective-permute-start(f32[2048,128]{1,0:T(8,128)S(1)} %bitcast.13), channel_id=1, source_target_pairs={{0,126},{2,0},{4,2},{6,4},{8,6},{10,8},{12,10},{14,12},{16,14},{18... | collective-permute-start | bytes 3145736 | tf_op jit(solution)/shard_map/ppermute | solution.py:18
  21.2 45.9 %copy-start.26 = (s32[2]{0:T(128)S(1)}, s32[2]{0:T(128)}, u32[]{:S(2)}) copy-start(s32[2]{0:T(128)} %pad_add_fusion.1.meta.refs_0_) | copy-start | bytes 28
  21.2 45.9 %copy-start.28 = (s32[4,24]{1,0:T(4,128)S(1)}, s32[4,24]{1,0:T(4,128)}, u32[]{:S(2)}) copy-start(s32[4,24]{1,0:T(4,128)} %refs_1_.12) | copy-start | bytes 1156
  36.9 42.4 %copy-start.8 = (f32[2056,128]{1,0:T(8,128)}, f32[2056,128]{1,0:T(8,128)S(1)}, u32[]{:S(2)}) copy-start(f32[2056,128]{1,0:T(8,128)S(1)} %collective-permute-done.refs_8_.refs_7_) | copy-start | bytes 3158020
  36.9 44.3 %collective-permute-start.5 = (f32[2056,128]{1,0:T(8,128)}, f32[2056,128]{1,0:T(8,128)S(1)}, u32[]{:S(2)}, u32[]{:S(2)}) collective-permute-start(f32[2056,128]{1,0:T(8,128)} %collective-permute-done.1.refs_10_.refs_11_), channel_id=1, source_target_pairs={{0,126},{2,0},{4,2},{6,4},{8,6},{10,8},{12,10},{14,12},{16,14},{18... | collective-permute-start | bytes 3158024 | tf_op jit(solution)/shard_map/ppermute | solution.py:18
  43.7 38.2 %collective-permute-start.4 = (f32[2056,128]{1,0:T(8,128)S(1)}, f32[2056,128]{1,0:T(8,128)S(1)}, u32[]{:S(2)}, u32[]{:S(2)}) collective-permute-start(f32[2056,128]{1,0:T(8,128)S(1)} %collective-permute-done.refs_8_.refs_7_), channel_id=1, source_target_pairs={{0,2},{2,4},{4,6},{6,8},{8,10},{10,12},{12,14},{14,16},{16,18},{18... | collective-permute-start | bytes 3158024 | tf_op jit(solution)/shard_map/ppermute | solution.py:18
  59.4 44.9 %collective-permute-start.7 = (f32[2048,128]{1,0:T(8,128)}, f32[2048,128]{1,0:T(8,128)S(1)}, u32[]{:S(2)}, u32[]{:S(2)}) collective-permute-start(f32[2048,128]{1,0:T(8,128)} %collective-permute-done.6.refs_9_.refs_8_), channel_id=1, source_target_pairs={{0,2},{2,4},{4,6},{6,8},{8,10},{10,12},{12,14},{14,16},{16,18},{18... | collective-permute-start | bytes 3145736 | tf_op jit(solution)/shard_map/ppermute | solution.py:18
  59.5 44.9 %collective-permute-start.9 = (f32[2048,128]{1,0:T(8,128)}, f32[2048,128]{1,0:T(8,128)S(1)}, u32[]{:S(2)}, u32[]{:S(2)}) collective-permute-start(f32[2048,128]{1,0:T(8,128)} %collective-permute-done.8.refs_11_.refs_12_), channel_id=1, source_target_pairs={{0,126},{2,0},{4,2},{6,4},{8,6},{10,8},{12,10},{14,12},{16,14},{18... | collective-permute-start | bytes 3145736 | tf_op jit(solution)/shard_map/ppermute | solution.py:18
  67.0 12.3 %copy-start.32 = (s32[2,40]{1,0:T(2,128)}, s32[2,40]{1,0:T(2,128)S(1)}, u32[]{:S(2)}) copy-start(s32[2,40]{1,0:T(2,128)S(1)} %slice_convert_fusion.refs_4_.refs_3_) | copy-start | bytes 964
  67.0 12.3 %copy-start.34 = (s32[2,40]{1,0:T(2,128)}, s32[2,40]{1,0:T(2,128)S(1)}, u32[]{:S(2)}) copy-start(s32[2,40]{1,0:T(2,128)S(1)} %slice_convert_fusion.1.refs_3_.refs_1_.refs_2_) | copy-start | bytes 964
  68.8 13.1 %copy-start.3 = (bf16[5,2,4,128,256]{4,3,2,1,0:T(8,128)(2,1)S(1)}, bf16[5,2,4,128,256]{4,3,2,1,0:T(8,128)(2,1)}, u32[]{:S(2)}) copy-start(bf16[5,2,4,128,256]{4,3,2,1,0:T(8,128)(2,1)} %get-tuple-element.37.refs_5_.refs_4_) | copy-start | bytes 7864324
  81.2 28.1 %copy-start.22 = (s32[2,40]{1,0:T(2,128)}, s32[2,40]{1,0:T(2,128)S(1)}, u32[]{:S(2)}) copy-start(s32[2,40]{1,0:T(2,128)S(1)} %slice_convert_fusion.2.refs_3_.refs_4_) | copy-start | bytes 964
  81.9 27.3 %copy-start.24 = (s32[2,40]{1,0:T(2,128)}, s32[2,40]{1,0:T(2,128)S(1)}, u32[]{:S(2)}) copy-start(s32[2,40]{1,0:T(2,128)S(1)} %slice_convert_fusion.3.refs_2_.refs_0_) | copy-start | bytes 964
  81.9 22.5 %copy-start.20 = (bf16[2,1,2,128,256]{4,3,2,1,0:T(8,128)(2,1)S(1)}, bf16[2,1,2,128,256]{4,3,2,1,0:T(8,128)(2,1)}, u32[]{:S(2)}) copy-start(bf16[2,1,2,128,256]{4,3,2,1,0:T(8,128)(2,1)} %get-tuple-element.38.refs_4_) | copy-start | bytes 786436
  108.5 7.2 %collective-permute-start.13 = (f32[1,24,128,128]{3,2,1,0:T(8,128)S(1)}, f32[1,24,128,128]{3,2,1,0:T(8,128)}, u32[]{:S(2)}, u32[]{:S(2)}) collective-permute-start(f32[1,24,128,128]{3,2,1,0:T(8,128)S(1)} %get-tuple-element.51), channel_id=1, source_target_pairs={{0,1},{1,0},{2,3},{3,2},{4,5},{5,4},{6,7},{7,6},{8,9},{9,8},{10,11... | collective-permute-start | bytes 4718600 | tf_op jit(solution)/shard_map/ppermute | solution.py:22
  115.7 8.9 %collective-permute-start.10 = (f32[1,24,128,128]{3,2,1,0:T(8,128)}, f32[1,24,128,128]{3,2,1,0:T(8,128)}, u32[]{:S(2)}, u32[]{:S(2)}) collective-permute-start(f32[1,24,128,128]{3,2,1,0:T(8,128)} %get-tuple-element.47), channel_id=1, source_target_pairs={{0,1},{1,0},{2,3},{3,2},{4,5},{5,4},{6,7},{7,6},{8,9},{9,8},{10,11... | collective-permute-start | bytes 4718600 | tf_op jit(solution)/shard_map/ppermute | solution.py:22
  115.7 8.8 %copy-start.15 = (f32[1,24,128,128]{3,2,1,0:T(8,128)S(1)}, f32[1,24,128,128]{3,2,1,0:T(8,128)}, u32[]{:S(2)}) copy-start(f32[1,24,128,128]{3,2,1,0:T(8,128)} %copy-done.14) | copy-start | bytes 4718596
  117.4 41.2 %collective-permute-start.17 = (f32[3072,128]{1,0:T(8,128)S(1)}, f32[3072,128]{1,0:T(8,128)}, u32[]{:S(2)}, u32[]{:S(2)}) collective-permute-start(f32[3072,128]{1,0:T(8,128)S(1)} %bitcast.6), channel_id=1, source_target_pairs={{0,2},{2,4},{4,6},{6,8},{8,10},{10,12},{12,14},{14,16},{16,18},{18... | collective-permute-start | bytes 4718600 | tf_op jit(solution)/shard_map/ppermute | solution.py:18
  117.5 41.1 %collective-permute-start.18 = (f32[3072,128]{1,0:T(8,128)S(1)}, f32[3072,128]{1,0:T(8,128)}, u32[]{:S(2)}, u32[]{:S(2)}) collective-permute-start(f32[3072,128]{1,0:T(8,128)S(1)} %bitcast.7), channel_id=1, source_target_pairs={{0,126},{2,0},{4,2},{6,4},{8,6},{10,8},{12,10},{14,12},{16,14},{18... | collective-permute-start | bytes 4718600 | tf_op jit(solution)/shard_map/ppermute | solution.py:18
  127.4 38.1 %collective-permute-start.14 = (f32[2,12,128,128]{3,2,1,0:T(8,128)}, f32[2,12,128,128]{3,2,1,0:T(8,128)}, u32[]{:S(2)}, u32[]{:S(2)}) collective-permute-start(f32[2,12,128,128]{3,2,1,0:T(8,128)} %fusion), channel_id=1, source_target_pairs={{0,1},{1,0},{2,3},{3,2},{4,5},{5,4},{6,7},{7,6},{8,9},{9,8},{10,11... | collective-permute-start | bytes 4718600 | tf_op jit(solution)/shard_map/ppermute | solution.py:22
  128.3 64.0 %collective-permute-start.11 = (f32[3072,128]{1,0:T(8,128)S(1)}, f32[3072,128]{1,0:T(8,128)}, u32[]{:S(2)}, u32[]{:S(2)}) collective-permute-start(f32[3072,128]{1,0:T(8,128)S(1)} %bitcast.9), channel_id=1, source_target_pairs={{0,2},{2,4},{4,6},{6,8},{8,10},{10,12},{12,14},{14,16},{16,18},{18... | collective-permute-start | bytes 4718600 | tf_op jit(solution)/shard_map/ppermute | solution.py:18
  128.3 64.0 %collective-permute-start.12 = (f32[3072,128]{1,0:T(8,128)S(1)}, f32[3072,128]{1,0:T(8,128)}, u32[]{:S(2)}, u32[]{:S(2)}) collective-permute-start(f32[3072,128]{1,0:T(8,128)S(1)} %bitcast.10), channel_id=1, source_target_pairs={{0,126},{2,0},{4,2},{6,4},{8,6},{10,8},{12,10},{14,12},{16,14},{18... | collective-permute-start | bytes 4718600 | tf_op jit(solution)/shard_map/ppermute | solution.py:18
  135.2 11.4 %copy-start.27 = (s32[2]{0:T(128)S(1)}, s32[2]{0:T(128)}, u32[]{:S(2)}) copy-start(s32[2]{0:T(128)} %pad_add_fusion.1.meta.refs_0_) | copy-start | bytes 28
  135.2 11.4 %copy-start.29 = (s32[4,24]{1,0:T(4,128)S(1)}, s32[4,24]{1,0:T(4,128)}, u32[]{:S(2)}) copy-start(s32[4,24]{1,0:T(4,128)} %refs_1_.17) | copy-start | bytes 1156
  135.2 11.4 %copy-start.31 = (s32[2,40]{1,0:T(2,128)S(1)}, s32[2,40]{1,0:T(2,128)}, u32[]{:S(2)}) copy-start(s32[2,40]{1,0:T(2,128)} %copy-done.30) | copy-start | bytes 964
  156.0 11.3 %copy-start.11 = (f32[4,12,128,128]{3,2,1,0:T(8,128)}, f32[4,12,128,128]{3,2,1,0:T(8,128)S(1)}, u32[]{:S(2)}) copy-start(f32[4,12,128,128]{3,2,1,0:T(8,128)S(1)} %get-tuple-element.57.refs_9_) | copy-start | bytes 9437188
  156.0 11.3 %copy-start.12 = (f32[4,12,128,128]{3,2,1,0:T(8,128)}, f32[4,12,128,128]{3,2,1,0:T(8,128)S(1)}, u32[]{:S(2)}) copy-start(f32[4,12,128,128]{3,2,1,0:T(8,128)S(1)} %get-tuple-element.58.refs_10_) | copy-start | bytes 9437188
  158.7 67.3 %collective-permute-start.19 = (f32[3072,128]{1,0:T(8,128)}, f32[3072,128]{1,0:T(8,128)S(1)}, u32[]{:S(2)}, u32[]{:S(2)}) collective-permute-start(f32[3072,128]{1,0:T(8,128)} %collective-permute-done.17.refs_5_), channel_id=1, source_target_pairs={{0,2},{2,4},{4,6},{6,8},{8,10},{10,12},{12,14},{14,16},{16,18},{18... | collective-permute-start | bytes 4718600 | tf_op jit(solution)/shard_map/ppermute | solution.py:18
  158.7 68.4 %collective-permute-start.20 = (f32[3072,128]{1,0:T(8,128)}, f32[3072,128]{1,0:T(8,128)}, u32[]{:S(2)}, u32[]{:S(2)}) collective-permute-start(f32[3072,128]{1,0:T(8,128)} %collective-permute-done.18.refs_7_), channel_id=1, source_target_pairs={{0,126},{2,0},{4,2},{6,4},{8,6},{10,8},{12,10},{14,12},{16,14},{18... | collective-permute-start | bytes 4718600 | tf_op jit(solution)/shard_map/ppermute | solution.py:18
  167.3 32.0 %copy-start.1 = (bf16[5,2,4,128,256]{4,3,2,1,0:T(8,128)(2,1)S(1)}, bf16[5,2,4,128,256]{4,3,2,1,0:T(8,128)(2,1)}, u32[]{:S(2)}) copy-start(bf16[5,2,4,128,256]{4,3,2,1,0:T(8,128)(2,1)} %get-tuple-element.56.refs_3_.refs_4_) | copy-start | bytes 7864324
  167.3 32.0 %copy-start.33 = (s32[2,40]{1,0:T(2,128)S(1)}, s32[2,40]{1,0:T(2,128)}, u32[]{:S(2)}) copy-start(s32[2,40]{1,0:T(2,128)} %copy-done.32) | copy-start | bytes 964
  167.3 32.0 %copy-start.35 = (s32[2,40]{1,0:T(2,128)S(1)}, s32[2,40]{1,0:T(2,128)}, u32[]{:S(2)}) copy-start(s32[2,40]{1,0:T(2,128)} %copy-done.34) | copy-start | bytes 964
  169.4 57.8 %copy-start.23 = (s32[2,40]{1,0:T(2,128)S(1)}, s32[2,40]{1,0:T(2,128)}, u32[]{:S(2)}) copy-start(s32[2,40]{1,0:T(2,128)} %copy-done.22) | copy-start | bytes 964
  169.4 57.8 %copy-start.25 = (s32[2,40]{1,0:T(2,128)S(1)}, s32[2,40]{1,0:T(2,128)}, u32[]{:S(2)}) copy-start(s32[2,40]{1,0:T(2,128)} %copy-done.24) | copy-start | bytes 964
  192.4 67.3 %collective-permute-start.15 = (f32[3072,128]{1,0:T(8,128)}, f32[3072,128]{1,0:T(8,128)S(1)}, u32[]{:S(2)}, u32[]{:S(2)}) collective-permute-start(f32[3072,128]{1,0:T(8,128)} %collective-permute-done.11.refs_6_), channel_id=1, source_target_pairs={{0,2},{2,4},{4,6},{6,8},{8,10},{10,12},{12,14},{14,16},{16,18},{18... | collective-permute-start | bytes 4718600 | tf_op jit(solution)/shard_map/ppermute | solution.py:18
  192.4 67.3 %collective-permute-start.16 = (f32[3072,128]{1,0:T(8,128)}, f32[3072,128]{1,0:T(8,128)S(1)}, u32[]{:S(2)}, u32[]{:S(2)}) collective-permute-start(f32[3072,128]{1,0:T(8,128)} %collective-permute-done.12.refs_8_), channel_id=1, source_target_pairs={{0,126},{2,0},{4,2},{6,4},{8,6},{10,8},{12,10},{14,12},{16,14},{18... | collective-permute-start | bytes 4718600 | tf_op jit(solution)/shard_map/ppermute | solution.py:18
  230.4 29.3 %copy-start.18 = (bf16[2,1,3,128,256]{4,3,2,1,0:T(8,128)(2,1)S(1)}, bf16[2,1,3,128,256]{4,3,2,1,0:T(8,128)(2,1)}, u32[]{:S(2)}) copy-start(bf16[2,1,3,128,256]{4,3,2,1,0:T(8,128)(2,1)} %get-tuple-element.53.refs_4_) | copy-start | bytes 1179652
  265.4 5.5 %collective-permute-start.21 = (f32[3,12,128,128]{3,2,1,0:T(8,128)S(1)}, f32[3,12,128,128]{3,2,1,0:T(8,128)S(1)}, u32[]{:S(2)}, u32[]{:S(2)}) collective-permute-start(f32[3,12,128,128]{3,2,1,0:T(8,128)S(1)} %get-tuple-element.66), channel_id=1, source_target_pairs={{0,1},{1,0},{2,3},{3,2},{4,5},{5,4},{6,7},{7,6},{8,9},{9,8},{10,11... | collective-permute-start | bytes 7077896 | tf_op jit(solution)/shard_map/ppermute | solution.py:22
  270.2 2.4 collective-permute-start.22
  (14 other events, 52.1 us)

commit v6 on v5

--- a/solution.py
+++ b/solution.py
@@ -124,7 +124,8 @@
     refs = refs[5:]
     held = sources if direct else [refs.pop(0) for _ in sources]
     acc = acc_sources if direct else [refs.pop(0) for _ in acc_sources]
-    outs = results if straight else refs
+    staged = by_rows and direct
+    outs = [refs[0], results[1]] if staged else results if straight else refs
     copies = []
 
     def start(source, target):
@@ -205,7 +206,7 @@
     kept_cols = outs[0].shape[1]
     places = [(portion, row) for portion, number in enumerate(portions) for row in range(number)]
     leaving = []
-    for which in (1, 0):
+    for which in (0, 1) if staged else (1, 0):
         side = core if which == 0 else 1 - core
         for row, (portion, local) in enumerate(places):
             source = side * len(places) + row if by_rows else row
@@ -220,7 +221,7 @@
                 return carry
 
             lax.fori_loop(0, kept_cols, out_body, 0, unroll=4)
-            if not straight:
+            if not straight or (staged and which == 0):
                 leaving.append(start(own, results[portion].at[local]))
     for copy in leaving:
         copy.wait()
@@ -229,6 +230,7 @@
 SMEM = pl.BlockSpec(memory_space=pltpu.SMEM)
 VMEM = pl.BlockSpec(memory_space=pltpu.VMEM)
 HERE = pl.BlockSpec(memory_space=pl.ANY)
+FAR = pl.BlockSpec(memory_space=pltpu.HBM)
 PARAMS = pltpu.CompilerParams(vmem_limit_bytes=60 << 20)
 
 
@@ -265,6 +267,10 @@
         held += [pltpu.VMEM(a.shape, F32) for a in acc]
     else:
         held = []
+    staged = by_rows and part is not None
+    in_vmem = [straight and not (staged and i == 0) for i in range(len(shapes))]
+    if staged:
+        held += [pltpu.VMEM(shapes[0], F32)]
     if not straight:
         held += [pltpu.VMEM(shape, F32) for shape in shapes]
     used = sum(math.prod(ref.shape) * jnp.dtype(ref.dtype).itemsize for ref in scratch + held)
@@ -272,9 +278,12 @@
     return pl.pallas_call(
         kernel,
         name=name,
-        out_shape=[pltpu.VMEM(shape, F32) if straight else jax.ShapeDtypeStruct(shape, F32) for shape in shapes],
+        out_shape=[
+            (pltpu.VMEM if inside else pltpu.HBM)(shape, F32) if straight else jax.ShapeDtypeStruct(shape, F32)
+            for shape, inside in zip(shapes, in_vmem)
+        ],
         in_specs=[SMEM] * (2 + len(gs)) + [HERE] + [HERE if part is None else VMEM] * (len(blocks) + len(acc)),
-        out_specs=[VMEM if straight else HERE] * len(shapes),
+        out_specs=[VMEM if inside else FAR if straight else HERE for inside in in_vmem],
         scratch_shapes=scratch + [pltpu.SemaphoreType.DMA((copies,))] + held,
         compiler_params=pltpu.CompilerParams(vmem_limit_bytes=used + (6 << 20)),
         cost_estimate=pl.CostEstimate(flops=0, transcendentals=0, bytes_accessed=0),

time: 275 us -> 275 us (level)
    unnamed x78 -> x76, local copies, waits for them, and re-layouts: 10.8 us -> 9.69 us
where the time goes in v6:
time: 275 us; the launch traced here: 274 us
  waiting for transfers between devices  109 us (40%)
  Pallas kernels  80.3 us (29%)
  starting transfers between devices  61.2 us (22%)
  local copies, waits for them, and re-layouts  11.7 us (4%)
  other arithmetic  11.4 us (4%)
    ppermute x16, waiting for transfers between devices, ring(): lax.ppermute(array, 'rows', [(i, (i + by) % devices) for i in range(devic...  106 us
    pallas_call x9, Pallas kernels, stage(): pl.pallas_call(kernel, name=name, out_shape=[(pltpu.VMEM if inside else p...  63.3 us
    ppermute x16, starting transfers between devices, ring(): lax.ppermute(array, 'rows', [(i, (i + by) % devices) for i in range(devic...  56.2 us
    pallas_call x2, Pallas kernels, left_call(): pl.pallas_call(kernel, name=name, out_shape=[out, *last], in_specs=[SMEM]...  17 us
    unnamed x76, local copies, waits for them, and re-layouts  9.69 us
  transfers between devices with their start and end apart: 23, of which 12 were waited for; matrix products, arithmetic and copies ran while one was open for 5% of the time, Pallas kernels for 25%

profile of v6, /device:TPU:1, one launch (start us, length us, event | category | flops | bytes accessed | tf_op | source)
XLA Modules:
  0.0 274.5 jit_solution(6102743267748357620)
XLA Ops:
  0.6 1.5 collective-permute-start.3
  2.1 0.8 pad_add_fusion
  2.9 1.7 constant_dynamic-slice_fusion
  4.7 1.4 collective-permute-start
  6.1 7.3 %collective-permute-start.1 = (f32[2056,128]{1,0:T(8,128)S(1)}, f32[2056,128]{1,0:T(8,128)}, u32[]{:S(2)}, u32[]{:S(2)}) collective-permute-start(f32[2056,128]{1,0:T(8,128)S(1)} %select_maximum_fusion.refs_6_.refs_9_), channel_id=1, source_target_pairs={{0,126},{2,0},{4,2},{6,4},{8,6},{10,8},{12,10},{14,12},{16,14},{18... | collective-permute-start | bytes 3158024 | tf_op jit(solution)/shard_map/ppermute | solution.py:18
  13.7 0.8 collective-permute-done.2.cols_b
  14.5 6.0 %collective-permute-start.8 = (f32[2048,128]{1,0:T(8,128)S(1)}, f32[2048,128]{1,0:T(8,128)}, u32[]{:S(2)}, u32[]{:S(2)}) collective-permute-start(f32[2048,128]{1,0:T(8,128)S(1)} %bitcast.13), channel_id=1, source_target_pairs={{0,126},{2,0},{4,2},{6,4},{8,6},{10,8},{12,10},{14,12},{16,14},{18... | collective-permute-start | bytes 3145736 | tf_op jit(solution)/shard_map/ppermute | solution.py:18
  21.2 5.6 %margin_left.1 = (bf16[5,2,4,128,256]{4,3,2,1,0:T(8,128)(2,1)}, bf16[2,1,2,128,256]{4,3,2,1,0:T(8,128)(2,1)}, bf16[2,1,2,128,256]{4,3,2,1,0:T(8,128)(2,1)}) custom-call(s32[2]{0:T(128)} %pad_add_fusion.1.meta.refs_0_, s32[4,8]{1,0:T(4,128)} %cols_a.1, s32[4,8]{1,0:T(4,128)} %copy-done.37, f32[4,8,128,128]{3,2,1,0:T(8,128)} %table_a.1, ...), custom_call_target="tpu_custom_call" | custom-call | tf_op jit(solution)/shard_map/margin_left/pallas_call | solution.py:298
  26.8 10.1 %collective-permute-done.refs_8_.refs_7_ = f32[2056,128]{1,0:T(8,128)S(1)} collective-permute-done((f32[2056,128]{1,0:T(8,128)S(1)}, f32[2056,128]{1,0:T(8,128)S(1)}, u32[]{:S(2)}, u32[]{:S(2)}) %collective-permute-start) | collective-permute-done | bytes 1052704 | tf_op jit(solution)/shard_map/ppermute | solution.py:18
  36.9 6.9 %collective-permute-start.5 = (f32[2056,128]{1,0:T(8,128)}, f32[2056,128]{1,0:T(8,128)S(1)}, u32[]{:S(2)}, u32[]{:S(2)}) collective-permute-start(f32[2056,128]{1,0:T(8,128)} %collective-permute-done.1.refs_10_.refs_11_), channel_id=1, source_target_pairs={{0,126},{2,0},{4,2},{6,4},{8,6},{10,8},{12,10},{14,12},{16,14},{18... | collective-permute-start | bytes 3158024 | tf_op jit(solution)/shard_map/ppermute | solution.py:18
  43.7 15.7 %collective-permute-done.6.refs_9_.refs_8_ = f32[2048,128]{1,0:T(8,128)} collective-permute-done((f32[2048,128]{1,0:T(8,128)S(1)}, f32[2048,128]{1,0:T(8,128)}, u32[]{:S(2)}, u32[]{:S(2)}) %collective-permute-start.6) | collective-permute-done | bytes 1048608 | tf_op jit(solution)/shard_map/ppermute | solution.py:18
  59.5 6.9 %collective-permute-start.9 = (f32[2048,128]{1,0:T(8,128)}, f32[2048,128]{1,0:T(8,128)S(1)}, u32[]{:S(2)}, u32[]{:S(2)}) collective-permute-start(f32[2048,128]{1,0:T(8,128)} %collective-permute-done.8.refs_11_.refs_12_), channel_id=1, source_target_pairs={{0,126},{2,0},{4,2},{6,4},{8,6},{10,8},{12,10},{14,12},{16,14},{18... | collective-permute-start | bytes 3145736 | tf_op jit(solution)/shard_map/ppermute | solution.py:18
  67.1 1.7 copy-done.2
  68.8 10.4 %product_near.1 = (f32[2,24,128,128]{3,2,1,0:T(8,128)S(1)}, f32[2,24,128,128]{3,2,1,0:T(8,128)S(1)}) custom-call(s32[2]{0:T(128)S(1)} %copy-done.24, s32[4,24]{1,0:T(4,128)S(1)} %copy-done.26, s32[2,40]{1,0:T(2,128)S(1)} %get-tuple-element.73.refs_2_, s32[2,40]{1,0:T(2,128)S(1)} %slice_convert_fusion.1.refs_3_.refs_1_.refs_2_, ...), custom_call_target="tpu_custom_call" | custom-call | tf_op jit(solution)/shard_map/product_near/pallas_call | solution.py:278
  79.3 1.8 collective-permute-done.5.refs_6_.refs_13_
  81.2 0.7 collective-permute-done.4.refs_5_
  81.9 6.1 %product_far0.1 = (f32[1,24,128,128]{3,2,1,0:T(8,128)S(1)}, f32[1,24,128,128]{3,2,1,0:T(8,128)S(1)}, f32[1,24,128,128]{3,2,1,0:T(8,128)S(1)}, f32[1,24,128,128]{3,2,1,0:T(8,128)S(1)}) custom-call(s32[2]{0:T(128)S(1)} %copy-done.24, s32[4,24]{1,0:T(4,128)S(1)} %copy-done.26, s32[2,40]{1,0:T(2,128)S(1)} %slice_convert_fusion.3.refs_2_.refs_0_, ...), custom_call_target="tpu_custom_call" | custom-call | tf_op jit(solution)/shard_map/product_far0/pallas_call | solution.py:278
  88.1 16.3 %collective-permute-done.7.refs_5_.refs_6_ = f32[2048,128]{1,0:T(8,128)S(1)} collective-permute-done((f32[2048,128]{1,0:T(8,128)}, f32[2048,128]{1,0:T(8,128)S(1)}, u32[]{:S(2)}, u32[]{:S(2)}) %collective-permute-start.7) | collective-permute-done | bytes 1048608 | tf_op jit(solution)/shard_map/ppermute | solution.py:18
  104.4 5.1 %product_far1.3 = (f32[1,24,128,128]{3,2,1,0:T(8,128)}, f32[1,24,128,128]{3,2,1,0:T(8,128)S(1)}) custom-call(s32[2]{0:T(128)S(1)} %copy-done.24, s32[4,24]{1,0:T(4,128)S(1)} %copy-done.26, s32[2,40]{1,0:T(2,128)S(1)} %slice_convert_fusion.3.refs_2_.refs_0_, s32[2,40]{1,0:T(2,128)S(1)} %slice_convert_fusion.2.refs_3_.refs_4_, ...), custom_call_target="tpu_custom_call" | custom-call | tf_op jit(solution)/shard_map/product_far1/pallas_call | solution.py:278
  109.5 0.7 collective-permute-start.13
  110.2 5.1 %product_far1.2 = (f32[1,24,128,128]{3,2,1,0:T(8,128)}, f32[1,24,128,128]{3,2,1,0:T(8,128)S(1)}) custom-call(s32[2]{0:T(128)S(1)} %copy-done.24, s32[4,24]{1,0:T(4,128)S(1)} %copy-done.26, s32[2,40]{1,0:T(2,128)S(1)} %slice_convert_fusion.3.refs_2_.refs_0_, s32[2,40]{1,0:T(2,128)S(1)} %slice_convert_fusion.2.refs_3_.refs_4_, ...), custom_call_target="tpu_custom_call" | custom-call | tf_op jit(solution)/shard_map/product_far1/pallas_call | solution.py:278
  115.4 2.2 add.39
  117.7 7.0 %collective-permute-start.18 = (f32[3072,128]{1,0:T(8,128)S(1)}, f32[3072,128]{1,0:T(8,128)}, u32[]{:S(2)}, u32[]{:S(2)}) collective-permute-start(f32[3072,128]{1,0:T(8,128)S(1)} %bitcast.7), channel_id=1, source_target_pairs={{0,126},{2,0},{4,2},{6,4},{8,6},{10,8},{12,10},{14,12},{16,14},{18... | collective-permute-start | bytes 4718600 | tf_op jit(solution)/shard_map/ppermute | solution.py:18
  124.7 1.6 add.38
  126.4 1.3 fusion
  127.6 0.9 collective-permute-start.14
  128.5 6.9 %collective-permute-start.12 = (f32[3072,128]{1,0:T(8,128)S(1)}, f32[3072,128]{1,0:T(8,128)}, u32[]{:S(2)}, u32[]{:S(2)}) collective-permute-start(f32[3072,128]{1,0:T(8,128)S(1)} %bitcast.10), channel_id=1, source_target_pairs={{0,126},{2,0},{4,2},{6,4},{8,6},{10,8},{12,10},{14,12},{16,14},{18... | collective-permute-start | bytes 4718600 | tf_op jit(solution)/shard_map/ppermute | solution.py:18
  135.4 11.4 %factor_left.1 = (bf16[5,2,4,128,256]{4,3,2,1,0:T(8,128)(2,1)}, bf16[2,1,3,128,256]{4,3,2,1,0:T(8,128)(2,1)}, bf16[2,1,1,128,256]{4,3,2,1,0:T(8,128)(2,1)}) custom-call(s32[2]{0:T(128)} %pad_add_fusion.1.meta.refs_0_, s32[2,40]{1,0:T(2,128)} %copy-done.22, s32[2,40]{1,0:T(2,128)} %copy-done.32, s32[2,40]{1,0:T(2,128)} %copy-done.28, s32[2,40]{1,0:T(2,128)} %copy-done.30, ...), custom_call_target="tpu_custom_call" | custom-call | tf_op jit(solution)/shard_map/factor_left/pallas_call | solution.py:298
  146.9 1.7 copy-done
  148.6 7.6 %metric_own.1 = (f32[4,12,128,128]{3,2,1,0:T(8,128)S(1)}, f32[4,12,128,128]{3,2,1,0:T(8,128)S(1)}) custom-call(s32[2]{0:T(128)S(1)} %copy-done.25, s32[4,24]{1,0:T(4,128)S(1)} %copy-done.27, s32[2,40]{1,0:T(2,128)S(1)} %copy-done.29, bf16[5,2,4,128,256]{4,3,2,1,0:T(8,128)(2,1)S(1)} %copy-done, f32[3072,128]{1,0:T(8,128)S(1)} %bitcast.8, f32[3072,128]{1,0:T(8,128)S(1)} %bitcast.11), custom_call_target="tpu_custom_call" | custom-call | tf_op jit(solution)/shard_map/metric_own/pallas_call | solution.py:278
  156.2 2.7 collective-permute-done.17.refs_5_
  158.8 6.9 %collective-permute-start.20 = (f32[3072,128]{1,0:T(8,128)}, f32[3072,128]{1,0:T(8,128)}, u32[]{:S(2)}, u32[]{:S(2)}) collective-permute-start(f32[3072,128]{1,0:T(8,128)} %collective-permute-done.18.refs_7_), channel_id=1, source_target_pairs={{0,126},{2,0},{4,2},{6,4},{8,6},{10,8},{12,10},{14,12},{16,14},{18... | collective-permute-start | bytes 4718600 | tf_op jit(solution)/shard_map/ppermute | solution.py:18
  165.7 1.7 broadcast_select_fusion.1
  167.5 2.0 pad_maximum_fusion
  169.5 23.0 %collective-permute-done.11.refs_6_ = f32[3072,128]{1,0:T(8,128)} collective-permute-done((f32[3072,128]{1,0:T(8,128)S(1)}, f32[3072,128]{1,0:T(8,128)}, u32[]{:S(2)}, u32[]{:S(2)}) %collective-permute-start.11) | collective-permute-done | bytes 1572896 | tf_op jit(solution)/shard_map/ppermute | solution.py:18
  192.5 6.9 %collective-permute-start.16 = (f32[3072,128]{1,0:T(8,128)}, f32[3072,128]{1,0:T(8,128)S(1)}, u32[]{:S(2)}, u32[]{:S(2)}) collective-permute-start(f32[3072,128]{1,0:T(8,128)} %collective-permute-done.12.refs_8_), channel_id=1, source_target_pairs={{0,126},{2,0},{4,2},{6,4},{8,6},{10,8},{12,10},{14,12},{16,14},{18... | collective-permute-start | bytes 4718600 | tf_op jit(solution)/shard_map/ppermute | solution.py:18
  199.4 12.9 %metric_near.1 = (f32[4,12,128,128]{3,2,1,0:T(8,128)S(1)}, f32[4,12,128,128]{3,2,1,0:T(8,128)}) custom-call(s32[2]{0:T(128)S(1)} %copy-done.25, s32[4,24]{1,0:T(4,128)S(1)} %copy-done.27, s32[2,40]{1,0:T(2,128)S(1)} %copy-done.33, s32[2,40]{1,0:T(2,128)S(1)} %copy-done.31, bf16[5,2,4,128,256]{4,3,2,1,0:T(8,128)(2,1)S(1)} %copy-done.1, ...), custom_call_target="tpu_custom_call" | custom-call | tf_op jit(solution)/shard_map/metric_near/pallas_call | solution.py:278
  212.3 13.8 %collective-permute-done.19.refs_5_ = f32[3072,128]{1,0:T(8,128)S(1)} collective-permute-done((f32[3072,128]{1,0:T(8,128)}, f32[3072,128]{1,0:T(8,128)S(1)}, u32[]{:S(2)}, u32[]{:S(2)}) %collective-permute-start.19) | collective-permute-done | bytes 1572896 | tf_op jit(solution)/shard_map/ppermute | solution.py:18
  226.1 1.1 copy-done.14
  227.3 1.9 copy-done.13
  229.2 1.4 copy-done.15
  230.6 7.0 %metric_far0.1 = (f32[3,12,128,128]{3,2,1,0:T(8,128)S(1)}, f32[1,12,128,128]{3,2,1,0:T(8,128)S(1)}, f32[3,12,128,128]{3,2,1,0:T(8,128)S(1)}, f32[1,12,128,128]{3,2,1,0:T(8,128)S(1)}) custom-call(s32[2]{0:T(128)S(1)} %copy-done.25, s32[4,24]{1,0:T(4,128)S(1)} %copy-done.27, s32[2,40]{1,0:T(2,128)S(1)} %copy-done.23, s32[2,40]{1,0:T(2,128)S(1)} %copy-done.21, ...), custom_call_target="tpu_custom_call" | custom-call | tf_op jit(solution)/shard_map/metric_far0/pallas_call | solution.py:278
  237.6 22.3 %collective-permute-done.15.refs_5_ = f32[3072,128]{1,0:T(8,128)S(1)} collective-permute-done((f32[3072,128]{1,0:T(8,128)}, f32[3072,128]{1,0:T(8,128)S(1)}, u32[]{:S(2)}, u32[]{:S(2)}) %collective-permute-start.15) | collective-permute-done | bytes 1572896 | tf_op jit(solution)/shard_map/ppermute | solution.py:18
  259.9 5.7 %metric_far1.2 = (f32[3,12,128,128]{3,2,1,0:T(8,128)S(1)}, f32[3,12,128,128]{3,2,1,0:T(8,128)S(1)}) custom-call(s32[2]{0:T(128)S(1)} %copy-done.25, s32[4,24]{1,0:T(4,128)S(1)} %copy-done.27, s32[2,40]{1,0:T(2,128)S(1)} %copy-done.23, s32[2,40]{1,0:T(2,128)S(1)} %copy-done.21, bf16[2,1,3,128,256]{4,3,2,1,0:T(8,128)(2,1)S(1)} %copy-done.16, ...), custom_call_target="tpu_custom_call" | custom-call | tf_op jit(solution)/shard_map/metric_far1/pallas_call | solution.py:278
  265.6 1.3 collective-permute-start.21
  266.9 3.4 %metric_far1.3 = (f32[1,12,128,128]{3,2,1,0:T(8,128)S(1)}, f32[1,12,128,128]{3,2,1,0:T(8,128)S(1)}) custom-call(s32[2]{0:T(128)S(1)} %copy-done.25, s32[4,24]{1,0:T(4,128)S(1)} %copy-done.27, s32[2,40]{1,0:T(2,128)S(1)} %copy-done.23, s32[2,40]{1,0:T(2,128)S(1)} %copy-done.21, bf16[2,1,1,128,256]{4,3,2,1,0:T(8,128)(2,1)S(1)} %copy-done.19, ...), custom_call_target="tpu_custom_call" | custom-call | tf_op jit(solution)/shard_map/metric_far1/pallas_call | solution.py:278
  271.8 1.0 collective-permute-done.22
  272.8 1.7 copy-done.34
  (102 shorter events, 3.6 us)
Async XLA Ops:
  0.6 20.6 %collective-permute-start.3 = (f32[4,8,128,128]{3,2,1,0:T(8,128)}, f32[4,8,128,128]{3,2,1,0:T(8,128)}, u32[]{:S(2)}, u32[]{:S(2)}) collective-permute-start(f32[4,8,128,128]{3,2,1,0:T(8,128)} %table_a.1), channel_id=1, source_target_pairs={{0,1},{1,0},{2,3},{3,2},{4,5},{5,4},{6,7},{7,6},{8,9},{9,8},{10,11... | collective-permute-start | bytes 6291464 | tf_op jit(solution)/shard_map/ppermute | solution.py:22
  2.9 64.1 %copy-start.28 = (s32[2,40]{1,0:T(2,128)}, s32[2,40]{1,0:T(2,128)S(1)}, u32[]{:S(2)}) copy-start(s32[2,40]{1,0:T(2,128)S(1)} %get-tuple-element.73.refs_2_) | copy-start | bytes 964
  4.6 62.4 %copy-start.5 = (f32[1,16,128,128]{3,2,1,0:T(8,128)}, f32[1,16,128,128]{3,2,1,0:T(8,128)S(1)}, u32[]{:S(2)}) copy-start(f32[1,16,128,128]{3,2,1,0:T(8,128)S(1)} %get-tuple-element.76) | copy-start | bytes 3145732
  4.6 8.7 %copy-start.36 = (s32[4,8]{1,0:T(4,128)S(1)}, s32[4,8]{1,0:T(4,128)}, u32[]{:S(2)}) copy-start(s32[4,8]{1,0:T(4,128)} %cols_a.1) | copy-start | bytes 388
  4.7 62.3 %copy-start.4 = (f32[2056,128]{1,0:T(8,128)}, f32[2056,128]{1,0:T(8,128)S(1)}, u32[]{:S(2)}) copy-start(f32[2056,128]{1,0:T(8,128)S(1)} %select_maximum_fusion.refs_6_.refs_9_) | copy-start | bytes 3158020
  4.7 32.2 %collective-permute-start = (f32[2056,128]{1,0:T(8,128)S(1)}, f32[2056,128]{1,0:T(8,128)S(1)}, u32[]{:S(2)}, u32[]{:S(2)}) collective-permute-start(f32[2056,128]{1,0:T(8,128)S(1)} %select_maximum_fusion.refs_6_.refs_9_), channel_id=1, source_target_pairs={{0,2},{2,4},{4,6},{6,8},{8,10},{10,12},{12,14},{14,16},{16,18},{18... | collective-permute-start | bytes 3158024 | tf_op jit(solution)/shard_map/ppermute | solution.py:18
  6.1 30.8 %collective-permute-start.1 = (f32[2056,128]{1,0:T(8,128)S(1)}, f32[2056,128]{1,0:T(8,128)}, u32[]{:S(2)}, u32[]{:S(2)}) collective-permute-start(f32[2056,128]{1,0:T(8,128)S(1)} %select_maximum_fusion.refs_6_.refs_9_), channel_id=1, source_target_pairs={{0,126},{2,0},{4,2},{6,4},{8,6},{10,8},{12,10},{14,12},{16,14},{18... | collective-permute-start | bytes 3158024 | tf_op jit(solution)/shard_map/ppermute | solution.py:18
  13.4 1.2 collective-permute-start.2
  13.7 45.8 %collective-permute-start.6 = (f32[2048,128]{1,0:T(8,128)S(1)}, f32[2048,128]{1,0:T(8,128)}, u32[]{:S(2)}, u32[]{:S(2)}) collective-permute-start(f32[2048,128]{1,0:T(8,128)S(1)} %bitcast.12), channel_id=1, source_target_pairs={{0,2},{2,4},{4,6},{6,8},{8,10},{10,12},{12,14},{14,16},{16,18},{18... | collective-permute-start | bytes 3145736 | tf_op jit(solution)/shard_map/ppermute | solution.py:18
  14.5 44.9 %collective-permute-start.8 = (f32[2048,128]{1,0:T(8,128)S(1)}, f32[2048,128]{1,0:T(8,128)}, u32[]{:S(2)}, u32[]{:S(2)}) collective-permute-start(f32[2048,128]{1,0:T(8,128)S(1)} %bitcast.13), channel_id=1, source_target_pairs={{0,126},{2,0},{4,2},{6,4},{8,6},{10,8},{12,10},{14,12},{16,14},{18... | collective-permute-start | bytes 3145736 | tf_op jit(solution)/shard_map/ppermute | solution.py:18
  21.2 45.9 %copy-start.24 = (s32[2]{0:T(128)S(1)}, s32[2]{0:T(128)}, u32[]{:S(2)}) copy-start(s32[2]{0:T(128)} %pad_add_fusion.1.meta.refs_0_) | copy-start | bytes 28
  21.2 45.9 %copy-start.26 = (s32[4,24]{1,0:T(4,128)S(1)}, s32[4,24]{1,0:T(4,128)}, u32[]{:S(2)}) copy-start(s32[4,24]{1,0:T(4,128)} %refs_1_.12) | copy-start | bytes 1156
  36.9 42.4 %copy-start.8 = (f32[2056,128]{1,0:T(8,128)}, f32[2056,128]{1,0:T(8,128)S(1)}, u32[]{:S(2)}) copy-start(f32[2056,128]{1,0:T(8,128)S(1)} %collective-permute-done.refs_8_.refs_7_) | copy-start | bytes 3158020
  36.9 44.3 %collective-permute-start.5 = (f32[2056,128]{1,0:T(8,128)}, f32[2056,128]{1,0:T(8,128)S(1)}, u32[]{:S(2)}, u32[]{:S(2)}) collective-permute-start(f32[2056,128]{1,0:T(8,128)} %collective-permute-done.1.refs_10_.refs_11_), channel_id=1, source_target_pairs={{0,126},{2,0},{4,2},{6,4},{8,6},{10,8},{12,10},{14,12},{16,14},{18... | collective-permute-start | bytes 3158024 | tf_op jit(solution)/shard_map/ppermute | solution.py:18
  43.7 38.2 %collective-permute-start.4 = (f32[2056,128]{1,0:T(8,128)S(1)}, f32[2056,128]{1,0:T(8,128)S(1)}, u32[]{:S(2)}, u32[]{:S(2)}) collective-permute-start(f32[2056,128]{1,0:T(8,128)S(1)} %collective-permute-done.refs_8_.refs_7_), channel_id=1, source_target_pairs={{0,2},{2,4},{4,6},{6,8},{8,10},{10,12},{12,14},{14,16},{16,18},{18... | collective-permute-start | bytes 3158024 | tf_op jit(solution)/shard_map/ppermute | solution.py:18
  59.4 44.9 %collective-permute-start.7 = (f32[2048,128]{1,0:T(8,128)}, f32[2048,128]{1,0:T(8,128)S(1)}, u32[]{:S(2)}, u32[]{:S(2)}) collective-permute-start(f32[2048,128]{1,0:T(8,128)} %collective-permute-done.6.refs_9_.refs_8_), channel_id=1, source_target_pairs={{0,2},{2,4},{4,6},{6,8},{8,10},{10,12},{12,14},{14,16},{16,18},{18... | collective-permute-start | bytes 3145736 | tf_op jit(solution)/shard_map/ppermute | solution.py:18
  59.5 44.9 %collective-permute-start.9 = (f32[2048,128]{1,0:T(8,128)}, f32[2048,128]{1,0:T(8,128)S(1)}, u32[]{:S(2)}, u32[]{:S(2)}) collective-permute-start(f32[2048,128]{1,0:T(8,128)} %collective-permute-done.8.refs_11_.refs_12_), channel_id=1, source_target_pairs={{0,126},{2,0},{4,2},{6,4},{8,6},{10,8},{12,10},{14,12},{16,14},{18... | collective-permute-start | bytes 3145736 | tf_op jit(solution)/shard_map/ppermute | solution.py:18
  67.0 12.3 %copy-start.30 = (s32[2,40]{1,0:T(2,128)}, s32[2,40]{1,0:T(2,128)S(1)}, u32[]{:S(2)}) copy-start(s32[2,40]{1,0:T(2,128)S(1)} %slice_convert_fusion.refs_4_.refs_3_) | copy-start | bytes 964
  67.0 12.3 %copy-start.32 = (s32[2,40]{1,0:T(2,128)}, s32[2,40]{1,0:T(2,128)S(1)}, u32[]{:S(2)}) copy-start(s32[2,40]{1,0:T(2,128)S(1)} %slice_convert_fusion.1.refs_3_.refs_1_.refs_2_) | copy-start | bytes 964
  68.8 13.1 %copy-start.3 = (bf16[5,2,4,128,256]{4,3,2,1,0:T(8,128)(2,1)S(1)}, bf16[5,2,4,128,256]{4,3,2,1,0:T(8,128)(2,1)}, u32[]{:S(2)}) copy-start(bf16[5,2,4,128,256]{4,3,2,1,0:T(8,128)(2,1)} %get-tuple-element.37.refs_5_.refs_4_) | copy-start | bytes 7864324
  81.2 29.0 %copy-start.20 = (s32[2,40]{1,0:T(2,128)}, s32[2,40]{1,0:T(2,128)S(1)}, u32[]{:S(2)}) copy-start(s32[2,40]{1,0:T(2,128)S(1)} %slice_convert_fusion.2.refs_3_.refs_4_) | copy-start | bytes 964
  81.9 28.3 %copy-start.22 = (s32[2,40]{1,0:T(2,128)}, s32[2,40]{1,0:T(2,128)S(1)}, u32[]{:S(2)}) copy-start(s32[2,40]{1,0:T(2,128)S(1)} %slice_convert_fusion.3.refs_2_.refs_0_) | copy-start | bytes 964
  81.9 22.5 %copy-start.18 = (bf16[2,1,2,128,256]{4,3,2,1,0:T(8,128)(2,1)S(1)}, bf16[2,1,2,128,256]{4,3,2,1,0:T(8,128)(2,1)}, u32[]{:S(2)}) copy-start(bf16[2,1,2,128,256]{4,3,2,1,0:T(8,128)(2,1)} %get-tuple-element.38.refs_4_) | copy-start | bytes 786436
  109.5 5.9 %collective-permute-start.13 = (f32[1,24,128,128]{3,2,1,0:T(8,128)S(1)}, f32[1,24,128,128]{3,2,1,0:T(8,128)}, u32[]{:S(2)}, u32[]{:S(2)}) collective-permute-start(f32[1,24,128,128]{3,2,1,0:T(8,128)S(1)} %get-tuple-element.51), channel_id=1, source_target_pairs={{0,1},{1,0},{2,3},{3,2},{4,5},{5,4},{6,7},{7,6},{8,9},{9,8},{10,11... | collective-permute-start | bytes 4718600 | tf_op jit(solution)/shard_map/ppermute | solution.py:22
  115.3 9.4 %collective-permute-start.10 = (f32[1,24,128,128]{3,2,1,0:T(8,128)S(1)}, f32[1,24,128,128]{3,2,1,0:T(8,128)}, u32[]{:S(2)}, u32[]{:S(2)}) collective-permute-start(f32[1,24,128,128]{3,2,1,0:T(8,128)S(1)} %get-tuple-element.47), channel_id=1, source_target_pairs={{0,1},{1,0},{2,3},{3,2},{4,5},{5,4},{6,7},{7,6},{8,9},{9,8},{10,11... | collective-permute-start | bytes 4718600 | tf_op jit(solution)/shard_map/ppermute | solution.py:22
  115.4 9.3 %copy-start.35 = (f32[1,24,128,128]{3,2,1,0:T(8,128)S(1)}, f32[1,24,128,128]{3,2,1,0:T(8,128)}, u32[]{:S(2)}) copy-start(f32[1,24,128,128]{3,2,1,0:T(8,128)} %get-tuple-element.46) | copy-start | bytes 4718596
  117.6 41.2 %collective-permute-start.17 = (f32[3072,128]{1,0:T(8,128)S(1)}, f32[3072,128]{1,0:T(8,128)}, u32[]{:S(2)}, u32[]{:S(2)}) collective-permute-start(f32[3072,128]{1,0:T(8,128)S(1)} %bitcast.6), channel_id=1, source_target_pairs={{0,2},{2,4},{4,6},{6,8},{8,10},{10,12},{12,14},{14,16},{16,18},{18... | collective-permute-start | bytes 4718600 | tf_op jit(solution)/shard_map/ppermute | solution.py:18
  117.7 41.1 %collective-permute-start.18 = (f32[3072,128]{1,0:T(8,128)S(1)}, f32[3072,128]{1,0:T(8,128)}, u32[]{:S(2)}, u32[]{:S(2)}) collective-permute-start(f32[3072,128]{1,0:T(8,128)S(1)} %bitcast.7), channel_id=1, source_target_pairs={{0,126},{2,0},{4,2},{6,4},{8,6},{10,8},{12,10},{14,12},{16,14},{18... | collective-permute-start | bytes 4718600 | tf_op jit(solution)/shard_map/ppermute | solution.py:18
  127.6 38.1 %collective-permute-start.14 = (f32[2,12,128,128]{3,2,1,0:T(8,128)}, f32[2,12,128,128]{3,2,1,0:T(8,128)}, u32[]{:S(2)}, u32[]{:S(2)}) collective-permute-start(f32[2,12,128,128]{3,2,1,0:T(8,128)} %fusion), channel_id=1, source_target_pairs={{0,1},{1,0},{2,3},{3,2},{4,5},{5,4},{6,7},{7,6},{8,9},{9,8},{10,11... | collective-permute-start | bytes 4718600 | tf_op jit(solution)/shard_map/ppermute | solution.py:22
  128.5 64.0 %collective-permute-start.11 = (f32[3072,128]{1,0:T(8,128)S(1)}, f32[3072,128]{1,0:T(8,128)}, u32[]{:S(2)}, u32[]{:S(2)}) collective-permute-start(f32[3072,128]{1,0:T(8,128)S(1)} %bitcast.9), channel_id=1, source_target_pairs={{0,2},{2,4},{4,6},{6,8},{8,10},{10,12},{12,14},{14,16},{16,18},{18... | collective-permute-start | bytes 4718600 | tf_op jit(solution)/shard_map/ppermute | solution.py:18
  128.5 64.0 %collective-permute-start.12 = (f32[3072,128]{1,0:T(8,128)S(1)}, f32[3072,128]{1,0:T(8,128)}, u32[]{:S(2)}, u32[]{:S(2)}) collective-permute-start(f32[3072,128]{1,0:T(8,128)S(1)} %bitcast.10), channel_id=1, source_target_pairs={{0,126},{2,0},{4,2},{6,4},{8,6},{10,8},{12,10},{14,12},{16,14},{18... | collective-permute-start | bytes 4718600 | tf_op jit(solution)/shard_map/ppermute | solution.py:18
  135.4 11.4 %copy-start.25 = (s32[2]{0:T(128)S(1)}, s32[2]{0:T(128)}, u32[]{:S(2)}) copy-start(s32[2]{0:T(128)} %pad_add_fusion.1.meta.refs_0_) | copy-start | bytes 28
  135.4 11.4 %copy-start.27 = (s32[4,24]{1,0:T(4,128)S(1)}, s32[4,24]{1,0:T(4,128)}, u32[]{:S(2)}) copy-start(s32[4,24]{1,0:T(4,128)} %refs_1_.17) | copy-start | bytes 1156
  135.4 11.4 %copy-start.29 = (s32[2,40]{1,0:T(2,128)S(1)}, s32[2,40]{1,0:T(2,128)}, u32[]{:S(2)}) copy-start(s32[2,40]{1,0:T(2,128)} %copy-done.28) | copy-start | bytes 964
  156.2 11.3 %copy-start.11 = (f32[4,12,128,128]{3,2,1,0:T(8,128)}, f32[4,12,128,128]{3,2,1,0:T(8,128)S(1)}, u32[]{:S(2)}) copy-start(f32[4,12,128,128]{3,2,1,0:T(8,128)S(1)} %get-tuple-element.57.refs_9_) | copy-start | bytes 9437188
  156.2 11.3 %copy-start.12 = (f32[4,12,128,128]{3,2,1,0:T(8,128)}, f32[4,12,128,128]{3,2,1,0:T(8,128)S(1)}, u32[]{:S(2)}) copy-start(f32[4,12,128,128]{3,2,1,0:T(8,128)S(1)} %get-tuple-element.58.refs_10_) | copy-start | bytes 9437188
  158.8 67.3 %collective-permute-start.19 = (f32[3072,128]{1,0:T(8,128)}, f32[3072,128]{1,0:T(8,128)S(1)}, u32[]{:S(2)}, u32[]{:S(2)}) collective-permute-start(f32[3072,128]{1,0:T(8,128)} %collective-permute-done.17.refs_5_), channel_id=1, source_target_pairs={{0,2},{2,4},{4,6},{6,8},{8,10},{10,12},{12,14},{14,16},{16,18},{18... | collective-permute-start | bytes 4718600 | tf_op jit(solution)/shard_map/ppermute | solution.py:18
  158.8 68.4 %collective-permute-start.20 = (f32[3072,128]{1,0:T(8,128)}, f32[3072,128]{1,0:T(8,128)}, u32[]{:S(2)}, u32[]{:S(2)}) collective-permute-start(f32[3072,128]{1,0:T(8,128)} %collective-permute-done.18.refs_7_), channel_id=1, source_target_pairs={{0,126},{2,0},{4,2},{6,4},{8,6},{10,8},{12,10},{14,12},{16,14},{18... | collective-permute-start | bytes 4718600 | tf_op jit(solution)/shard_map/ppermute | solution.py:18
  167.5 32.0 %copy-start.1 = (bf16[5,2,4,128,256]{4,3,2,1,0:T(8,128)(2,1)S(1)}, bf16[5,2,4,128,256]{4,3,2,1,0:T(8,128)(2,1)}, u32[]{:S(2)}) copy-start(bf16[5,2,4,128,256]{4,3,2,1,0:T(8,128)(2,1)} %get-tuple-element.56.refs_3_.refs_4_) | copy-start | bytes 7864324
  167.5 32.0 %copy-start.31 = (s32[2,40]{1,0:T(2,128)S(1)}, s32[2,40]{1,0:T(2,128)}, u32[]{:S(2)}) copy-start(s32[2,40]{1,0:T(2,128)} %copy-done.30) | copy-start | bytes 964
  167.5 32.0 %copy-start.33 = (s32[2,40]{1,0:T(2,128)S(1)}, s32[2,40]{1,0:T(2,128)}, u32[]{:S(2)}) copy-start(s32[2,40]{1,0:T(2,128)} %copy-done.32) | copy-start | bytes 964
  169.5 57.8 %copy-start.21 = (s32[2,40]{1,0:T(2,128)S(1)}, s32[2,40]{1,0:T(2,128)}, u32[]{:S(2)}) copy-start(s32[2,40]{1,0:T(2,128)} %copy-done.20) | copy-start | bytes 964
  169.5 57.8 %copy-start.23 = (s32[2,40]{1,0:T(2,128)S(1)}, s32[2,40]{1,0:T(2,128)}, u32[]{:S(2)}) copy-start(s32[2,40]{1,0:T(2,128)} %copy-done.22) | copy-start | bytes 964
  192.5 67.3 %collective-permute-start.15 = (f32[3072,128]{1,0:T(8,128)}, f32[3072,128]{1,0:T(8,128)S(1)}, u32[]{:S(2)}, u32[]{:S(2)}) collective-permute-start(f32[3072,128]{1,0:T(8,128)} %collective-permute-done.11.refs_6_), channel_id=1, source_target_pairs={{0,2},{2,4},{4,6},{6,8},{8,10},{10,12},{12,14},{14,16},{16,18},{18... | collective-permute-start | bytes 4718600 | tf_op jit(solution)/shard_map/ppermute | solution.py:18
  192.5 67.3 %collective-permute-start.16 = (f32[3072,128]{1,0:T(8,128)}, f32[3072,128]{1,0:T(8,128)S(1)}, u32[]{:S(2)}, u32[]{:S(2)}) collective-permute-start(f32[3072,128]{1,0:T(8,128)} %collective-permute-done.12.refs_8_), channel_id=1, source_target_pairs={{0,126},{2,0},{4,2},{6,4},{8,6},{10,8},{12,10},{14,12},{16,14},{18... | collective-permute-start | bytes 4718600 | tf_op jit(solution)/shard_map/ppermute | solution.py:18
  230.6 29.3 %copy-start.16 = (bf16[2,1,3,128,256]{4,3,2,1,0:T(8,128)(2,1)S(1)}, bf16[2,1,3,128,256]{4,3,2,1,0:T(8,128)(2,1)}, u32[]{:S(2)}) copy-start(bf16[2,1,3,128,256]{4,3,2,1,0:T(8,128)(2,1)} %get-tuple-element.53.refs_4_) | copy-start | bytes 1179652
  265.6 5.5 %collective-permute-start.21 = (f32[3,12,128,128]{3,2,1,0:T(8,128)S(1)}, f32[3,12,128,128]{3,2,1,0:T(8,128)S(1)}, u32[]{:S(2)}, u32[]{:S(2)}) collective-permute-start(f32[3,12,128,128]{3,2,1,0:T(8,128)S(1)} %get-tuple-element.66), channel_id=1, source_target_pairs={{0,1},{1,0},{2,3},{3,2},{4,5},{5,4},{6,7},{7,6},{8,9},{9,8},{10,11... | collective-permute-start | bytes 7077896 | tf_op jit(solution)/shard_map/ppermute | solution.py:22
  270.3 2.4 collective-permute-start.22
  (13 other events, 53.9 us)
